TPU v7x, 256 devices: a whole 4x4x8 slice. The times are simulated.
256 devices in a mesh: tm: 4 (over x), height: 4 (over y), width: 16 (over z, core).
Axes of the slice: x: 4, y: 4, z: 8, core: 2. Of those that a mesh axis runs over, the one named last changes fastest.
Arguments:
- video: bfloat16 [64, 64, 256, 256], P('tm', 'height', 'width'), may hold values from -12 to 12
- w_space: bfloat16 [3, 3, 256, 256], replicated, may hold values from -0.125 to 0.125
- w_time: bfloat16 [3, 256, 256], replicated, may hold values from -0.21875 to 0.21875
- norm_gain: float32 [256], replicated, may hold values from 0.1 to 1.9
- norm_bias: float32 [256], replicated, may hold values from -1 to 1
- w_qkv: bfloat16 [256, 768], replicated, may hold values from -64 to 64
- w_out: bfloat16 [256, 256], replicated, may hold values from -0.375 to 0.375
Outputs:
- block_out: bfloat16 [64, 64, 256, 256], P('tm', 'height', 'width')
All inputs are finite; a program needn't handle non-finite values.
Results may differ from a plain program's by a relative error of at most 0.012.
Values may be sent and summed in bfloat16 or wider, within the bound.
No kernel may reach another device: no remote copies, remote signals or barrier semaphores. Data moves between devices by JAX's collectives and lax.ppermute only.
A program may use at most 128 MiB of HBM per device.

v0:
```python
import math

import jax
import jax.numpy as jnp
from jax import lax
from jax.sharding import Mesh
from jax.sharding import PartitionSpec as P

HEADS = 8
GROUPS = 32
WIDTH = ("width_0", "width_1")
TM_HEIGHT_WIDTH = ("tm", "height", "width_0", "width_1")


def padded_2(value, sides, width):
    for axis, dim in sides:
        size, length = (lax.axis_size(axis), value.shape[dim])
        up = [(i, (i + 1) % size) for i in range(size - 1)]
        down = [(j, i) for i, j in up]
        last = lax.slice_in_dim(value, length - width, length, axis=dim)
        first = lax.slice_in_dim(value, 0, width, axis=dim)
        before = lax.ppermute(last, axis, up)
        after = lax.ppermute(first, axis, down)
        value = jnp.concatenate([before, value, after], axis=dim)
    return value


def by_axis(value, axes):
    for axis in axes:
        value = lax.psum(value, axis)
    return value


def attend(block, w_qkv, w_out):
    frames, pixels, channels = block.shape
    head_size = channels // HEADS
    flattened = block.reshape(frames * pixels, channels)
    projected = jnp.dot(flattened, w_qkv, preferred_element_type=jnp.float32).astype(jnp.bfloat16)
    projected = projected.reshape(frames, pixels, 3, HEADS, head_size)
    scores = jnp.einsum(
        "fphd,gphd->phfg",
        projected[:, :, 0],
        projected[:, :, 1],
        preferred_element_type=jnp.float32,
    ) / math.sqrt(head_size)
    weights = jax.nn.softmax(scores, axis=-1).astype(jnp.bfloat16)
    context = jnp.einsum(
        "phfg,gphd->fphd", weights, projected[:, :, 2], preferred_element_type=jnp.float32
    ).astype(jnp.bfloat16)
    context = context.reshape(frames * pixels, channels)
    result = flattened.astype(jnp.float32) + jnp.dot(
        context, w_out, preferred_element_type=jnp.float32
    )
    return result.reshape(frames, pixels, channels).astype(jnp.bfloat16)


def attend_slot(block, w_qkv, w_out):
    return attend(block[:, 0], w_qkv, w_out)[:, None]


def per_device(video, w_space, w_time, norm_gain, norm_bias, w_qkv, w_out):
    frames, rows, cols, channels = video.shape
    pixels = rows * cols
    padded = padded_2(video, (("height", 1), (WIDTH, 2)), 1)
    running = jnp.zeros((frames * pixels, channels), jnp.float32)
    for row_step in range(3):
        for col_step in range(3):
            window_piece = padded[
                :, row_step : row_step + rows, col_step : col_step + cols
            ].reshape(frames * pixels, channels)
            running = running + jnp.dot(
                window_piece, w_space[row_step, col_step], preferred_element_type=jnp.float32
            )
    spatial = running.reshape(frames, pixels, channels).astype(jnp.bfloat16)
    framed = padded_2(spatial, (("tm", 0),), 1)
    running = spatial.astype(jnp.float32).reshape(frames * pixels, channels)
    for tap in range(3):
        running = running + jnp.dot(
            framed[tap : tap + frames].reshape(frames * pixels, channels),
            w_time[tap],
            preferred_element_type=jnp.float32,
        )
    temporal = running.astype(jnp.bfloat16)
    grouped = temporal.astype(jnp.float32).reshape(frames * pixels, GROUPS, channels // GROUPS)
    cell_count = float(
        frames
        * lax.axis_size("tm")
        * rows
        * lax.axis_size("height")
        * cols
        * lax.axis_size(WIDTH)
        * (channels // GROUPS)
    )
    local_sum = jnp.sum(grouped, axis=(0, 2))
    total_sum, total_square = (
        by_axis(local_sum, TM_HEIGHT_WIDTH),
        by_axis(jnp.sum(grouped * grouped, axis=(0, 2)), TM_HEIGHT_WIDTH),
    )
    group_mean = total_sum / cell_count
    group_var = jnp.maximum(total_square / cell_count - group_mean * group_mean, 0.0)
    centered = grouped - group_mean[None, :, None]
    scaled = centered * lax.rsqrt(group_var + 1e-05)[None, :, None]
    scaled = scaled.reshape(frames * pixels, channels) * norm_gain + norm_bias
    normed = jax.nn.silu(scaled).astype(jnp.bfloat16).reshape(frames, pixels, channels)
    tm_count = lax.axis_size("tm")
    slotted = normed.reshape(frames, tm_count, pixels // tm_count, channels)
    outcome = (lambda block: attend_slot(block, w_qkv, w_out))(
        lax.all_to_all(slotted, "tm", split_axis=1, concat_axis=0, tiled=True)
    )
    result = lax.all_to_all(outcome, "tm", split_axis=0, concat_axis=1, tiled=True)
    return result.reshape(frames, rows, cols, channels)


def solution(mesh):
    torus = Mesh(
        mesh.devices.reshape(mesh.shape["tm"], mesh.shape["height"], 8, 2),
        ("tm", "height", "width_0", "width_1"),
    )
    in_specs = (P("tm", "height", WIDTH, None), P(), P(), P(), P(), P(), P())
    out_specs = P("tm", "height", WIDTH, None)
    return jax.shard_map(
        per_device, mesh=torus, in_specs=in_specs, out_specs=out_specs, check_vma=False
    )
```

profile of v0, /device:TPU:1, one launch (start us, length us, event | category | flops | bytes accessed | tf_op | source)
XLA Modules:
  0.0 273.6 jit_solution(925118517245756419)
XLA Ops:
  0.0 1.0 fusion.61
  1.0 4.0 %collective-permute-start = (bf16[16,1,16,256]{3,2,1,0:T(8,128)(2,1)S(1)}, bf16[16,1,16,256]{3,2,1,0:T(8,128)(2,1)S(1)}, u32[]{:S(2)}, u32[]{:S(2)}) collective-permute-start(bf16[16,1,16,256]{3,2,1,0:T(8,128)(2,1)S(1)} %get-tuple-element.37), channel_id=1, source_target_pairs={{0,16},{16,32},{32,48},{1,17},{17,33},{33,49},{2,18},{18,34},{34,5... | collective-permute-start | bytes 393224 | tf_op jit(solution)/shard_map/ppermute | solution.py:22
  5.1 1.3 collective-permute-start.1
  6.4 0.9 collective-permute-done
  7.2 3.5 %collective-permute-done.1 = bf16[16,1,16,256]{3,2,1,0:T(8,128)(2,1)S(1)} collective-permute-done((bf16[16,1,16,256]{3,2,1,0:T(8,128)(2,1)S(1)}, bf16[16,1,16,256]{3,2,1,0:T(8,128)(2,1)S(1)}, u32[]{:S(2)}, u32[]{:S(2)}) %collective-permute-start.1) | collective-permute-done | bytes 131104 | tf_op jit(solution)/shard_map/ppermute | solution.py:23
  10.8 3.3 %pad_maximum_fusion.3 = (bf16[16,16,16,256]{3,2,1,0:T(8,128)(2,1)S(1)}, bf16[16,18,16,256]{3,2,1,0:T(8,128)(2,1)S(1)}, bf16[16,16,16,256]{3,2,1,0:T(8,128)(2,1)S(1)}) fusion(bf16[16,1,16,256]{3,2,1,0:T(8,128)(2,1)S(1)} %collective-permute-done.1, bf16[16,16,16,256]{3,2,1,0:T(8,128)(2,1)} %param.7, ...), kind=kLoop, calls=%fused_computation.56 | loop fusion | flops 8388608 | bytes 8650752 | tf_op jit(solution)/shard_map/concatenate | solution.py:24
  14.1 0.5 fusion.60
  14.6 4.0 %collective-permute-start.3 = (bf16[16,18,1,256]{3,0,2,1:T(8,128)(2,1)S(1)}, bf16[16,18,1,256]{3,0,2,1:T(8,128)(2,1)S(1)}, u32[]{:S(2)}, u32[]{:S(2)}) collective-permute-start(bf16[16,18,1,256]{3,0,2,1:T(8,128)(2,1)S(1)} %copy.38), channel_id=1, source_target_pairs={{1,0},{2,1},{3,2},{4,3},{5,4},{6,5},{7,6},{8,7},{9,8},{10,9},{11,1... | collective-permute-start | bytes 442376 | tf_op jit(solution)/shard_map/ppermute | solution.py:23
  18.6 3.4 %collective-permute-start.2 = (bf16[16,18,1,256]{3,0,2,1:T(8,128)(2,1)S(1)}, bf16[16,18,1,256]{3,0,2,1:T(8,128)(2,1)S(1)}, u32[]{:S(2)}, u32[]{:S(2)}) collective-permute-start(bf16[16,18,1,256]{3,0,2,1:T(8,128)(2,1)S(1)} %copy.36), channel_id=1, source_target_pairs={{0,1},{1,2},{2,3},{3,4},{4,5},{5,6},{6,7},{7,8},{8,9},{9,10},{10,1... | collective-permute-start | bytes 442376 | tf_op jit(solution)/shard_map/ppermute | solution.py:22
  22.1 0.9 collective-permute-done.3
  23.0 0.2 copy.39
  23.2 1.0 collective-permute-done.2
  24.2 0.2 copy.37
  24.4 0.0 copy-start.3
  24.4 7.0 %pad_maximum_fusion.4 = (bf16[16,16,16,256]{3,2,1,0:T(8,128)(2,1)S(1)}, bf16[16,16,16,256]{3,2,1,0:T(8,128)(2,1)S(1)}, bf16[16,16,16,256]{3,2,1,0:T(8,128)(2,1)S...) fusion(bf16[16,18,16,256]{3,2,1,0:T(8,128)(2,1)S(1)} %constant_, ...), kind=kLoop, calls=%fused_computation.57 | loop fusion | flops 25165824 | bytes 15237120 | tf_op jit(solution)/shard_map/concatenate | solution.py:24
  31.5 0.7 fusion.44
  32.2 0.7 fusion.35
  32.9 0.7 convolution_add_fusion.9
  33.6 0.8 convolution_add_fusion.8
  34.4 0.7 convolution_add_fusion.7
  35.1 0.9 copy-done.2
  36.0 0.8 convolution_add_fusion.6
  36.8 0.8 convolution_add_fusion.5
  37.5 0.7 convolution_add_fusion.4
  38.3 0.9 fusion.10
  39.2 1.3 collective-permute-start.5
  40.5 4.0 %collective-permute-start.4 = (bf16[1,256,256]{2,1,0:T(8,128)(2,1)S(1)}, bf16[1,256,256]{2,1,0:T(8,128)(2,1)S(1)}, u32[]{:S(2)}, u32[]{:S(2)}) collective-permute-start(bf16[1,256,256]{2,1,0:T(8,128)(2,1)S(1)} %get-tuple-element.32), channel_id=1, source_target_pairs={{0,64},{64,128},{128,192},{1,65},{65,129},{129,193},{2,66},{66,130... | collective-permute-start | bytes 393224 | tf_op jit(solution)/shard_map/ppermute | solution.py:22
  44.5 0.7 fusion.32
  45.2 1.2 collective-permute-done.4
  46.4 0.4 pad_maximum_fusion
  46.8 0.7 fusion.6
  47.5 0.0 copy-start.7
  47.5 1.0 convert_reduce_fusion
  48.5 0.1 reduce_sum.32
  48.6 0.1 reduce_sum.45
  48.7 0.1 reduce_sum.36
  48.8 0.1 reduce_sum.46
  48.9 9.7 %all-reduce.2 = (f32[32]{0:T(128)S(1)}, f32[32]{0:T(128)S(1)}) all-reduce(f32[32]{0:T(128)S(1)} %reduce_sum.46, f32[32]{0:T(128)S(1)} %reduce_sum.36), channel_id=1, replica_groups=mesh['tm'=4,'height'=4,'width_0'=8,'width_1'=2] {'tm'}, use_global_device_ids=true, to_apply=%region_8.0 | all-reduce | flops 64 | bytes 512 | tf_op jit(solution)/shard_map/psum | solution.py:30
  58.6 7.3 %all-reduce.1 = (f32[32]{0:T(128)S(1)}, f32[32]{0:T(128)S(1)}) all-reduce(f32[32]{0:T(128)S(1)} %get-tuple-element.11, f32[32]{0:T(128)S(1)} %get-tuple-element.12), channel_id=1, replica_groups=mesh['tm'=4,'height'=4,'width_0'=8,'width_1'=2] {'height'}, use_global_device_ids=true, to_apply=%region_9.0 | all-reduce | flops 64 | bytes 512 | tf_op jit(solution)/shard_map/psum | solution.py:30
  65.9 15.7 %all-reduce = (f32[32]{0:T(128)S(1)}, f32[32]{0:T(128)S(1)}) all-reduce(f32[32]{0:T(128)S(1)} %get-tuple-element.9, f32[32]{0:T(128)S(1)} %get-tuple-element.10), channel_id=1, replica_groups=mesh['tm'=4,'height'=4,'width_0'=8,'width_1'=2] {'width_0'}, use_global_device_ids=true, to_apply=%region_10.11 | all-reduce | flops 64 | bytes 512 | tf_op jit(solution)/shard_map/psum | solution.py:30
  81.6 12.7 %all-reduce.3 = (f32[32]{0:T(128)S(1)}, f32[32]{0:T(128)S(1)}) all-reduce(f32[32]{0:T(128)S(1)} %get-tuple-element.7, f32[32]{0:T(128)S(1)} %get-tuple-element.8), channel_id=1, replica_groups=mesh['tm'=4,'height'=4,'width_0'=8,'width_1'=2] {'width_1'}, use_global_device_ids=true, to_apply=%region_11.12 | all-reduce | flops 64 | bytes 512 | tf_op jit(solution)/shard_map/psum | solution.py:30
  94.3 0.1 sub.24
  94.4 0.1 sub.25
  94.5 0.1 mul.34
  94.6 0.1 mul.35
  94.7 1.4 fusion.19
  96.1 0.2 copy.40
  96.4 28.6 %all_to_all.30 = bf16[16,4,64,256]{3,2,0,1:T(8,128)(2,1)S(1)} all-to-all(bf16[16,4,64,256]{3,2,0,1:T(8,128)(2,1)S(1)} %copy.40), channel_id=1, replica_groups=mesh['tm'=4,'height'=4,'width_0'=8,'width_1'=2] {'tm'}, dimensions={1} | all-to-all | bytes 4194304 | tf_op jit(solution)/shard_map/all_to_all | solution.py:108
  124.9 4.5 %convolution_convert_fusion = bf16[4096,768]{1,0:T(8,128)(2,1)} fusion(bf16[4096,256]{1,0:T(8,128)(2,1)S(1)} %bitcast.103, bf16[256,768]{1,0:T(8,128)(2,1)S(1)} %copy-done), kind=kOutput, calls=%fused_computation.7 | convolution fusion | flops 1613758464 | bytes 8781824 | tf_op jit(solution)/shard_map/dot_general | solution.py:38
  129.4 8.6 %copy.41 = bf16[4096,768]{0,1:T(8,128)(2,1)} copy(bf16[4096,768]{1,0:T(8,128)(2,1)} %convolution_convert_fusion) | data formatting | bytes 12582912 | tf_op jit(solution)/shard_map/convert_element_type | solution.py:38
  138.0 17.9 %reshape.85 = bf16[64,64,3,8,32]{1,0,4,3,2:T(8,128)(2,1)} reshape(bf16[4096,768]{0,1:T(8,128)(2,1)} %copy.41) | data formatting | bytes 12582912 | tf_op jit(solution)/shard_map/reshape | solution.py:39
  155.9 9.3 %fusion.59 = (bf16[64,64,1,8,32]{1,0,4,3,2:T(8,128)(2,1)}, bf16[64,64,1,8,32]{1,0,4,3,2:T(8,128)(2,1)}, bf16[64,64,1,8,32]{1,0,4,3,2:T(8,128)(2,1)}) fusion(bf16[64,64,3,8,32]{1,0,4,3,2:T(8,128)(2,1)} %reshape.85), kind=kLoop, calls=%fused_computation.94 | loop fusion | bytes 12582912 | tf_op jit(solution)/shard_map/slice | solution.py:48
  165.2 7.2 %copy.50 = bf16[64,64,1,8,32]{0,4,3,1,2:T(8,128)(2,1)} copy(bf16[64,64,1,8,32]{1,0,4,3,2:T(8,128)(2,1)} %get-tuple-element.15) | data formatting | bytes 4194304
  172.4 7.2 %copy.51 = bf16[64,64,1,8,32]{0,4,3,1,2:T(8,128)(2,1)} copy(bf16[64,64,1,8,32]{1,0,4,3,2:T(8,128)(2,1)} %get-tuple-element.16) | data formatting | bytes 4194304
  179.5 7.2 %copy.52 = bf16[64,64,1,8,32]{0,4,3,1,2:T(8,128)(2,1)} copy(bf16[64,64,1,8,32]{1,0,4,3,2:T(8,128)(2,1)} %get-tuple-element.17) | data formatting | bytes 4194304
  186.7 11.6 %fusion.21 = f32[64,8,64,64]{2,3,1,0:T(8,128)} fusion(bf16[64,64,1,8,32]{0,4,3,1,2:T(8,128)(2,1)} %copy.52, bf16[64,64,1,8,32]{0,4,3,1,2:T(8,128)(2,1)} %copy.51), kind=kOutput, calls=%fused_computation.40 | convolution fusion | flops 134217728 | bytes 12582912 | tf_op jit(solution)/shard_map/fphd,gphd->phfg/dot_general | solution.py:40
  198.3 18.4 %fusion.62 = (f32[64,8,64]{2,1,0:T(8,128)S(1)}, f32[64,8,64,64]{2,3,1,0:T(8,128)}) fusion(f32[64,8,64,64]{2,3,1,0:T(8,128)} %fusion.21), kind=kOutput, calls=%fused_computation.97 | output fusion | flops 8388671 | bytes 16908288 | tf_op jit(solution)/shard_map/sub | solution.py:46
  216.7 11.3 %convert_bitcast_fusion = bf16[64,64,8,32]{0,3,2,1:T(8,128)(2,1)} fusion(f32[64,8,64,64]{2,3,1,0:T(8,128)} %get-tuple-element.42, f32[64,8,64]{2,1,0:T(8,128)S(1)} %get-tuple-element.41, bf16[64,64,1,8,32]{0,4,3,1,2:T(8,128)(2,1)} %copy.50), kind=kOutput, calls=%fused_computation.44 | convolution fusion | flops 139460608 | bytes 12713984 | tf_op jit(solution)/shard_map/phfg,gphd->fphd/dot_general | solution.py:47
  228.0 7.2 %copy.46 = bf16[64,64,8,32]{1,0,3,2:T(8,128)(2,1)} copy(bf16[64,64,8,32]{0,3,2,1:T(8,128)(2,1)} %convert_bitcast_fusion) | data formatting | bytes 4194304 | tf_op jit(solution)/shard_map/convert_element_type | solution.py:49
  235.2 6.6 %reshape.86 = bf16[4096,256]{0,1:T(8,128)(2,1)} reshape(bf16[64,64,8,32]{1,0,3,2:T(8,128)(2,1)} %copy.46) | data formatting | bytes 4194304 | tf_op jit(solution)/shard_map/reshape | solution.py:50
  241.9 2.4 fusion.9
  244.3 0.0 copy-start.1
  244.3 27.8 %all_to_all.31 = bf16[64,1,64,256]{3,2,1,0:T(8,128)(2,1)S(1)} all-to-all(bf16[64,1,64,256]{3,2,1,0:T(8,128)(2,1)S(1)} %bitcast.110), channel_id=1, replica_groups=mesh['tm'=4,'height'=4,'width_0'=8,'width_1'=2] {'tm'}, dimensions={0} | all-to-all | bytes 4194304 | tf_op jit(solution)/shard_map/all_to_all | solution.py:110
  272.1 1.5 copy.48
  (19 shorter events, 0.1 us)
Async XLA Ops:
  0.0 124.9 %copy-start = (bf16[256,768]{1,0:T(8,128)(2,1)S(1)}, bf16[256,768]{1,0:T(8,128)(2,1)}, u32[]{:S(2)}) copy-start(bf16[256,768]{1,0:T(8,128)(2,1)} %param.12) | copy-start | bytes 1179652
  1.0 6.2 %collective-permute-start = (bf16[16,1,16,256]{3,2,1,0:T(8,128)(2,1)S(1)}, bf16[16,1,16,256]{3,2,1,0:T(8,128)(2,1)S(1)}, u32[]{:S(2)}, u32[]{:S(2)}) collective-permute-start(bf16[16,1,16,256]{3,2,1,0:T(8,128)(2,1)S(1)} %get-tuple-element.37), channel_id=1, source_target_pairs={{0,16},{16,32},{32,48},{1,17},{17,33},{33,49},{2,18},{18,34},{34,5... | collective-permute-start | bytes 393224 | tf_op jit(solution)/shard_map/ppermute | solution.py:22
  5.1 5.7 %collective-permute-start.1 = (bf16[16,1,16,256]{3,2,1,0:T(8,128)(2,1)S(1)}, bf16[16,1,16,256]{3,2,1,0:T(8,128)(2,1)S(1)}, u32[]{:S(2)}, u32[]{:S(2)}) collective-permute-start(bf16[16,1,16,256]{3,2,1,0:T(8,128)(2,1)S(1)} %get-tuple-element.36), channel_id=1, source_target_pairs={{16,0},{32,16},{48,32},{17,1},{33,17},{49,33},{18,2},{34,18},{50,3... | collective-permute-start | bytes 393224 | tf_op jit(solution)/shard_map/ppermute | solution.py:23
  14.6 8.4 %collective-permute-start.3 = (bf16[16,18,1,256]{3,0,2,1:T(8,128)(2,1)S(1)}, bf16[16,18,1,256]{3,0,2,1:T(8,128)(2,1)S(1)}, u32[]{:S(2)}, u32[]{:S(2)}) collective-permute-start(bf16[16,18,1,256]{3,0,2,1:T(8,128)(2,1)S(1)} %copy.38), channel_id=1, source_target_pairs={{1,0},{2,1},{3,2},{4,3},{5,4},{6,5},{7,6},{8,7},{9,8},{10,9},{11,1... | collective-permute-start | bytes 442376 | tf_op jit(solution)/shard_map/ppermute | solution.py:23
  18.6 5.5 %collective-permute-start.2 = (bf16[16,18,1,256]{3,0,2,1:T(8,128)(2,1)S(1)}, bf16[16,18,1,256]{3,0,2,1:T(8,128)(2,1)S(1)}, u32[]{:S(2)}, u32[]{:S(2)}) collective-permute-start(bf16[16,18,1,256]{3,0,2,1:T(8,128)(2,1)S(1)} %copy.36), channel_id=1, source_target_pairs={{0,1},{1,2},{2,3},{3,4},{4,5},{5,6},{6,7},{7,8},{8,9},{9,10},{10,1... | collective-permute-start | bytes 442376 | tf_op jit(solution)/shard_map/ppermute | solution.py:22
  24.4 7.1 %copy-start.3 = (bf16[3,3,256,256]{3,2,1,0:T(8,128)(2,1)S(1)}, bf16[3,3,256,256]{3,2,1,0:T(8,128)(2,1)}, u32[]{:S(2)}) copy-start(bf16[3,3,256,256]{3,2,1,0:T(8,128)(2,1)} %param.8) | copy-start | bytes 3538948
  34.4 1.6 copy-start.2
  38.3 6.2 %copy-start.4 = (bf16[3,256,256]{2,1,0:T(8,128)(2,1)S(1)}, bf16[3,256,256]{2,1,0:T(8,128)(2,1)}, u32[]{:S(2)}) copy-start(bf16[3,256,256]{2,1,0:T(8,128)(2,1)} %param.9) | copy-start | bytes 1179652
  39.2 6.0 %collective-permute-start.5 = (bf16[1,256,256]{2,1,0:T(8,128)(2,1)S(1)}, bf16[1,256,256]{2,1,0:T(8,128)(2,1)S(1)}, u32[]{:S(2)}, u32[]{:S(2)}) collective-permute-start(bf16[1,256,256]{2,1,0:T(8,128)(2,1)S(1)} %get-tuple-element.31), channel_id=1, source_target_pairs={{64,0},{128,64},{192,128},{65,1},{129,65},{193,129},{66,2},{130,66... | collective-permute-start | bytes 393224 | tf_op jit(solution)/shard_map/ppermute | solution.py:23
  40.5 5.9 %collective-permute-start.4 = (bf16[1,256,256]{2,1,0:T(8,128)(2,1)S(1)}, bf16[1,256,256]{2,1,0:T(8,128)(2,1)S(1)}, u32[]{:S(2)}, u32[]{:S(2)}) collective-permute-start(bf16[1,256,256]{2,1,0:T(8,128)(2,1)S(1)} %get-tuple-element.32), channel_id=1, source_target_pairs={{0,64},{64,128},{128,192},{1,65},{65,129},{129,193},{2,66},{66,130... | collective-permute-start | bytes 393224 | tf_op jit(solution)/shard_map/ppermute | solution.py:22
  47.5 47.2 %copy-start.6 = (f32[256]{0:T(256)S(1)}, f32[256]{0:T(256)}, u32[]{:S(2)}) copy-start(f32[256]{0:T(256)} %param.11) | copy-start | bytes 3076
  47.5 47.2 %copy-start.7 = (f32[256]{0:T(256)S(1)}, f32[256]{0:T(256)}, u32[]{:S(2)}) copy-start(f32[256]{0:T(256)} %param.10) | copy-start | bytes 3076
  235.2 6.7 %copy-start.5 = (bf16[256,256]{1,0:T(8,128)(2,1)S(1)}, bf16[256,256]{1,0:T(8,128)(2,1)}, u32[]{:S(2)}) copy-start(bf16[256,256]{1,0:T(8,128)(2,1)} %param.13) | copy-start | bytes 393220
  244.3 29.3 %copy-start.1 = (bf16[256,768]{1,0:T(8,128)(2,1)S(1)}, bf16[256,768]{1,0:T(8,128)(2,1)}, u32[]{:S(2)}) copy-start(bf16[256,768]{1,0:T(8,128)(2,1)} %param.12) | copy-start | bytes 1179652
where the time goes:
time: 275 us; the launch traced here: 274 us
  blocking collectives  102 us (37%)
  local copies, waits for them, and re-layouts  76.3 us (28%)
  matrix products  38.9 us (14%)
  other arithmetic  30.8 us (11%)
  starting transfers between devices  18.1 us (7%)
  waiting for transfers between devices  7.44 us (3%)
    psum x4, blocking collectives, by_axis(): value = lax.psum(value, axis)  45.4 us
    all_to_all x1, blocking collectives, per_device(): lax.all_to_all(slotted, 'tm', split_axis=1, concat_axis=0, tiled=True)  28.6 us
    all_to_all x1, blocking collectives, per_device(): lax.all_to_all(outcome, 'tm', split_axis=0, concat_axis=1, tiled=True)  27.8 us
    unnamed x20, local copies, waits for them, and re-layouts  22.5 us
    sub x1, other arithmetic, attend(): weights = jax.nn.softmax(scores, axis=-1).astype(jnp.bfloat16)  18.4 us
    reshape x1, local copies, waits for them, and re-layouts, attend(): projected = projected.reshape(frames, pixels, 3, HEADS, head_size)  17.9 us
    dot_general x1, matrix products, attend(): jnp.einsum('fphd,gphd->phfg', projected[:, :, 0], projected[:, :, 1], pre...  11.6 us
    ppermute x3, starting transfers between devices, padded_2(): before = lax.ppermute(last, axis, up)  11.5 us
  transfers between devices with their start and end apart: 6, of which 5 were waited for; matrix products, arithmetic and copies ran while one was open for 0% of the time, Pallas kernels for 0%

commit v1 on v0

v1 whole, which is shorter than its diff:
```python
import functools
import math

import jax
import jax.numpy as jnp
from jax import lax
from jax.experimental import pallas as pl
from jax.experimental.pallas import tpu as pltpu
from jax.sharding import Mesh
from jax.sharding import PartitionSpec as P

HEADS = 8
GROUPS = 32
WIDTH = ("width_0", "width_1")
BF16 = jnp.bfloat16
F32 = jnp.float32
VMEM_BYTES = 60 * 1024 * 1024


def params(**kw):
    return pltpu.CompilerParams(vmem_limit_bytes=VMEM_BYTES, **kw)


def cost(flops, nbytes, trans=0):
    return pl.CostEstimate(flops=flops, bytes_accessed=nbytes, transcendentals=trans)


def shift(value, axis, step):
    size = lax.axis_size(axis)
    if step > 0:
        pairs = [(i, i + 1) for i in range(size - 1)]
    else:
        pairs = [(i + 1, i) for i in range(size - 1)]
    return lax.ppermute(value, axis, pairs)


def to_pixels(video):
    frames, rows, cols, channels = video.shape
    step = 4

    def kernel(v_ref, out_ref, first_ref, last_ref):
        for r in range(step):
            turned = jnp.swapaxes(v_ref[:, r], 0, 1)
            out_ref[r] = turned
            first_ref[r] = turned[0]
            last_ref[r] = turned[cols - 1]

    edge = jax.ShapeDtypeStruct((rows, frames, channels), BF16)
    return pl.pallas_call(
        kernel,
        grid=(rows // step,),
        in_specs=[pl.BlockSpec((frames, step, cols, channels), lambda i: (0, i, 0, 0))],
        out_specs=[
            pl.BlockSpec((step, cols, frames, channels), lambda i: (i, 0, 0, 0)),
            pl.BlockSpec((step, frames, channels), lambda i: (i, 0, 0)),
            pl.BlockSpec((step, frames, channels), lambda i: (i, 0, 0)),
        ],
        out_shape=[jax.ShapeDtypeStruct((rows, cols, frames, channels), BF16), edge, edge],
        compiler_params=params(),
        cost_estimate=cost(0, 2 * video.size * 2),
        name="to_pixels",
    )(video)


def spatial_conv(pixels, left, right, above, below, w_space):
    rows, cols, frames, channels = pixels.shape
    taps = 9
    span = 2
    count = span * cols * frames

    def kernel(p_ref, l_ref, r_ref, a_ref, b_ref, w_ref, out_ref, first_ref, last_ref, pad, acc):
        pad[0] = a_ref[...]
        pad[rows + 1] = b_ref[...]
        for r in range(rows):
            pad[r + 1, 0] = l_ref[r]
            pad[r + 1, pl.ds(1, cols)] = p_ref[r]
            pad[r + 1, cols + 1] = r_ref[r]

        def body(i, carry):
            base = i * span
            pieces = []
            for row_step in range(3):
                for col_step in range(3):
                    piece = pad[pl.ds(base + row_step, span), pl.ds(col_step, cols)]
                    pieces.append(piece.reshape(count, channels))
            window = jnp.concatenate(pieces, axis=1)
            total = jnp.dot(window, w_ref[...], preferred_element_type=F32)
            out_ref[pl.ds(base, span)] = total.astype(BF16).reshape(span, cols, frames, channels)
            for j in range(channels // 128):
                acc[j] = total[:, 128 * j : 128 * (j + 1)]
            chunk = span * cols
            for ref, frame in ((first_ref, 0), (last_ref, frames - 1)):
                picked = [
                    acc[j, pl.ds(frame, chunk, stride=frames)]
                    for j in range(channels // 128)
                ]
                ref[pl.ds(i * chunk, chunk)] = jnp.concatenate(picked, axis=1).astype(BF16)
            return carry

        lax.fori_loop(0, rows // span, body, 0)

    edge = jax.ShapeDtypeStruct((rows * cols, channels), BF16)
    size = rows * cols * frames * channels
    return pl.pallas_call(
        kernel,
        out_shape=[jax.ShapeDtypeStruct((rows, cols, frames, channels), BF16), edge, edge],
        scratch_shapes=[
            pltpu.VMEM((rows + 2, cols + 2, frames, channels), BF16),
            pltpu.VMEM((channels // 128, count, 128), F32),
        ],
        compiler_params=params(),
        cost_estimate=cost(2 * size * channels * taps, 4 * size),
        name="spatial_conv",
    )(pixels, left, right, above, below, w_space.reshape(taps * channels, channels))


def temporal_conv(me, spatial, before, after, w_time):
    pixels, frames, channels = spatial.shape
    parts = lax.axis_size("tm")
    quarter = pixels // parts
    chunk = 16
    count = chunk * frames
    per_group = channels // GROUPS

    def kernel(me_ref, s_ref, b_ref, a_ref, w_ref, *rest):
        outs, stats_ref = rest[:parts], rest[parts]
        row = lax.broadcasted_iota(jnp.int32, (count, channels), 0) % frames
        stats_ref[...] = jnp.zeros_like(stats_ref)
        for d in range(parts):
            start = lax.rem(me_ref[0] + d, parts) * quarter

            def body(i, carry):
                base = start + i * chunk
                x = s_ref[pl.ds(base, chunk)].reshape(count, channels)
                xf = x.astype(F32)
                prev = b_ref[pl.ds(pl.multiple_of(base, chunk), chunk)].astype(F32)
                nxt = a_ref[pl.ds(pl.multiple_of(base, chunk), chunk)].astype(F32)
                shape = (chunk, frames, channels)
                prev = jnp.broadcast_to(prev[:, None, :], shape).reshape(count, channels)
                nxt = jnp.broadcast_to(nxt[:, None, :], shape).reshape(count, channels)
                down = jnp.where(row == 0, prev, pltpu.roll(xf, 1, 0)).astype(BF16)
                up = jnp.where(row == frames - 1, nxt, pltpu.roll(xf, count - 1, 0)).astype(BF16)
                window = jnp.concatenate([down, x, up], axis=1)
                total = xf + jnp.dot(window, w_ref[...], preferred_element_type=F32)
                rounded = total.astype(BF16)
                outs[d][pl.ds(i * chunk, chunk)] = rounded.reshape(shape)
                kept = rounded.astype(F32)
                stats_ref[0:1] += jnp.sum(kept, axis=0, keepdims=True)
                stats_ref[1:2] += jnp.sum(kept * kept, axis=0, keepdims=True)
                return carry

            lax.fori_loop(0, quarter // chunk, body, 0)
        same = (
            lax.broadcasted_iota(jnp.int32, (channels, channels), 0) // per_group
            == lax.broadcasted_iota(jnp.int32, (channels, channels), 1) // per_group
        ).astype(F32)
        stats_ref[...] = jnp.dot(
            stats_ref[...], same, precision=lax.Precision.HIGHEST, preferred_element_type=F32
        )

    vmem = pl.BlockSpec(memory_space=pltpu.VMEM)
    size = pixels * frames * channels
    res = pl.pallas_call(
        kernel,
        in_specs=[pl.BlockSpec(memory_space=pltpu.SMEM)] + [vmem] * 4,
        out_specs=[vmem] * (parts + 1),
        out_shape=[jax.ShapeDtypeStruct((quarter, frames, channels), BF16)] * parts
        + [jax.ShapeDtypeStruct((8, channels), F32)],
        compiler_params=params(),
        cost_estimate=cost(2 * size * channels * 3, 4 * size),
        name="temporal_conv",
    )(me, spatial, before, after, w_time.reshape(3 * channels, channels))
    return res[:parts], res[parts]


def attention(blocks, stats, gain, bias, w_qkv, w_out, cell_count):
    parts = len(blocks)
    pixels, frames, channels = blocks[0].shape
    length = parts * frames
    group = 8
    head = channels // HEADS
    half = channels // 2
    per_half = HEADS // 2
    factor = math.log2(math.e) / math.sqrt(head)

    def kernel(*refs):
        ins, refs = refs[:parts], refs[parts:]
        stats_ref, gain_ref, bias_ref, qkv_ref, out_w_ref = refs[:5]
        outs = refs[5:]
        mean = stats_ref[0:1] / cell_count
        var = jnp.maximum(stats_ref[1:2] / cell_count - mean * mean, 0.0)
        scale = lax.rsqrt(var + 1e-05) * gain_ref[...]
        x = jnp.concatenate([ref[...] for ref in ins], axis=1).astype(F32)
        x = x.reshape(group * length, channels)
        v = (x - mean) * scale + bias_ref[...]
        normed = (v * (0.5 + 0.5 * jnp.tanh(0.5 * v))).astype(BF16)
        projected = jnp.dot(normed, qkv_ref[...], preferred_element_type=F32).astype(BF16)
        lane = lax.broadcasted_iota(jnp.int32, (length, channels), 1)
        halves = [(lane // half) == i for i in range(2)]
        heads = [((lane // head) % per_half) == i for i in range(per_half)]
        zero = jnp.zeros((length, channels), BF16)
        contexts = []
        for g in range(group):
            rows = slice(g * length, (g + 1) * length)
            q = projected[rows, :channels]
            k = projected[rows, channels : 2 * channels]
            val = projected[rows, 2 * channels :]
            qm = jnp.concatenate([jnp.where(m, q, zero) for m in halves], axis=0)
            km = jnp.concatenate([jnp.where(m, k, zero) for m in heads], axis=0)
            vm = jnp.concatenate([jnp.where(m, val, zero) for m in heads], axis=0)
            scores = lax.dot_general(
                km, qm, (((1,), (1,)), ((), ())), preferred_element_type=F32
            ).reshape(per_half, length, 2 * length)
            top = jnp.max(scores, axis=1, keepdims=True)
            e = jnp.exp2((scores - top) * factor)
            weights = (e * (1.0 / jnp.sum(e, axis=1, keepdims=True))).astype(BF16)
            mixed = lax.dot_general(
                weights.reshape(per_half * length, 2 * length),
                vm,
                (((0,), (0,)), ((), ())),
                preferred_element_type=F32,
            )
            contexts.append(
                jnp.concatenate([mixed[:length, :half], mixed[length:, half:]], axis=1).astype(BF16)
            )
        context = jnp.concatenate(contexts, axis=0)
        result = normed.astype(F32) + jnp.dot(
            context, out_w_ref[...], preferred_element_type=F32
        )
        result = result.astype(BF16).reshape(group, parts, frames, channels)
        for d in range(parts):
            outs[d][...] = result[:, d]

    block = pl.BlockSpec((group, frames, channels), lambda i: (i, 0, 0))

    def whole(a):
        return pl.BlockSpec(a.shape, lambda i: (0,) * a.ndim)

    rest = (stats, gain, bias, w_qkv, w_out)
    size = parts * pixels * frames * channels
    return pl.pallas_call(
        kernel,
        grid=(pixels // group,),
        in_specs=[block] * parts + [whole(a) for a in rest],
        out_specs=[block] * parts,
        out_shape=[jax.ShapeDtypeStruct((pixels, frames, channels), BF16)] * parts,
        compiler_params=params(),
        cost_estimate=cost(2 * size * channels * 8, 4 * size, size * 3),
        name="attention",
    )(*blocks, *rest)


def from_pixels(me, blocks, rows, cols):
    parts = len(blocks)
    pixels, frames, channels = blocks[0].shape
    part_rows = pixels // cols

    def kernel(me_ref, *refs):
        ins, out_ref = refs[:parts], refs[parts]
        for d in range(parts):
            base = lax.rem(me_ref[0] + d, parts) * part_rows
            for r in range(part_rows):
                out_ref[:, base + r] = jnp.swapaxes(ins[d][pl.ds(r * cols, cols)], 0, 1)

    vmem = pl.BlockSpec(memory_space=pltpu.VMEM)
    return pl.pallas_call(
        kernel,
        in_specs=[pl.BlockSpec(memory_space=pltpu.SMEM)] + [vmem] * parts,
        out_specs=vmem,
        out_shape=jax.ShapeDtypeStruct((frames, rows, cols, channels), BF16),
        compiler_params=params(),
        cost_estimate=cost(0, 4 * parts * pixels * frames * channels),
        name="from_pixels",
    )(me, *blocks)


def rotate(value, step):
    size = lax.axis_size("tm")
    return lax.ppermute(value, "tm", [(i, (i + step) % size) for i in range(size)])


def summed(stats):
    for axis in ("width_1", "tm", "height", "width_0"):
        size = lax.axis_size(axis)
        step = 1
        while step < size:
            stats = stats + lax.ppermute(stats, axis, [(i, i ^ step) for i in range(size)])
            step *= 2
    return stats


def per_device(video, w_space, w_time, norm_gain, norm_bias, w_qkv, w_out):
    frames, rows, cols, channels = video.shape
    parts = lax.axis_size("tm")
    me = lax.axis_index("tm").astype(jnp.int32).reshape(1)
    pixels, first, last = to_pixels(video)
    left = shift(last, WIDTH, 1)
    right = shift(first, WIDTH, -1)

    def border(r):
        return jnp.concatenate([left[r][None], pixels[r], right[r][None]], axis=0)

    above = shift(border(rows - 1), "height", 1)
    below = shift(border(0), "height", -1)
    spatial, early, late = spatial_conv(pixels, left, right, above, below, w_space)
    before = shift(late, "tm", 1)
    after = shift(early, "tm", -1)
    blocks, stats = temporal_conv(
        me, spatial.reshape(rows * cols, frames, channels), before, after, w_time
    )
    moved = [blocks[0]] + [rotate(blocks[d], d) for d in range(1, parts)]
    stats = summed(stats)
    cell_count = float(
        frames * parts * rows * lax.axis_size("height") * cols * lax.axis_size(WIDTH)
        * (channels // GROUPS)
    )
    results = attention(
        moved, stats, norm_gain.reshape(1, -1), norm_bias.reshape(1, -1), w_qkv, w_out, cell_count
    )
    back = [results[0]] + [rotate(results[d], -d) for d in range(1, parts)]
    return from_pixels(me, back, rows, cols)


def solution(mesh):
    torus = Mesh(
        mesh.devices.reshape(mesh.shape["tm"], mesh.shape["height"], 8, 2),
        ("tm", "height", "width_0", "width_1"),
    )
    in_specs = (P("tm", "height", WIDTH, None), P(), P(), P(), P(), P(), P())
    out_specs = P("tm", "height", WIDTH, None)
    return jax.shard_map(
        per_device, mesh=torus, in_specs=in_specs, out_specs=out_specs, check_vma=False
    )
```

time: 275 us -> 164 us (0.60)
  blocking collectives: 102 us -> 0 us
  local copies, waits for them, and re-layouts: 76.3 us -> 4.26 us
  waiting for transfers between devices: 7.44 us -> 64.2 us
  Pallas kernels: 0 us -> 50.9 us
  matrix products: 38.9 us -> 0 us
  other arithmetic: 30.8 us -> 1.36 us
  starting transfers between devices: 18.1 us -> 41.2 us
    ppermute x6 -> x20, waiting for transfers between devices: 7.44 us -> 64.2 us  [the longest x8 31.3 us: summed(): lax.ppermute(stats, axis, [(i, i ^ step) for i in range(size)])]
    all_to_all x2 -> x0, blocking collectives: 56.4 us -> none  [the longest x1 28.6 us: per_device(): lax.all_to_all(slotted, 'tm', split_axis=1, concat_axis=0, tiled=True)]
    pallas_call x0 -> x5, Pallas kernels: none -> 50.9 us  [the longest x1 25.8 us: attention(): pl.pallas_call(kernel, grid=(pixels // group,), in_specs=[block] * parts...]
    psum x4 -> x0, blocking collectives: 45.4 us -> none  [by_axis(): value = lax.psum(value, axis)]
    dot_general x16 -> x0, matrix products: 38.9 us -> none  [the longest x1 11.6 us: attend(): jnp.einsum('fphd,gphd->phfg', projected[:, :, 0], projected[:, :, 1], pre...]
    reshape x2 -> x0, local copies, waits for them, and re-layouts: 24.5 us -> none  [the longest x1 17.9 us: attend(): projected = projected.reshape(frames, pixels, 3, HEADS, head_size)]
    ppermute x6 -> x20, starting transfers between devices: 18.1 us -> 41.2 us  [the longest x8 16.8 us: summed(): lax.ppermute(stats, axis, [(i, i ^ step) for i in range(size)])]
    unnamed x20 -> x24, local copies, waits for them, and re-layouts: 22.5 us -> 3.27 us
  transfers between devices with their start and end apart: 6 -> 20, of which waited for: 5 -> 16; matrix products, arithmetic and copies ran while one was open for 0% -> 1% of each run, Pallas kernels for 0% -> 0%
where the time goes in v1:
time: 164 us; the launch traced here: 162 us
  waiting for transfers between devices  64.2 us (39%)
  Pallas kernels  50.9 us (31%)
  starting transfers between devices  41.2 us (25%)
  local copies, waits for them, and re-layouts  4.26 us (3%)
    ppermute x8, waiting for transfers between devices, summed(): lax.ppermute(stats, axis, [(i, i ^ step) for i in range(size)])  31.3 us
    pallas_call x1, Pallas kernels, attention(): pl.pallas_call(kernel, grid=(pixels // group,), in_specs=[block] * parts...  25.8 us
    ppermute x6, waiting for transfers between devices, rotate(): lax.ppermute(value, 'tm', [(i, (i + step) % size) for i in range(size)])  22.4 us
    ppermute x8, starting transfers between devices, summed(): lax.ppermute(stats, axis, [(i, i ^ step) for i in range(size)])  16.8 us
    ppermute x6, starting transfers between devices, shift(): return lax.ppermute(value, axis, pairs)  16.5 us
    ppermute x6, waiting for transfers between devices, shift(): return lax.ppermute(value, axis, pairs)  10.5 us
    pallas_call x1, Pallas kernels, spatial_conv(): pl.pallas_call(kernel, out_shape=[jax.ShapeDtypeStruct((rows, cols, frame...  10.1 us
    ppermute x6, starting transfers between devices, rotate(): lax.ppermute(value, 'tm', [(i, (i + step) % size) for i in range(size)])  7.89 us
  transfers between devices with their start and end apart: 20, of which 16 were waited for; matrix products, arithmetic and copies ran while one was open for 1% of the time, Pallas kernels for 0%

profile of v1, /device:TPU:1, one launch (start us, length us, event | category | flops | bytes accessed | tf_op | source)
XLA Modules:
  0.0 162.1 jit_solution(15831899990758109172)
XLA Ops:
  0.0 4.0 %to_pixels.1 = (bf16[16,16,16,256]{3,2,1,0:T(8,128)(2,1)}, bf16[16,16,256]{2,1,0:T(8,128)(2,1)}, bf16[16,16,256]{2,1,0:T(8,128)(2,1)}) custom-call(bf16[16,16,16,256]{3,2,1,0:T(8,128)(2,1)} %v_ref.1), custom_call_target="tpu_custom_call" | custom-call | bytes 4194304 | tf_op jit(solution)/shard_map/to_pixels/pallas_call | solution.py:49
  4.0 4.9 %collective-permute-start = (bf16[16,16,256]{2,1,0:T(8,128)(2,1)}, bf16[16,16,256]{2,1,0:T(8,128)(2,1)S(1)}, u32[]{:S(2)}, u32[]{:S(2)}) collective-permute-start(bf16[16,16,256]{2,1,0:T(8,128)(2,1)} %get-tuple-element.21), channel_id=1, source_target_pairs={{0,1},{1,2},{2,3},{3,4},{4,5},{5,6},{6,7},{7,8},{8,9},{9,10},{10,1... | collective-permute-start | bytes 393224 | tf_op jit(solution)/shard_map/ppermute | solution.py:34
  8.9 1.9 %collective-permute-start.1 = (bf16[16,16,256]{2,1,0:T(8,128)(2,1)}, bf16[16,16,256]{2,1,0:T(8,128)(2,1)S(1)}, u32[]{:S(2)}, u32[]{:S(2)}) collective-permute-start(bf16[16,16,256]{2,1,0:T(8,128)(2,1)} %get-tuple-element.22), channel_id=1, source_target_pairs={{1,0},{2,1},{3,2},{4,3},{5,4},{6,5},{7,6},{8,7},{9,8},{10,9},{11,1... | collective-permute-start | bytes 393224 | tf_op jit(solution)/shard_map/ppermute | solution.py:34
  10.8 1.0 slice_bitcast_fusion
  11.8 0.0 collective-permute-done.l_ref
  11.8 0.0 copy-start.3
  11.8 3.5 %collective-permute-done.1.r_ref = bf16[16,16,256]{2,1,0:T(8,128)(2,1)S(1)} collective-permute-done((bf16[16,16,256]{2,1,0:T(8,128)(2,1)}, bf16[16,16,256]{2,1,0:T(8,128)(2,1)S(1)}, u32[]{:S(2)}, u32[]{:S(2)}) %collective-permute-start.1) | collective-permute-done | bytes 131104 | tf_op jit(solution)/shard_map/ppermute | solution.py:34
  15.4 0.0 copy-start.4
  15.4 1.3 collective-permute-start.3
  16.8 4.0 %collective-permute-start.2 = (bf16[18,16,256]{2,1,0:T(8,128)(2,1)S(1)}, bf16[18,16,256]{2,1,0:T(8,128)(2,1)S(1)}, u32[]{:S(2)}, u32[]{:S(2)}) collective-permute-start(bf16[18,16,256]{2,1,0:T(8,128)(2,1)S(1)} %pad_maximum_fusion), channel_id=1, source_target_pairs={{0,16},{16,32},{32,48},{1,17},{17,33},{33,49},{2,18},{18,34},{34,5... | collective-permute-start | bytes 442376 | tf_op jit(solution)/shard_map/ppermute | solution.py:34
  20.8 0.6 collective-permute-done.3.b_ref
  21.3 1.5 collective-permute-done.2.a_ref
  22.8 0.0 copy-done.3
  22.8 0.0 copy-done.4
  22.8 0.0 copy-done.8
  22.8 0.6 copy-done.9
  23.5 10.1 %spatial_conv.1 = (bf16[16,16,16,256]{3,2,1,0:T(8,128)(2,1)}, bf16[256,256]{1,0:T(8,128)(2,1)}, bf16[256,256]{1,0:T(8,128)(2,1)}) custom-call(bf16[16,16,16,256]{3,2,1,0:T(8,128)(2,1)} %get-tuple-element.20.p_ref, bf16[16,16,256]{2,1,0:T(8,128)(2,1)} %copy-done.3, bf16[16,16,256]{2,1,0:T(8,128)(2,1)} %copy-done.4, bf16[18,16,256]{2,1,0:T(8,128)(2,1)} %copy-done.9, ...), custom_call_target="tpu_custom_call" | custom-call | flops 4831838208 | bytes 4194304 | tf_op jit(solution)/shard_map/spatial_conv/pallas_call | solution.py:104
  33.6 3.1 %collective-permute-start.4 = (bf16[256,256]{1,0:T(8,128)(2,1)}, bf16[256,256]{1,0:T(8,128)(2,1)S(1)}, u32[]{:S(2)}, u32[]{:S(2)}) collective-permute-start(bf16[256,256]{1,0:T(8,128)(2,1)} %get-tuple-element.24), channel_id=1, source_target_pairs={{0,64},{64,128},{128,192},{1,65},{65,129},{129,193},{2,66},{66,130... | collective-permute-start | bytes 393224 | tf_op jit(solution)/shard_map/ppermute | solution.py:34
  36.8 1.3 collective-permute-start.5
  38.1 0.9 collective-permute-done.4.b_ref
  39.0 3.9 %collective-permute-done.5.a_ref = bf16[256,256]{1,0:T(8,128)(2,1)S(1)} collective-permute-done((bf16[256,256]{1,0:T(8,128)(2,1)}, bf16[256,256]{1,0:T(8,128)(2,1)S(1)}, u32[]{:S(2)}, u32[]{:S(2)}) %collective-permute-start.5) | collective-permute-done | bytes 131104 | tf_op jit(solution)/shard_map/ppermute | solution.py:34
  42.9 0.0 copy-done.10
  42.9 0.7 copy-done.11
  43.6 7.6 %temporal_conv.1 = (bf16[64,16,256]{2,1,0:T(8,128)(2,1)}, bf16[64,16,256]{2,1,0:T(8,128)(2,1)}, bf16[64,16,256]{2,1,0:T(8,128)(2,1)}, bf16[64,16,256]{2,1,0:T(8,128)(2,1)}, f32[8,256]{1,0:T(8,128)}) custom-call(s32[1]{0:T(128)} %bitcast.me_ref, bf16[256,16,256]{2,1,0:T(8,128)(2,1)} %bitcast.14, bf16[256,256]{1,0:T(8,128)(2,1)} %copy-done.10, ...), custom_call_target="tpu_custom_call" | custom-call | flops 1610612736 | bytes 4194304 | tf_op jit(solution)/shard_map/temporal_conv/pallas_call | solution.py:163
  51.2 1.2 collective-permute-start.6
  52.4 1.2 collective-permute-start.7
  53.7 2.1 %collective-permute-start.8 = (bf16[64,16,256]{2,1,0:T(8,128)(2,1)}, bf16[64,16,256]{2,1,0:T(8,128)(2,1)S(1)}, u32[]{:S(2)}, u32[]{:S(2)}) collective-permute-start(bf16[64,16,256]{2,1,0:T(8,128)(2,1)} %get-tuple-element.29), channel_id=1, source_target_pairs={{0,192},{64,0},{128,64},{192,128},{1,193},{65,1},{129,65},{193,129... | collective-permute-start | bytes 1572872 | tf_op jit(solution)/shard_map/ppermute | solution.py:279
  55.8 0.4 collective-permute-start.9
  56.1 1.0 collective-permute-done.9
  57.2 0.7 add.24
  57.9 0.0 collective-permute-start.10
  57.9 20.5 %collective-permute-done.10 = f32[8,256]{1,0:T(8,128)S(1)} collective-permute-done((f32[8,256]{1,0:T(8,128)S(1)}, f32[8,256]{1,0:T(8,128)S(1)}, u32[]{:S(2)}, u32[]{:S(2)}) %collective-permute-start.10) | collective-permute-done | bytes 8224 | tf_op jit(solution)/shard_map/ppermute | solution.py:287
  78.4 2.5 %collective-permute-start.11 = (f32[8,256]{1,0:T(8,128)S(1)}, f32[8,256]{1,0:T(8,128)S(1)}, u32[]{:S(2)}, u32[]{:S(2)}) collective-permute-start(f32[8,256]{1,0:T(8,128)S(1)} %add.25), channel_id=1, source_target_pairs={{0,128},{64,192},{128,0},{192,64},{1,129},{65,193},{129,1},{193,65... | collective-permute-start | bytes 24584 | tf_op jit(solution)/shard_map/ppermute | solution.py:287
  80.8 1.5 collective-permute-done.11
  82.4 1.9 %collective-permute-start.12 = (f32[8,256]{1,0:T(8,128)S(1)}, f32[8,256]{1,0:T(8,128)S(1)}, u32[]{:S(2)}, u32[]{:S(2)}) collective-permute-start(f32[8,256]{1,0:T(8,128)S(1)} %add.26), channel_id=1, source_target_pairs={{0,16},{16,0},{32,48},{48,32},{1,17},{17,1},{33,49},{49,33},{2,18}... | collective-permute-start | bytes 24584 | tf_op jit(solution)/shard_map/ppermute | solution.py:287
  84.3 1.0 collective-permute-done.12
  85.3 3.1 %collective-permute-start.13 = (f32[8,256]{1,0:T(8,128)S(1)}, f32[8,256]{1,0:T(8,128)S(1)}, u32[]{:S(2)}, u32[]{:S(2)}) collective-permute-start(f32[8,256]{1,0:T(8,128)S(1)} %add.27), channel_id=1, source_target_pairs={{0,32},{16,48},{32,0},{48,16},{1,33},{17,49},{33,1},{49,17},{2,34}... | collective-permute-start | bytes 24584 | tf_op jit(solution)/shard_map/ppermute | solution.py:287
  88.4 1.0 collective-permute-done.13
  89.4 2.0 %collective-permute-start.14 = (f32[8,256]{1,0:T(8,128)S(1)}, f32[8,256]{1,0:T(8,128)S(1)}, u32[]{:S(2)}, u32[]{:S(2)}) collective-permute-start(f32[8,256]{1,0:T(8,128)S(1)} %add.28), channel_id=1, source_target_pairs={{0,2},{2,0},{4,6},{6,4},{8,10},{10,8},{12,14},{14,12},{1,3},{3,1},... | collective-permute-start | bytes 24584 | tf_op jit(solution)/shard_map/ppermute | solution.py:287
  91.5 1.3 collective-permute-done.14
  92.8 4.4 %collective-permute-start.15 = (f32[8,256]{1,0:T(8,128)S(1)}, f32[8,256]{1,0:T(8,128)S(1)}, u32[]{:S(2)}, u32[]{:S(2)}) collective-permute-start(f32[8,256]{1,0:T(8,128)S(1)} %add.29), channel_id=1, source_target_pairs={{0,4},{2,6},{4,0},{6,2},{8,12},{10,14},{12,8},{14,10},{1,5},{3,7},... | collective-permute-start | bytes 24584 | tf_op jit(solution)/shard_map/ppermute | solution.py:287
  97.2 1.0 collective-permute-done.15
  98.2 2.6 %collective-permute-start.16 = (f32[8,256]{1,0:T(8,128)S(1)}, f32[8,256]{1,0:T(8,128)S(1)}, u32[]{:S(2)}, u32[]{:S(2)}) collective-permute-start(f32[8,256]{1,0:T(8,128)S(1)} %add.30), channel_id=1, source_target_pairs={{0,8},{2,10},{4,12},{6,14},{8,0},{10,2},{12,4},{14,6},{1,9},{3,11}... | collective-permute-start | bytes 24584 | tf_op jit(solution)/shard_map/ppermute | solution.py:287
  100.8 3.8 %collective-permute-done.16 = f32[8,256]{1,0:T(8,128)S(1)} collective-permute-done((f32[8,256]{1,0:T(8,128)S(1)}, f32[8,256]{1,0:T(8,128)S(1)}, u32[]{:S(2)}, u32[]{:S(2)}) %collective-permute-start.16) | collective-permute-done | bytes 8224 | tf_op jit(solution)/shard_map/ppermute | solution.py:287
  104.6 0.6 add.31.refs_4_
  105.2 0.0 collective-permute-done.6.refs_1_
  105.2 0.0 collective-permute-done.7.refs_2_
  105.2 0.0 copy-start.6
  105.3 0.0 collective-permute-done.8.refs_3_
  105.3 0.0 copy-start.7
  105.3 0.8 copy-done.5
  106.0 0.2 copy-done.6
  106.2 0.2 copy-done.7
  106.4 25.8 %attention.1 = (bf16[64,16,256]{2,1,0:T(8,128)(2,1)}, bf16[64,16,256]{2,1,0:T(8,128)(2,1)}, bf16[64,16,256]{2,1,0:T(8,128)(2,1)}, bf16[64,16,256]{2,1,0:T(8,128)(2,1)}) custom-call(bf16[64,16,256]{2,1,0:T(8,128)(2,1)} %get-tuple-element.26.refs_0_, bf16[64,16,256]{2,1,0:T(8,128)(2,1)} %copy-done.5, bf16[64,16,256]{2,1,0:T(8,128)(2,1)} %copy-done.6, ...), custom_call_target="tpu_custom_call" | custom-call | flops 4294967296 | bytes 4194304 | tf_op jit(solution)/shard_map/attention/pallas_call | solution.py:241
  132.2 0.9 collective-permute-start.17
  133.1 1.7 %collective-permute-start.18 = (bf16[64,16,256]{2,1,0:T(8,128)(2,1)}, bf16[64,16,256]{2,1,0:T(8,128)(2,1)S(1)}, u32[]{:S(2)}, u32[]{:S(2)}) collective-permute-start(bf16[64,16,256]{2,1,0:T(8,128)(2,1)} %get-tuple-element.33), channel_id=1, source_target_pairs={{0,128},{64,192},{128,0},{192,64},{1,129},{65,193},{129,1},{193,65... | collective-permute-start | bytes 1572872 | tf_op jit(solution)/shard_map/ppermute | solution.py:279
  134.8 0.8 collective-permute-start.19
  135.6 4.9 %collective-permute-done.17.refs_1_ = bf16[64,16,256]{2,1,0:T(8,128)(2,1)S(1)} collective-permute-done((bf16[64,16,256]{2,1,0:T(8,128)(2,1)}, bf16[64,16,256]{2,1,0:T(8,128)(2,1)S(1)}, u32[]{:S(2)}, u32[]{:S(2)}) %collective-permute-start.17) | collective-permute-done | bytes 524320 | tf_op jit(solution)/shard_map/ppermute | solution.py:279
  140.5 2.4 %collective-permute-done.18.refs_2_ = bf16[64,16,256]{2,1,0:T(8,128)(2,1)S(1)} collective-permute-done((bf16[64,16,256]{2,1,0:T(8,128)(2,1)}, bf16[64,16,256]{2,1,0:T(8,128)(2,1)S(1)}, u32[]{:S(2)}, u32[]{:S(2)}) %collective-permute-start.18) | collective-permute-done | bytes 524320 | tf_op jit(solution)/shard_map/ppermute | solution.py:279
  142.9 15.0 %collective-permute-done.19.refs_3_ = bf16[64,16,256]{2,1,0:T(8,128)(2,1)S(1)} collective-permute-done((bf16[64,16,256]{2,1,0:T(8,128)(2,1)}, bf16[64,16,256]{2,1,0:T(8,128)(2,1)S(1)}, u32[]{:S(2)}, u32[]{:S(2)}) %collective-permute-start.19) | collective-permute-done | bytes 524320 | tf_op jit(solution)/shard_map/ppermute | solution.py:279
  157.9 0.0 copy-done
  157.9 0.0 copy-done.1
  157.9 0.8 copy-done.2
  158.7 3.4 %from_pixels.1 = bf16[16,16,16,256]{3,2,1,0:T(8,128)(2,1)} custom-call(s32[1]{0:T(128)} %bitcast.me_ref, bf16[64,16,256]{2,1,0:T(8,128)(2,1)} %get-tuple-element.31.refs_0_, bf16[64,16,256]{2,1,0:T(8,128)(2,1)} %copy-done, bf16[64,16,256]{2,1,0:T(8,128)(2,1)} %copy-done.1, bf16[64,16,256]{2,1,0:T(8,128)(2,1)} %copy-done.2), custom_call_target="tpu_custom_call" | custom-call | bytes 4194304 | tf_op jit(solution)/shard_map/from_pixels/pallas_call | solution.py:266
  (18 shorter events, 0.1 us)
Async XLA Ops:
  4.0 7.8 %collective-permute-start = (bf16[16,16,256]{2,1,0:T(8,128)(2,1)}, bf16[16,16,256]{2,1,0:T(8,128)(2,1)S(1)}, u32[]{:S(2)}, u32[]{:S(2)}) collective-permute-start(bf16[16,16,256]{2,1,0:T(8,128)(2,1)} %get-tuple-element.21), channel_id=1, source_target_pairs={{0,1},{1,2},{2,3},{3,4},{4,5},{5,6},{6,7},{7,8},{8,9},{9,10},{10,1... | collective-permute-start | bytes 393224 | tf_op jit(solution)/shard_map/ppermute | solution.py:34
  8.9 6.5 %collective-permute-start.1 = (bf16[16,16,256]{2,1,0:T(8,128)(2,1)}, bf16[16,16,256]{2,1,0:T(8,128)(2,1)S(1)}, u32[]{:S(2)}, u32[]{:S(2)}) collective-permute-start(bf16[16,16,256]{2,1,0:T(8,128)(2,1)} %get-tuple-element.22), channel_id=1, source_target_pairs={{1,0},{2,1},{3,2},{4,3},{5,4},{6,5},{7,6},{8,7},{9,8},{10,9},{11,1... | collective-permute-start | bytes 393224 | tf_op jit(solution)/shard_map/ppermute | solution.py:34
  11.8 11.0 %copy-start.3 = (bf16[16,16,256]{2,1,0:T(8,128)(2,1)}, bf16[16,16,256]{2,1,0:T(8,128)(2,1)S(1)}, u32[]{:S(2)}) copy-start(bf16[16,16,256]{2,1,0:T(8,128)(2,1)S(1)} %collective-permute-done.l_ref) | copy-start | bytes 393220
  15.4 7.4 %copy-start.4 = (bf16[16,16,256]{2,1,0:T(8,128)(2,1)}, bf16[16,16,256]{2,1,0:T(8,128)(2,1)S(1)}, u32[]{:S(2)}) copy-start(bf16[16,16,256]{2,1,0:T(8,128)(2,1)S(1)} %collective-permute-done.1.r_ref) | copy-start | bytes 393220
  15.4 5.9 %collective-permute-start.3 = (bf16[18,16,256]{2,1,0:T(8,128)(2,1)S(1)}, bf16[18,16,256]{2,1,0:T(8,128)(2,1)S(1)}, u32[]{:S(2)}, u32[]{:S(2)}) collective-permute-start(bf16[18,16,256]{2,1,0:T(8,128)(2,1)S(1)} %pad_maximum_fusion.1), channel_id=1, source_target_pairs={{16,0},{32,16},{48,32},{17,1},{33,17},{49,33},{18,2},{34,18},{50,3... | collective-permute-start | bytes 442376 | tf_op jit(solution)/shard_map/ppermute | solution.py:34
  16.8 6.1 %collective-permute-start.2 = (bf16[18,16,256]{2,1,0:T(8,128)(2,1)S(1)}, bf16[18,16,256]{2,1,0:T(8,128)(2,1)S(1)}, u32[]{:S(2)}, u32[]{:S(2)}) collective-permute-start(bf16[18,16,256]{2,1,0:T(8,128)(2,1)S(1)} %pad_maximum_fusion), channel_id=1, source_target_pairs={{0,16},{16,32},{32,48},{1,17},{17,33},{33,49},{2,18},{18,34},{34,5... | collective-permute-start | bytes 442376 | tf_op jit(solution)/shard_map/ppermute | solution.py:34
  21.3 1.5 copy-start.8
  22.8 0.7 copy-start.9
  33.6 5.4 %collective-permute-start.4 = (bf16[256,256]{1,0:T(8,128)(2,1)}, bf16[256,256]{1,0:T(8,128)(2,1)S(1)}, u32[]{:S(2)}, u32[]{:S(2)}) collective-permute-start(bf16[256,256]{1,0:T(8,128)(2,1)} %get-tuple-element.24), channel_id=1, source_target_pairs={{0,64},{64,128},{128,192},{1,65},{65,129},{129,193},{2,66},{66,130... | collective-permute-start | bytes 393224 | tf_op jit(solution)/shard_map/ppermute | solution.py:34
  36.8 6.2 %collective-permute-start.5 = (bf16[256,256]{1,0:T(8,128)(2,1)}, bf16[256,256]{1,0:T(8,128)(2,1)S(1)}, u32[]{:S(2)}, u32[]{:S(2)}) collective-permute-start(bf16[256,256]{1,0:T(8,128)(2,1)} %get-tuple-element.25), channel_id=1, source_target_pairs={{64,0},{128,64},{192,128},{65,1},{129,65},{193,129},{66,2},{130,66... | collective-permute-start | bytes 393224 | tf_op jit(solution)/shard_map/ppermute | solution.py:34
  39.0 3.9 %copy-start.10 = (bf16[256,256]{1,0:T(8,128)(2,1)}, bf16[256,256]{1,0:T(8,128)(2,1)S(1)}, u32[]{:S(2)}) copy-start(bf16[256,256]{1,0:T(8,128)(2,1)S(1)} %collective-permute-done.4.b_ref) | copy-start | bytes 393220
  42.9 0.7 copy-start.11
  51.2 54.0 %collective-permute-start.6 = (bf16[64,16,256]{2,1,0:T(8,128)(2,1)}, bf16[64,16,256]{2,1,0:T(8,128)(2,1)S(1)}, u32[]{:S(2)}, u32[]{:S(2)}) collective-permute-start(bf16[64,16,256]{2,1,0:T(8,128)(2,1)} %get-tuple-element.27), channel_id=1, source_target_pairs={{0,64},{64,128},{128,192},{192,0},{1,65},{65,129},{129,193},{193,1... | collective-permute-start | bytes 1572872 | tf_op jit(solution)/shard_map/ppermute | solution.py:279
  52.4 52.8 %collective-permute-start.7 = (bf16[64,16,256]{2,1,0:T(8,128)(2,1)}, bf16[64,16,256]{2,1,0:T(8,128)(2,1)S(1)}, u32[]{:S(2)}, u32[]{:S(2)}) collective-permute-start(bf16[64,16,256]{2,1,0:T(8,128)(2,1)} %get-tuple-element.28), channel_id=1, source_target_pairs={{0,128},{64,192},{128,0},{192,64},{1,129},{65,193},{129,1},{193,65... | collective-permute-start | bytes 1572872 | tf_op jit(solution)/shard_map/ppermute | solution.py:279
  53.7 51.6 %collective-permute-start.8 = (bf16[64,16,256]{2,1,0:T(8,128)(2,1)}, bf16[64,16,256]{2,1,0:T(8,128)(2,1)S(1)}, u32[]{:S(2)}, u32[]{:S(2)}) collective-permute-start(bf16[64,16,256]{2,1,0:T(8,128)(2,1)} %get-tuple-element.29), channel_id=1, source_target_pairs={{0,192},{64,0},{128,64},{192,128},{1,193},{65,1},{129,65},{193,129... | collective-permute-start | bytes 1572872 | tf_op jit(solution)/shard_map/ppermute | solution.py:279
  55.8 1.4 collective-permute-start.9
  57.9 20.5 %collective-permute-start.10 = (f32[8,256]{1,0:T(8,128)S(1)}, f32[8,256]{1,0:T(8,128)S(1)}, u32[]{:S(2)}, u32[]{:S(2)}) collective-permute-start(f32[8,256]{1,0:T(8,128)S(1)} %add.24), channel_id=1, source_target_pairs={{0,64},{64,0},{128,192},{192,128},{1,65},{65,1},{129,193},{193,129... | collective-permute-start | bytes 24584 | tf_op jit(solution)/shard_map/ppermute | solution.py:287
  78.4 4.0 %collective-permute-start.11 = (f32[8,256]{1,0:T(8,128)S(1)}, f32[8,256]{1,0:T(8,128)S(1)}, u32[]{:S(2)}, u32[]{:S(2)}) collective-permute-start(f32[8,256]{1,0:T(8,128)S(1)} %add.25), channel_id=1, source_target_pairs={{0,128},{64,192},{128,0},{192,64},{1,129},{65,193},{129,1},{193,65... | collective-permute-start | bytes 24584 | tf_op jit(solution)/shard_map/ppermute | solution.py:287
  82.4 2.9 %collective-permute-start.12 = (f32[8,256]{1,0:T(8,128)S(1)}, f32[8,256]{1,0:T(8,128)S(1)}, u32[]{:S(2)}, u32[]{:S(2)}) collective-permute-start(f32[8,256]{1,0:T(8,128)S(1)} %add.26), channel_id=1, source_target_pairs={{0,16},{16,0},{32,48},{48,32},{1,17},{17,1},{33,49},{49,33},{2,18}... | collective-permute-start | bytes 24584 | tf_op jit(solution)/shard_map/ppermute | solution.py:287
  85.3 4.1 %collective-permute-start.13 = (f32[8,256]{1,0:T(8,128)S(1)}, f32[8,256]{1,0:T(8,128)S(1)}, u32[]{:S(2)}, u32[]{:S(2)}) collective-permute-start(f32[8,256]{1,0:T(8,128)S(1)} %add.27), channel_id=1, source_target_pairs={{0,32},{16,48},{32,0},{48,16},{1,33},{17,49},{33,1},{49,17},{2,34}... | collective-permute-start | bytes 24584 | tf_op jit(solution)/shard_map/ppermute | solution.py:287
  89.4 3.4 %collective-permute-start.14 = (f32[8,256]{1,0:T(8,128)S(1)}, f32[8,256]{1,0:T(8,128)S(1)}, u32[]{:S(2)}, u32[]{:S(2)}) collective-permute-start(f32[8,256]{1,0:T(8,128)S(1)} %add.28), channel_id=1, source_target_pairs={{0,2},{2,0},{4,6},{6,4},{8,10},{10,8},{12,14},{14,12},{1,3},{3,1},... | collective-permute-start | bytes 24584 | tf_op jit(solution)/shard_map/ppermute | solution.py:287
  92.8 5.4 %collective-permute-start.15 = (f32[8,256]{1,0:T(8,128)S(1)}, f32[8,256]{1,0:T(8,128)S(1)}, u32[]{:S(2)}, u32[]{:S(2)}) collective-permute-start(f32[8,256]{1,0:T(8,128)S(1)} %add.29), channel_id=1, source_target_pairs={{0,4},{2,6},{4,0},{6,2},{8,12},{10,14},{12,8},{14,10},{1,5},{3,7},... | collective-permute-start | bytes 24584 | tf_op jit(solution)/shard_map/ppermute | solution.py:287
  98.2 6.4 %collective-permute-start.16 = (f32[8,256]{1,0:T(8,128)S(1)}, f32[8,256]{1,0:T(8,128)S(1)}, u32[]{:S(2)}, u32[]{:S(2)}) collective-permute-start(f32[8,256]{1,0:T(8,128)S(1)} %add.30), channel_id=1, source_target_pairs={{0,8},{2,10},{4,12},{6,14},{8,0},{10,2},{12,4},{14,6},{1,9},{3,11}... | collective-permute-start | bytes 24584 | tf_op jit(solution)/shard_map/ppermute | solution.py:287
  105.2 0.8 copy-start.5
  105.2 1.0 copy-start.6
  105.3 1.2 copy-start.7
  132.2 8.3 %collective-permute-start.17 = (bf16[64,16,256]{2,1,0:T(8,128)(2,1)}, bf16[64,16,256]{2,1,0:T(8,128)(2,1)S(1)}, u32[]{:S(2)}, u32[]{:S(2)}) collective-permute-start(bf16[64,16,256]{2,1,0:T(8,128)(2,1)} %get-tuple-element.32), channel_id=1, source_target_pairs={{0,192},{64,0},{128,64},{192,128},{1,193},{65,1},{129,65},{193,129... | collective-permute-start | bytes 1572872 | tf_op jit(solution)/shard_map/ppermute | solution.py:279
  133.1 9.8 %collective-permute-start.18 = (bf16[64,16,256]{2,1,0:T(8,128)(2,1)}, bf16[64,16,256]{2,1,0:T(8,128)(2,1)S(1)}, u32[]{:S(2)}, u32[]{:S(2)}) collective-permute-start(bf16[64,16,256]{2,1,0:T(8,128)(2,1)} %get-tuple-element.33), channel_id=1, source_target_pairs={{0,128},{64,192},{128,0},{192,64},{1,129},{65,193},{129,1},{193,65... | collective-permute-start | bytes 1572872 | tf_op jit(solution)/shard_map/ppermute | solution.py:279
  134.8 23.1 %collective-permute-start.19 = (bf16[64,16,256]{2,1,0:T(8,128)(2,1)}, bf16[64,16,256]{2,1,0:T(8,128)(2,1)S(1)}, u32[]{:S(2)}, u32[]{:S(2)}) collective-permute-start(bf16[64,16,256]{2,1,0:T(8,128)(2,1)} %get-tuple-element.34), channel_id=1, source_target_pairs={{0,64},{64,128},{128,192},{192,0},{1,65},{65,129},{129,193},{193,1... | collective-permute-start | bytes 1572872 | tf_op jit(solution)/shard_map/ppermute | solution.py:279
  140.5 17.4 %copy-start = (bf16[64,16,256]{2,1,0:T(8,128)(2,1)}, bf16[64,16,256]{2,1,0:T(8,128)(2,1)S(1)}, u32[]{:S(2)}) copy-start(bf16[64,16,256]{2,1,0:T(8,128)(2,1)S(1)} %collective-permute-done.17.refs_1_) | copy-start | bytes 1572868
  142.9 15.0 %copy-start.1 = (bf16[64,16,256]{2,1,0:T(8,128)(2,1)}, bf16[64,16,256]{2,1,0:T(8,128)(2,1)S(1)}, u32[]{:S(2)}) copy-start(bf16[64,16,256]{2,1,0:T(8,128)(2,1)S(1)} %collective-permute-done.18.refs_2_) | copy-start | bytes 1572868
  157.9 0.8 copy-start.2

commit v2 on v1

v2 whole, which is shorter than its diff:
```python
import math

import jax
import jax.numpy as jnp
from jax import lax
from jax.experimental import pallas as pl
from jax.experimental.pallas import tpu as pltpu
from jax.sharding import Mesh
from jax.sharding import PartitionSpec as P

HEADS = 8
GROUPS = 32
WIDTH = ("width_0", "width_1")
BF16 = jnp.bfloat16
F32 = jnp.float32
VMEM_BYTES = 60 * 1024 * 1024


def params(**kw):
    return pltpu.CompilerParams(vmem_limit_bytes=VMEM_BYTES, **kw)


def cost(flops, nbytes, trans=0):
    return pl.CostEstimate(flops=flops, bytes_accessed=nbytes, transcendentals=trans)


def shift(value, axis, step):
    size = lax.axis_size(axis)
    if step > 0:
        pairs = [(i, i + 1) for i in range(size - 1)]
    else:
        pairs = [(i + 1, i) for i in range(size - 1)]
    return lax.ppermute(value, axis, pairs)


def edge_columns(video):
    frames, rows, cols, channels = video.shape
    step = 4

    def kernel(v_ref, first_ref, last_ref):
        for r in range(step):
            turned = jnp.swapaxes(v_ref[:, r], 0, 1)
            first_ref[r] = turned[0]
            last_ref[r] = turned[cols - 1]

    return pl.pallas_call(
        kernel,
        grid=(rows // step,),
        in_specs=[pl.BlockSpec((frames, step, cols, channels), lambda i: (0, i, 0, 0))],
        out_specs=[pl.BlockSpec((step, frames, channels), lambda i: (i, 0, 0))] * 2,
        out_shape=[jax.ShapeDtypeStruct((rows, frames, channels), BF16)] * 2,
        compiler_params=params(),
        cost_estimate=cost(0, video.size * 2),
        name="edge_columns",
    )(video)


def to_pixels(video):
    frames, rows, cols, channels = video.shape
    step = 4

    def kernel(v_ref, out_ref):
        for r in range(step):
            out_ref[r] = jnp.swapaxes(v_ref[:, r], 0, 1)

    return pl.pallas_call(
        kernel,
        grid=(rows // step,),
        in_specs=[pl.BlockSpec((frames, step, cols, channels), lambda i: (0, i, 0, 0))],
        out_specs=pl.BlockSpec((step, cols, frames, channels), lambda i: (i, 0, 0, 0)),
        out_shape=jax.ShapeDtypeStruct((rows, cols, frames, channels), BF16),
        compiler_params=params(),
        cost_estimate=cost(0, 2 * video.size * 2),
        name="to_pixels",
    )(video)


def convolve(pad, base, span, cols, w_ref):
    pieces = []
    for row_step in range(3):
        for col_step in range(3):
            piece = pad[pl.ds(base + row_step, span), pl.ds(col_step, cols)]
            pieces.append(piece.reshape(span * cols * piece.shape[2], piece.shape[3]))
    window = jnp.concatenate(pieces, axis=1)
    return jnp.dot(window, w_ref[...], preferred_element_type=F32)


def end_frames(acc, total, frames, count):
    slabs = total.shape[1] // 128
    for j in range(slabs):
        acc[j] = total[:, 128 * j : 128 * (j + 1)]
    return [
        jnp.concatenate(
            [acc[j, pl.ds(frame, count, stride=frames)] for j in range(slabs)], axis=1
        ).astype(BF16)
        for frame in (0, frames - 1)
    ]


def inner_conv(pixels, left, right, w_space):
    rows, cols, frames, channels = pixels.shape
    span = 2
    chunk = span * cols
    count = chunk * frames

    def kernel(p_ref, l_ref, r_ref, w_ref, out_ref, first_ref, last_ref, pad, acc):
        for r in range(rows):
            pad[r, 0] = l_ref[r]
            pad[r, pl.ds(1, cols)] = p_ref[r]
            pad[r, cols + 1] = r_ref[r]

        def body(i, carry):
            base = i * span
            total = convolve(pad, base, span, cols, w_ref)
            out_ref[pl.ds(base + 1, span)] = total.astype(BF16).reshape(span, cols, frames, channels)
            ends = end_frames(acc, total, frames, chunk)
            for ref, value in zip((first_ref, last_ref), ends):
                ref[pl.ds(pl.multiple_of(base * cols + cols, cols), chunk)] = value
            return carry

        lax.fori_loop(0, (rows - 2) // span, body, 0)

    edge = jax.ShapeDtypeStruct((rows * cols, channels), BF16)
    size = (rows - 2) * cols * frames * channels
    return pl.pallas_call(
        kernel,
        out_shape=[jax.ShapeDtypeStruct((rows, cols, frames, channels), BF16), edge, edge],
        scratch_shapes=[
            pltpu.VMEM((rows, cols + 2, frames, channels), BF16),
            pltpu.VMEM((channels // 128, count, 128), F32),
        ],
        compiler_params=params(),
        cost_estimate=cost(2 * size * channels * 9, 4 * size),
        name="inner_conv",
    )(pixels, left, right, w_space)


def outer_conv(pixels, left, right, above, below, w_space, results):
    rows, cols, frames, channels = pixels.shape
    count = cols * frames

    def kernel(p_ref, l_ref, r_ref, a_ref, b_ref, w_ref, *refs):
        outs, (pad, acc, wide, ends, sem) = refs[3:6], refs[6:]
        fetch = [
            pltpu.make_async_copy(
                p_ref.at[pl.ds(start, 2)], pad.at[pl.ds(to, 2), pl.ds(1, cols)], sem.at[i]
            )
            for i, (start, to) in enumerate(((0, 1), (rows - 2, 3)))
        ]
        for copy in fetch:
            copy.start()
        pad[0] = a_ref[...]
        pad[5] = b_ref[...]
        for r, to in ((0, 1), (1, 2), (rows - 2, 3), (rows - 1, 4)):
            pad[to, 0] = l_ref[r]
            pad[to, cols + 1] = r_ref[r]
        for copy in fetch:
            copy.wait()
        copies = []
        for k, row in enumerate((0, rows - 1)):
            total = convolve(pad, 3 * k, 1, cols, w_ref)
            wide[k] = total.astype(BF16).reshape(cols, frames, channels)
            for e, value in enumerate(end_frames(acc.at[k], total, frames, cols)):
                ends[k, e] = value
            copies.append((wide.at[k], outs[0].at[row]))
            for e in range(2):
                copies.append((ends.at[k, e], outs[1 + e].at[pl.ds(row * cols, cols)]))
        started = []
        for i, (source, target) in enumerate(copies):
            copy = pltpu.make_async_copy(source, target, sem.at[2 + i])
            copy.start()
            started.append(copy)
        for copy in started:
            copy.wait()

    anywhere = pl.BlockSpec(memory_space=pl.ANY)
    vmem = pl.BlockSpec(memory_space=pltpu.VMEM)
    size = 2 * cols * frames * channels
    return pl.pallas_call(
        kernel,
        in_specs=[anywhere] + [vmem] * 5 + [anywhere] * 3,
        out_specs=[anywhere] * 3,
        out_shape=[jax.ShapeDtypeStruct(a.shape, a.dtype) for a in results],
        input_output_aliases={6: 0, 7: 1, 8: 2},
        scratch_shapes=[
            pltpu.VMEM((6, cols + 2, frames, channels), BF16),
            pltpu.VMEM((2, channels // 128, count, 128), F32),
            pltpu.VMEM((2, cols, frames, channels), BF16),
            pltpu.VMEM((2, 2, cols, channels), BF16),
            pltpu.SemaphoreType.DMA((8,)),
        ],
        compiler_params=params(),
        cost_estimate=cost(2 * size * channels * 9, 4 * size),
        name="outer_conv",
    )(pixels, left, right, above, below, w_space, *results)


def group_lanes(channels):
    shape = (channels, 128)
    channel = lax.broadcasted_iota(jnp.int32, shape, 0)
    lane = lax.broadcasted_iota(jnp.int32, shape, 1)
    return (channel // (channels // GROUPS) == lane).astype(F32)


def temporal_conv(me, spatial, before, after, w_time):
    pixels, frames, channels = spatial.shape
    parts = lax.axis_size("tm")
    quarter = pixels // parts
    chunk = 16
    count = chunk * frames
    lanes = 128
    slabs = channels // lanes
    pitch = frames + 8
    per_part = quarter // chunk
    steps = parts * per_part

    def kernel(me_ref, s_ref, b_ref, a_ref, w_ref, *rest):
        outs, stats_ref = rest[:parts], rest[parts]
        wides, windows, totals = rest[parts + 1 : parts + 3], rest[parts + 3 : parts + 5], rest[parts + 5 :]

        def base_of(t):
            start = lax.rem(me_ref[0] + t // per_part, parts) * quarter
            return pl.multiple_of(start + (t % per_part) * chunk, chunk)

        def prepare(t):
            base = base_of(t)
            wide, window = wides[t % 2], windows[t % 2]
            x = s_ref[pl.ds(base, chunk)].reshape(count, channels)
            xf = x.astype(F32)
            prev = b_ref[pl.ds(base, chunk)].astype(F32)
            nxt = a_ref[pl.ds(base, chunk)].astype(F32)
            window[:, channels : 2 * channels] = x
            for j in range(slabs):
                cut = slice(j * lanes, (j + 1) * lanes)
                wide[j, pl.ds(7, chunk, stride=pitch)] = prev[:, cut]
                wide[j, pl.ds(pitch, chunk, stride=pitch)] = nxt[:, cut]
                for p in range(chunk):
                    wide[j, pl.ds(p * pitch + 8, frames)] = xf[p * frames : (p + 1) * frames, cut]
            for p in range(chunk):
                for j in range(slabs):
                    for offset, to in ((7, 0), (9, 2)):
                        window[
                            p * frames : (p + 1) * frames,
                            to * channels + j * lanes : to * channels + (j + 1) * lanes,
                        ] = wide[j, pl.ds(p * pitch + offset, frames)].astype(BF16)

        def multiply(t):
            window = windows[t % 2]
            totals[t % 2][...] = jnp.dot(window[...], w_ref[...], preferred_element_type=F32)

        def finish(t, sums):
            x = s_ref[pl.ds(base_of(t), chunk)].reshape(count, channels).astype(F32)
            rounded = (x + totals[t % 2][...]).astype(BF16)
            outs[t // per_part][pl.ds(t % per_part * chunk, chunk)] = rounded.reshape(
                chunk, frames, channels
            )
            kept = rounded.astype(F32).reshape(count // 8, 8, channels)
            return sums[0] + jnp.sum(kept, axis=0), sums[1] + jnp.sum(kept * kept, axis=0)

        sums = (jnp.zeros((8, channels), F32),) * 2
        prepare(0)
        for t in range(steps + 1):
            if t < steps:
                multiply(t)
            if t + 1 < steps:
                prepare(t + 1)
            if t > 0:
                sums = finish(t - 1, sums)
        folded = [jnp.sum(v, axis=0, keepdims=True) for v in sums] + [jnp.zeros((6, channels), F32)]
        stats_ref[...] = jnp.dot(
            jnp.concatenate(folded, axis=0),
            group_lanes(channels),
            precision=lax.Precision.HIGHEST,
            preferred_element_type=F32,
        )

    vmem = pl.BlockSpec(memory_space=pltpu.VMEM)
    size = pixels * frames * channels
    res = pl.pallas_call(
        kernel,
        in_specs=[pl.BlockSpec(memory_space=pltpu.SMEM)] + [vmem] * 4,
        out_specs=[vmem] * (parts + 1),
        out_shape=[jax.ShapeDtypeStruct((quarter, frames, channels), BF16)] * parts
        + [jax.ShapeDtypeStruct((8, 128), F32)],
        scratch_shapes=[pltpu.VMEM((slabs, chunk * pitch + 8, lanes), F32)] * 2
        + [pltpu.VMEM((count, 3 * channels), BF16)] * 2
        + [pltpu.VMEM((count, channels), F32)] * 2,
        compiler_params=params(),
        cost_estimate=cost(2 * size * channels * 3, 4 * size),
        name="temporal_conv",
    )(me, spatial, before, after, w_time.reshape(3 * channels, channels))
    return res[:parts], res[parts]


def attention(blocks, stats, gain, bias, w_qkv, w_out, cell_count, first, pixels):
    parts = len(blocks)
    frames, channels = blocks[0].shape[1:]
    length = parts * frames
    group = 8
    head = channels // HEADS
    half = channels // 2
    per_half = HEADS // 2
    factor = math.log2(math.e) / math.sqrt(head)
    batch = 4

    def kernel(*refs):
        ins, refs = refs[:parts], refs[parts:]
        stats_ref, gain_ref, bias_ref, qkv_ref, out_w_ref = refs[:5]
        outs, refs = refs[5 : 5 + parts], refs[5 + parts :]
        normed, projected, contexts, affine = refs[:2], refs[2:4], refs[4], refs[5]
        spread = lax.dot_general(
            stats_ref[...],
            group_lanes(channels),
            (((1,), (1,)), ((), ())),
            precision=lax.Precision.HIGHEST,
            preferred_element_type=F32,
        )
        mean = spread[0:1] / cell_count
        var = jnp.maximum(spread[1:2] / cell_count - mean * mean, 0.0)
        scale = 0.5 * lax.rsqrt(var + 1e-05) * gain_ref[...]
        affine[0:8] = jnp.broadcast_to(scale, (8, channels))
        affine[8:16] = jnp.broadcast_to(0.5 * bias_ref[...] - mean * scale, (8, channels))
        lane = lax.broadcasted_iota(jnp.int32, (length, channels), 1)
        halves = [(lane // half) == i for i in range(2)]
        heads = [((lane // head) % per_half) == i for i in range(per_half)]

        def normalize(slot, pixel, g):
            x = jnp.concatenate([ref[pixel + g] for ref in ins], axis=0).astype(F32)
            x = x.reshape(length // 8, 8, channels)
            u = (x * affine[0:8][None] + affine[8:16][None]).reshape(length, channels)
            normed[slot][g * length : (g + 1) * length] = (u + u * jnp.tanh(u)).astype(BF16)

        def project(slot, b):
            rows = slice(b * batch * length, (b + 1) * batch * length)
            projected[slot][rows] = jnp.dot(
                normed[slot][rows], qkv_ref[...], preferred_element_type=F32
            ).astype(BF16)

        zero = jnp.zeros((length, channels), BF16)

        def score(slot, g):
            rows = slice(g * length, (g + 1) * length)
            q = projected[slot][rows, :channels]
            k = projected[slot][rows, channels : 2 * channels]
            qm = jnp.concatenate([jnp.where(m, q, zero) for m in halves], axis=0)
            km = jnp.concatenate([jnp.where(m, k, zero) for m in heads], axis=0)
            return lax.dot_general(
                km, qm, (((1,), (1,)), ((), ())), preferred_element_type=F32
            ).reshape(per_half, length, 2 * length)

        def soften(scores):
            top = jnp.max(scores, axis=1, keepdims=True)
            e = jnp.exp2((scores - top) * factor)
            weights = (e * (1.0 / jnp.sum(e, axis=1, keepdims=True))).astype(BF16)
            return weights.reshape(per_half * length, 2 * length)

        def mix(slot, g, weights):
            rows = slice(g * length, (g + 1) * length)
            val = projected[slot][rows, 2 * channels :]
            vm = jnp.concatenate([jnp.where(m, val, zero) for m in heads], axis=0)
            mixed = lax.dot_general(
                weights, vm, (((0,), (0,)), ((), ())), preferred_element_type=F32
            )
            contexts[rows] = jnp.concatenate(
                [mixed[:length, :half], mixed[length:, half:]], axis=1
            ).astype(BF16)

        def finish(slot, pixel, b):
            rows = slice(b * batch * length, (b + 1) * batch * length)
            result = normed[slot][rows].astype(F32) + jnp.dot(
                contexts[rows], out_w_ref[...], preferred_element_type=F32
            )
            result = result.astype(BF16).reshape(batch, parts, frames, channels)
            for d in range(parts):
                outs[d][pl.ds(pixel - first + b * batch, batch)] = result[:, d]

        def work(slot, pixel, ahead):
            scores, weights = {}, {}
            for t in range(group + 2):
                if t < group:
                    scores[t] = score(slot, t)
                    normalize(1 - slot, ahead, t)
                    if (t + 1) % batch == 0:
                        project(1 - slot, t // batch)
                if 0 <= t - 1 < group:
                    weights[t - 1] = soften(scores.pop(t - 1))
                if 0 <= t - 2 < group:
                    mix(slot, t - 2, weights.pop(t - 2))
                    if (t - 1) % batch == 0:
                        finish(slot, pixel, (t - 2) // batch)

        for g in range(group):
            normalize(0, first, g)
        for b in range(group // batch):
            project(0, b)

        def body(i, carry):
            pixel = first + i * 2 * group
            work(0, pixel, pixel + group)
            ahead = jnp.minimum(pixel + 2 * group, first + pixels - group)
            work(1, pixel + group, ahead)
            return carry

        lax.fori_loop(0, pixels // (2 * group), body, 0)

    rest = (stats, gain, bias, w_qkv, w_out)
    vmem = pl.BlockSpec(memory_space=pltpu.VMEM)
    size = parts * pixels * frames * channels
    return pl.pallas_call(
        kernel,
        in_specs=[vmem] * (parts + len(rest)),
        out_specs=[vmem] * parts,
        out_shape=[jax.ShapeDtypeStruct((pixels, frames, channels), BF16)] * parts,
        scratch_shapes=[pltpu.VMEM((group * length, channels), BF16)] * 2
        + [pltpu.VMEM((group * length, 3 * channels), BF16)] * 2
        + [pltpu.VMEM((group * length, channels), BF16), pltpu.VMEM((16, channels), F32)],
        compiler_params=params(),
        cost_estimate=cost(2 * size * channels * 8, 4 * size, size * 3),
        name="attention",
    )(*blocks, *rest)


def from_pixels(me, halves, rows, cols):
    parts = len(halves[0])
    pixels, frames, channels = halves[0][0].shape
    half_rows = pixels // cols
    part_rows = half_rows * len(halves)
    flat = [block for blocks in halves for block in blocks]
    total = len(flat) * half_rows

    def kernel(me_ref, *refs):
        ins, out_ref, turned, sem = refs[: len(flat)], refs[-3], refs[-2], refs[-1]
        copies = []
        for h in range(len(halves)):
            for d in range(parts):
                base = lax.rem(me_ref[0] + d, parts) * part_rows + h * half_rows
                for r in range(half_rows):
                    slot = len(copies)
                    turned[slot] = jnp.swapaxes(ins[h * parts + d][pl.ds(r * cols, cols)], 0, 1)
                    copy = pltpu.make_async_copy(
                        turned.at[slot], out_ref.at[:, base + r], sem.at[slot]
                    )
                    copy.start()
                    copies.append(copy)
        for copy in copies:
            copy.wait()

    vmem = pl.BlockSpec(memory_space=pltpu.VMEM)
    return pl.pallas_call(
        kernel,
        in_specs=[pl.BlockSpec(memory_space=pltpu.SMEM)] + [vmem] * len(flat),
        out_specs=pl.BlockSpec(memory_space=pl.ANY),
        out_shape=jax.ShapeDtypeStruct((frames, rows, cols, channels), BF16),
        scratch_shapes=[
            pltpu.VMEM((total, frames, cols, channels), BF16),
            pltpu.SemaphoreType.DMA((total,)),
        ],
        compiler_params=params(),
        cost_estimate=cost(0, 4 * frames * rows * cols * channels),
        name="from_pixels",
    )(me, *flat)


def rotate(value, step):
    size = lax.axis_size("tm")
    return lax.ppermute(value, "tm", [(i, (i + step) % size) for i in range(size)])


def per_device(video, w_space, w_time, norm_gain, norm_bias, w_qkv, w_out):
    frames, rows, cols, channels = video.shape
    parts = lax.axis_size("tm")
    me = lax.axis_index("tm").astype(jnp.int32).reshape(1)
    first, last = edge_columns(video)
    left = shift(last, WIDTH, 1)
    right = shift(first, WIDTH, -1)
    pixels = to_pixels(video)

    def border(r):
        return jnp.concatenate([left[r][None], pixels[r], right[r][None]], axis=0)

    above = shift(border(rows - 1), "height", 1)
    below = shift(border(0), "height", -1)
    taps = w_space.reshape(9 * channels, channels)
    inner = inner_conv(pixels, left, right, taps)
    spatial, early, late = outer_conv(pixels, left, right, above, below, taps, inner)
    before = shift(late, "tm", 1)
    after = shift(early, "tm", -1)
    blocks, stats = temporal_conv(
        me, spatial.reshape(rows * cols, frames, channels), before, after, w_time
    )
    stats = stats + sum(rotate(stats, d) for d in range(1, parts))
    moved = [blocks[0]]
    for d in range(1, parts):
        moved.append(rotate(blocks[d], d))
    stats = stats + lax.ppermute(stats, "width_1", [(0, 1), (1, 0)])
    others = ("height", "width_0")
    count = lax.axis_size(others)
    shared = jnp.broadcast_to(stats[None], (count, *stats.shape))
    stats = jnp.sum(lax.all_to_all(shared, others, 0, 0), axis=0)
    cell_count = float(
        frames * parts * rows * lax.axis_size("height") * cols * lax.axis_size(WIDTH)
        * (channels // GROUPS)
    )
    weights = (norm_gain.reshape(1, -1), norm_bias.reshape(1, -1), w_qkv, w_out)
    share = rows * cols // parts // 2
    halves = []
    for h in range(2):
        results = attention(moved, stats, *weights, cell_count, h * share, share)
        halves.append([results[0]] + [rotate(results[d], -d) for d in range(1, parts)])
    return from_pixels(me, halves, rows, cols)


def solution(mesh):
    torus = Mesh(
        mesh.devices.reshape(mesh.shape["tm"], mesh.shape["height"], 8, 2),
        ("tm", "height", "width_0", "width_1"),
    )
    in_specs = (P("tm", "height", WIDTH, None), P(), P(), P(), P(), P(), P())
    out_specs = P("tm", "height", WIDTH, None)
    return jax.shard_map(
        per_device, mesh=torus, in_specs=in_specs, out_specs=out_specs, check_vma=False
    )
```

time: 164 us -> 146 us (0.89); the launches traced: 162 us -> 146 us
  waiting for transfers between devices: 64.2 us -> 41.4 us
  blocking collectives: 0 us -> 20.1 us
  starting transfers between devices: 41.2 us -> 33.4 us
  Pallas kernels: 50.9 us -> 45 us
    ppermute x8 -> x1, waiting for transfers between devices: 31.3 us -> 0.82 us  [per_device(): stats = stats + lax.ppermute(stats, 'width_1', [(0, 1), (1, 0)])]
    all_to_all x0 -> x1, blocking collectives: none -> 20.1 us  [per_device(): stats = jnp.sum(lax.all_to_all(shared, others, 0, 0), axis=0)]
    ppermute x8 -> x1, starting transfers between devices: 16.8 us -> 2.02 us  [per_device(): stats = stats + lax.ppermute(stats, 'width_1', [(0, 1), (1, 0)])]
    ppermute x6 -> x12, waiting for transfers between devices: 22.4 us -> 35.5 us  [rotate(): lax.ppermute(value, 'tm', [(i, (i + step) % size) for i in range(size)])]
    ppermute x6 -> x12, starting transfers between devices: 7.89 us -> 14.8 us  [rotate(): lax.ppermute(value, 'tm', [(i, (i + step) % size) for i in range(size)])]
    ppermute x6, waiting for transfers between devices: 10.5 us -> 5.02 us  [shift(): return lax.ppermute(value, axis, pairs)]
    pallas_call x2 -> x5, Pallas kernels: 35.9 us -> 32.8 us  [the longest x2 16 us: attention(): pl.pallas_call(kernel, in_specs=[vmem] * (parts + len(rest)), out_specs=[...]
    pallas_call x1, Pallas kernels: 7.65 us -> 5.22 us  [temporal_conv(): pl.pallas_call(kernel, in_specs=[pl.BlockSpec(memory_space=pltpu.SMEM)] +...]
  transfers between devices with their start and end apart: 20 -> 19, of which waited for: 16 -> 9; matrix products, arithmetic and copies ran while one was open for 1% -> 2% of each run, Pallas kernels for 0% -> 15%
where the time goes in v2:
time: 146 us
  Pallas kernels  45 us (31%)
  waiting for transfers between devices  41.4 us (28%)
  starting transfers between devices  33.4 us (23%)
  blocking collectives  20.1 us (14%)
  local copies, waits for them, and re-layouts  4.24 us (3%)
    ppermute x12, waiting for transfers between devices, rotate(): lax.ppermute(value, 'tm', [(i, (i + step) % size) for i in range(size)])  35.5 us
    all_to_all x1, blocking collectives, per_device(): stats = jnp.sum(lax.all_to_all(shared, others, 0, 0), axis=0)  20.1 us
    ppermute x6, starting transfers between devices, shift(): return lax.ppermute(value, axis, pairs)  16.5 us
    pallas_call x2, Pallas kernels, attention(): pl.pallas_call(kernel, in_specs=[vmem] * (parts + len(rest)), out_specs=[...  16 us
    ppermute x12, starting transfers between devices, rotate(): lax.ppermute(value, 'tm', [(i, (i + step) % size) for i in range(size)])  14.8 us
    pallas_call x1, Pallas kernels, inner_conv(): pl.pallas_call(kernel, out_shape=[jax.ShapeDtypeStruct((rows, cols, frame...  9.21 us
    pallas_call x1, Pallas kernels, temporal_conv(): pl.pallas_call(kernel, in_specs=[pl.BlockSpec(memory_space=pltpu.SMEM)] +...  5.22 us
    ppermute x6, waiting for transfers between devices, shift(): return lax.ppermute(value, axis, pairs)  5.02 us
  transfers between devices with their start and end apart: 19, of which 9 were waited for; matrix products, arithmetic and copies ran while one was open for 2% of the time, Pallas kernels for 15%

profile of v2, /device:TPU:1, one launch (start us, length us, event | category | flops | bytes accessed | tf_op | source)
XLA Modules:
  0.0 145.8 jit_solution(15214168806977334726)
XLA Ops:
  0.0 3.5 %edge_columns.1 = (bf16[16,16,256]{2,1,0:T(8,128)(2,1)}, bf16[16,16,256]{2,1,0:T(8,128)(2,1)}) custom-call(bf16[16,16,16,256]{3,2,1,0:T(8,128)(2,1)} %v_ref.3), custom_call_target="tpu_custom_call" | custom-call | bytes 2097152 | tf_op jit(solution)/shard_map/edge_columns/pallas_call | solution.py:46
  3.5 4.9 %collective-permute-start = (bf16[16,16,256]{2,1,0:T(8,128)(2,1)}, bf16[16,16,256]{2,1,0:T(8,128)(2,1)S(1)}, u32[]{:S(2)}, u32[]{:S(2)}) collective-permute-start(bf16[16,16,256]{2,1,0:T(8,128)(2,1)} %get-tuple-element.26), channel_id=1, source_target_pairs={{0,1},{1,2},{2,3},{3,4},{4,5},{5,6},{6,7},{7,8},{8,9},{9,10},{10,1... | collective-permute-start | bytes 393224 | tf_op jit(solution)/shard_map/ppermute | solution.py:33
  8.4 1.9 %collective-permute-start.1 = (bf16[16,16,256]{2,1,0:T(8,128)(2,1)}, bf16[16,16,256]{2,1,0:T(8,128)(2,1)S(1)}, u32[]{:S(2)}, u32[]{:S(2)}) collective-permute-start(bf16[16,16,256]{2,1,0:T(8,128)(2,1)} %get-tuple-element.27), channel_id=1, source_target_pairs={{1,0},{2,1},{3,2},{4,3},{5,4},{6,5},{7,6},{8,7},{9,8},{10,9},{11,1... | collective-permute-start | bytes 393224 | tf_op jit(solution)/shard_map/ppermute | solution.py:33
  10.3 4.0 %to_pixels.1.p_ref = bf16[16,16,16,256]{3,2,1,0:T(8,128)(2,1)} custom-call(bf16[16,16,16,256]{3,2,1,0:T(8,128)(2,1)} %v_ref.3), custom_call_target="tpu_custom_call" | custom-call | bytes 4194304 | tf_op jit(solution)/shard_map/to_pixels/pallas_call | solution.py:66
  14.3 1.0 slice_bitcast_fusion
  15.3 0.0 collective-permute-done.l_ref
  15.3 0.0 copy-start.6
  15.3 0.0 collective-permute-done.1.r_ref
  15.3 0.0 copy-start.7
  15.4 1.3 collective-permute-start.3
  16.7 4.0 %collective-permute-start.2 = (bf16[18,16,256]{2,1,0:T(8,128)(2,1)S(1)}, bf16[18,16,256]{2,1,0:T(8,128)(2,1)S(1)}, u32[]{:S(2)}, u32[]{:S(2)}) collective-permute-start(bf16[18,16,256]{2,1,0:T(8,128)(2,1)S(1)} %pad_maximum_fusion), channel_id=1, source_target_pairs={{0,16},{16,32},{32,48},{1,17},{17,33},{33,49},{2,18},{18,34},{34,5... | collective-permute-start | bytes 442376 | tf_op jit(solution)/shard_map/ppermute | solution.py:33
  20.7 0.0 copy-done.6
  20.7 0.0 copy-done.7
  20.8 9.2 %inner_conv.1 = (bf16[16,16,16,256]{3,2,1,0:T(8,128)(2,1)}, bf16[256,256]{1,0:T(8,128)(2,1)}, bf16[256,256]{1,0:T(8,128)(2,1)}) custom-call(bf16[16,16,16,256]{3,2,1,0:T(8,128)(2,1)} %to_pixels.1.p_ref, bf16[16,16,256]{2,1,0:T(8,128)(2,1)} %copy-done.6, bf16[16,16,256]{2,1,0:T(8,128)(2,1)} %copy-done.7, bf16[2304,256]{1,0:T(8,128)(2,1)} %bitcast.11), custom_call_target="tpu_custom_call" | custom-call | flops 4227858432 | bytes 3670016 | tf_op jit(solution)/shard_map/inner_conv/pallas_call | solution.py:125
  30.0 0.0 collective-permute-done.3.b_ref
  30.0 0.0 collective-permute-done.2.a_ref
  30.0 0.6 copy-done.8
  30.6 0.1 copy-done.9
  30.7 4.1 %outer_conv.1 = (bf16[16,16,16,256]{3,2,1,0:T(8,128)(2,1)}, bf16[256,256]{1,0:T(8,128)(2,1)}, bf16[256,256]{1,0:T(8,128)(2,1)}) custom-call(bf16[16,16,16,256]{3,2,1,0:T(8,128)(2,1)} %to_pixels.1.p_ref, bf16[16,16,256]{2,1,0:T(8,128)(2,1)} %copy-done.6, bf16[16,16,256]{2,1,0:T(8,128)(2,1)} %copy-done.7, ...), custom_call_target="tpu_custom_call", output_to_operand_aliasing={{0}: (6, {}), {1}: (7, {}), {2}: (8, {})} | custom-call | flops 603979776 | bytes 524288 | tf_op jit(solution)/shard_map/outer_conv/pallas_call | solution.py:179
  34.8 3.1 %collective-permute-start.4 = (bf16[256,256]{1,0:T(8,128)(2,1)}, bf16[256,256]{1,0:T(8,128)(2,1)S(1)}, u32[]{:S(2)}, u32[]{:S(2)}) collective-permute-start(bf16[256,256]{1,0:T(8,128)(2,1)} %get-tuple-element.32), channel_id=1, source_target_pairs={{0,64},{64,128},{128,192},{1,65},{65,129},{129,193},{2,66},{66,130... | collective-permute-start | bytes 393224 | tf_op jit(solution)/shard_map/ppermute | solution.py:33
  38.0 1.3 collective-permute-start.5
  39.3 1.0 collective-permute-done.4.b_ref
  40.3 4.0 %collective-permute-done.5.a_ref = bf16[256,256]{1,0:T(8,128)(2,1)S(1)} collective-permute-done((bf16[256,256]{1,0:T(8,128)(2,1)}, bf16[256,256]{1,0:T(8,128)(2,1)S(1)}, u32[]{:S(2)}, u32[]{:S(2)}) %collective-permute-start.5) | collective-permute-done | bytes 131104 | tf_op jit(solution)/shard_map/ppermute | solution.py:33
  44.3 0.7 copy-done.14
  45.0 5.2 %temporal_conv.1 = (bf16[64,16,256]{2,1,0:T(8,128)(2,1)}, bf16[64,16,256]{2,1,0:T(8,128)(2,1)}, bf16[64,16,256]{2,1,0:T(8,128)(2,1)}, bf16[64,16,256]{2,1,0:T(8,128)(2,1)}, f32[8,128]{1,0:T(8,128)}) custom-call(s32[1]{0:T(128)} %bitcast.me_ref, bf16[256,16,256]{2,1,0:T(8,128)(2,1)} %bitcast.10, bf16[256,256]{1,0:T(8,128)(2,1)} %copy-done.13, ...), custom_call_target="tpu_custom_call" | custom-call | flops 1610612736 | bytes 4194304 | tf_op jit(solution)/shard_map/temporal_conv/pallas_call | solution.py:279
  50.2 1.2 collective-permute-start.6
  51.4 1.2 collective-permute-start.7
  52.6 2.1 %collective-permute-start.8 = (bf16[64,16,256]{2,1,0:T(8,128)(2,1)}, bf16[64,16,256]{2,1,0:T(8,128)(2,1)S(1)}, u32[]{:S(2)}, u32[]{:S(2)}) collective-permute-start(bf16[64,16,256]{2,1,0:T(8,128)(2,1)} %get-tuple-element.37), channel_id=1, source_target_pairs={{0,192},{64,0},{128,64},{192,128},{1,193},{65,1},{129,65},{193,129... | collective-permute-start | bytes 1572872 | tf_op jit(solution)/shard_map/ppermute | solution.py:466
  54.7 0.5 collective-permute-start.10
  55.2 1.3 collective-permute-start.11
  56.5 19.9 %collective-permute-done.10 = f32[8,128]{1,0:T(8,128)S(1)} collective-permute-done((f32[8,128]{1,0:T(8,128)}, f32[8,128]{1,0:T(8,128)S(1)}, u32[]{:S(2)}, u32[]{:S(2)}) %collective-permute-start.10) | collective-permute-done | bytes 4128 | tf_op jit(solution)/shard_map/ppermute | solution.py:466
  76.4 2.2 %collective-permute-start.9 = (f32[8,128]{1,0:T(8,128)}, f32[8,128]{1,0:T(8,128)S(1)}, u32[]{:S(2)}, u32[]{:S(2)}) collective-permute-start(f32[8,128]{1,0:T(8,128)} %get-tuple-element.38), channel_id=1, source_target_pairs={{0,64},{64,128},{128,192},{192,0},{1,65},{65,129},{129,193},{193,1... | collective-permute-start | bytes 12296 | tf_op jit(solution)/shard_map/ppermute | solution.py:466
  78.6 0.0 collective-permute-done.11
  78.6 1.8 %collective-permute-done.9 = f32[8,128]{1,0:T(8,128)S(1)} collective-permute-done((f32[8,128]{1,0:T(8,128)}, f32[8,128]{1,0:T(8,128)S(1)}, u32[]{:S(2)}, u32[]{:S(2)}) %collective-permute-start.9) | collective-permute-done | bytes 4128 | tf_op jit(solution)/shard_map/ppermute | solution.py:466
  80.4 0.7 add_add_fusion
  81.0 2.0 %collective-permute-start.12 = (f32[8,128]{1,0:T(8,128)S(1)}, f32[8,128]{1,0:T(8,128)S(1)}, u32[]{:S(2)}, u32[]{:S(2)}) collective-permute-start(f32[8,128]{1,0:T(8,128)S(1)} %add_add_fusion), channel_id=1, source_target_pairs={{0,1},{1,0},{2,3},{3,2},{4,5},{5,4},{6,7},{7,6},{8,9},{9,8},{10,11... | collective-permute-start | bytes 12296 | tf_op jit(solution)/shard_map/ppermute | solution.py:495
  83.1 0.8 collective-permute-done.12
  83.9 20.1 %all_to_all.5 = f32[32,8,128]{2,1,0:T(8,128)S(1)} all-to-all(f32[32,8,128]{2,1,0:T(8,128)S(1)} %broadcast_in_dim.2), channel_id=1, replica_groups=mesh['tm'=4,'height'=4,'width_0'=8,'width_1'=2] {'height','width_0'}, dimensions={0} | all-to-all | bytes 262144 | tf_op jit(solution)/shard_map/all_to_all | solution.py:499
  104.0 0.6 reduce_sum.9.refs_4_
  104.6 0.0 collective-permute-done.6.refs_1_
  104.7 0.0 collective-permute-done.7.refs_2_
  104.7 0.0 collective-permute-done.8.refs_3_
  104.7 0.0 copy-start.12
  104.7 0.8 copy-done.10
  105.5 0.2 copy-done.11
  105.6 0.2 copy-done.12
  105.8 8.0 %attention.3 = (bf16[32,16,256]{2,1,0:T(8,128)(2,1)}, bf16[32,16,256]{2,1,0:T(8,128)(2,1)}, bf16[32,16,256]{2,1,0:T(8,128)(2,1)}, bf16[32,16,256]{2,1,0:T(8,128)(2,1)}) custom-call(bf16[64,16,256]{2,1,0:T(8,128)(2,1)} %get-tuple-element.34.refs_0_, bf16[64,16,256]{2,1,0:T(8,128)(2,1)} %copy-done.10, bf16[64,16,256]{2,1,0:T(8,128)(2,1)} %copy-done.11, ...), custom_call_target="tpu_custom_call" | custom-call | flops 2147483648 | bytes 2097152 | tf_op jit(solution)/shard_map/attention/pallas_call | solution.py:409
  113.8 1.7 %collective-permute-start.16 = (bf16[32,16,256]{2,1,0:T(8,128)(2,1)}, bf16[32,16,256]{2,1,0:T(8,128)(2,1)S(1)}, u32[]{:S(2)}, u32[]{:S(2)}) collective-permute-start(bf16[32,16,256]{2,1,0:T(8,128)(2,1)} %get-tuple-element.44), channel_id=1, source_target_pairs={{0,192},{64,0},{128,64},{192,128},{1,193},{65,1},{129,65},{193,129... | collective-permute-start | bytes 786440 | tf_op jit(solution)/shard_map/ppermute | solution.py:466
  115.6 1.3 collective-permute-start.17
  116.8 0.0 collective-permute-start.18
  116.8 8.0 %attention.2 = (bf16[32,16,256]{2,1,0:T(8,128)(2,1)}, bf16[32,16,256]{2,1,0:T(8,128)(2,1)}, bf16[32,16,256]{2,1,0:T(8,128)(2,1)}, bf16[32,16,256]{2,1,0:T(8,128)(2,1)}) custom-call(bf16[64,16,256]{2,1,0:T(8,128)(2,1)} %get-tuple-element.34.refs_0_, bf16[64,16,256]{2,1,0:T(8,128)(2,1)} %copy-done.10, bf16[64,16,256]{2,1,0:T(8,128)(2,1)} %copy-done.11, ...), custom_call_target="tpu_custom_call" | custom-call | flops 2147483648 | bytes 2097152 | tf_op jit(solution)/shard_map/attention/pallas_call | solution.py:409
  124.8 2.7 %collective-permute-start.13 = (bf16[32,16,256]{2,1,0:T(8,128)(2,1)}, bf16[32,16,256]{2,1,0:T(8,128)(2,1)S(1)}, u32[]{:S(2)}, u32[]{:S(2)}) collective-permute-start(bf16[32,16,256]{2,1,0:T(8,128)(2,1)} %get-tuple-element.40), channel_id=1, source_target_pairs={{0,192},{64,0},{128,64},{192,128},{1,193},{65,1},{129,65},{193,129... | collective-permute-start | bytes 786440 | tf_op jit(solution)/shard_map/ppermute | solution.py:466
  127.5 0.5 collective-permute-start.14
  128.0 0.0 collective-permute-done.16.refs_5_
  128.0 0.1 collective-permute-start.15
  128.1 0.0 collective-permute-done.17.refs_6_
  128.1 2.5 %collective-permute-done.18.refs_7_ = bf16[32,16,256]{2,1,0:T(8,128)(2,1)S(1)} collective-permute-done((bf16[32,16,256]{2,1,0:T(8,128)(2,1)}, bf16[32,16,256]{2,1,0:T(8,128)(2,1)S(1)}, u32[]{:S(2)}, u32[]{:S(2)}) %collective-permute-start.18) | collective-permute-done | bytes 262176 | tf_op jit(solution)/shard_map/ppermute | solution.py:466
  130.6 1.8 %collective-permute-done.13.refs_1_ = bf16[32,16,256]{2,1,0:T(8,128)(2,1)S(1)} collective-permute-done((bf16[32,16,256]{2,1,0:T(8,128)(2,1)}, bf16[32,16,256]{2,1,0:T(8,128)(2,1)S(1)}, u32[]{:S(2)}, u32[]{:S(2)}) %collective-permute-start.13) | collective-permute-done | bytes 262176 | tf_op jit(solution)/shard_map/ppermute | solution.py:466
  132.4 2.1 %collective-permute-done.14.refs_2_ = bf16[32,16,256]{2,1,0:T(8,128)(2,1)S(1)} collective-permute-done((bf16[32,16,256]{2,1,0:T(8,128)(2,1)}, bf16[32,16,256]{2,1,0:T(8,128)(2,1)S(1)}, u32[]{:S(2)}, u32[]{:S(2)}) %collective-permute-start.14) | collective-permute-done | bytes 262176 | tf_op jit(solution)/shard_map/ppermute | solution.py:466
  134.5 7.5 %collective-permute-done.15.refs_3_ = bf16[32,16,256]{2,1,0:T(8,128)(2,1)S(1)} collective-permute-done((bf16[32,16,256]{2,1,0:T(8,128)(2,1)}, bf16[32,16,256]{2,1,0:T(8,128)(2,1)S(1)}, u32[]{:S(2)}, u32[]{:S(2)}) %collective-permute-start.15) | collective-permute-done | bytes 262176 | tf_op jit(solution)/shard_map/ppermute | solution.py:466
  142.0 0.0 copy-done
  142.0 0.0 copy-done.2
  142.0 0.7 copy-done.5
  142.7 3.0 %from_pixels.1 = bf16[16,16,16,256]{3,2,1,0:T(8,128)(2,1)} custom-call(s32[1]{0:T(128)} %bitcast.me_ref, bf16[32,16,256]{2,1,0:T(8,128)(2,1)} %get-tuple-element.39.refs_0_, bf16[32,16,256]{2,1,0:T(8,128)(2,1)} %copy-done.3, bf16[32,16,256]{2,1,0:T(8,128)(2,1)} %copy-done.4, bf16[32,16,256]{2,1,0:T(8,128)(2,1)} %copy-done.5, ...), custom_call_target="tpu_custom_call" | custom-call | bytes 4194304 | tf_op jit(solution)/shard_map/from_pixels/pallas_call | solution.py:449
  (22 shorter events, 0.1 us)
Async XLA Ops:
  3.5 11.8 %collective-permute-start = (bf16[16,16,256]{2,1,0:T(8,128)(2,1)}, bf16[16,16,256]{2,1,0:T(8,128)(2,1)S(1)}, u32[]{:S(2)}, u32[]{:S(2)}) collective-permute-start(bf16[16,16,256]{2,1,0:T(8,128)(2,1)} %get-tuple-element.26), channel_id=1, source_target_pairs={{0,1},{1,2},{2,3},{3,4},{4,5},{5,6},{6,7},{7,8},{8,9},{9,10},{10,1... | collective-permute-start | bytes 393224 | tf_op jit(solution)/shard_map/ppermute | solution.py:33
  8.4 6.9 %collective-permute-start.1 = (bf16[16,16,256]{2,1,0:T(8,128)(2,1)}, bf16[16,16,256]{2,1,0:T(8,128)(2,1)S(1)}, u32[]{:S(2)}, u32[]{:S(2)}) collective-permute-start(bf16[16,16,256]{2,1,0:T(8,128)(2,1)} %get-tuple-element.27), channel_id=1, source_target_pairs={{1,0},{2,1},{3,2},{4,3},{5,4},{6,5},{7,6},{8,7},{9,8},{10,9},{11,1... | collective-permute-start | bytes 393224 | tf_op jit(solution)/shard_map/ppermute | solution.py:33
  15.3 5.4 %copy-start.6 = (bf16[16,16,256]{2,1,0:T(8,128)(2,1)}, bf16[16,16,256]{2,1,0:T(8,128)(2,1)S(1)}, u32[]{:S(2)}) copy-start(bf16[16,16,256]{2,1,0:T(8,128)(2,1)S(1)} %collective-permute-done.l_ref) | copy-start | bytes 393220
  15.3 5.4 %copy-start.7 = (bf16[16,16,256]{2,1,0:T(8,128)(2,1)}, bf16[16,16,256]{2,1,0:T(8,128)(2,1)S(1)}, u32[]{:S(2)}) copy-start(bf16[16,16,256]{2,1,0:T(8,128)(2,1)S(1)} %collective-permute-done.1.r_ref) | copy-start | bytes 393220
  15.4 14.6 %collective-permute-start.3 = (bf16[18,16,256]{2,1,0:T(8,128)(2,1)S(1)}, bf16[18,16,256]{2,1,0:T(8,128)(2,1)S(1)}, u32[]{:S(2)}, u32[]{:S(2)}) collective-permute-start(bf16[18,16,256]{2,1,0:T(8,128)(2,1)S(1)} %pad_maximum_fusion.1), channel_id=1, source_target_pairs={{16,0},{32,16},{48,32},{17,1},{33,17},{49,33},{18,2},{34,18},{50,3... | collective-permute-start | bytes 442376 | tf_op jit(solution)/shard_map/ppermute | solution.py:33
  16.7 13.2 %collective-permute-start.2 = (bf16[18,16,256]{2,1,0:T(8,128)(2,1)S(1)}, bf16[18,16,256]{2,1,0:T(8,128)(2,1)S(1)}, u32[]{:S(2)}, u32[]{:S(2)}) collective-permute-start(bf16[18,16,256]{2,1,0:T(8,128)(2,1)S(1)} %pad_maximum_fusion), channel_id=1, source_target_pairs={{0,16},{16,32},{32,48},{1,17},{17,33},{33,49},{2,18},{18,34},{34,5... | collective-permute-start | bytes 442376 | tf_op jit(solution)/shard_map/ppermute | solution.py:33
  30.0 0.7 copy-start.8
  30.0 0.7 copy-start.9
  34.8 5.4 %collective-permute-start.4 = (bf16[256,256]{1,0:T(8,128)(2,1)}, bf16[256,256]{1,0:T(8,128)(2,1)S(1)}, u32[]{:S(2)}, u32[]{:S(2)}) collective-permute-start(bf16[256,256]{1,0:T(8,128)(2,1)} %get-tuple-element.32), channel_id=1, source_target_pairs={{0,64},{64,128},{128,192},{1,65},{65,129},{129,193},{2,66},{66,130... | collective-permute-start | bytes 393224 | tf_op jit(solution)/shard_map/ppermute | solution.py:33
  38.0 6.3 %collective-permute-start.5 = (bf16[256,256]{1,0:T(8,128)(2,1)}, bf16[256,256]{1,0:T(8,128)(2,1)S(1)}, u32[]{:S(2)}, u32[]{:S(2)}) collective-permute-start(bf16[256,256]{1,0:T(8,128)(2,1)} %get-tuple-element.33), channel_id=1, source_target_pairs={{64,0},{128,64},{192,128},{65,1},{129,65},{193,129},{66,2},{130,66... | collective-permute-start | bytes 393224 | tf_op jit(solution)/shard_map/ppermute | solution.py:33
  40.3 4.0 %copy-start.13 = (bf16[256,256]{1,0:T(8,128)(2,1)}, bf16[256,256]{1,0:T(8,128)(2,1)S(1)}, u32[]{:S(2)}) copy-start(bf16[256,256]{1,0:T(8,128)(2,1)S(1)} %collective-permute-done.4.b_ref) | copy-start | bytes 393220
  44.3 0.7 copy-start.14
  50.2 54.5 %collective-permute-start.6 = (bf16[64,16,256]{2,1,0:T(8,128)(2,1)}, bf16[64,16,256]{2,1,0:T(8,128)(2,1)S(1)}, u32[]{:S(2)}, u32[]{:S(2)}) collective-permute-start(bf16[64,16,256]{2,1,0:T(8,128)(2,1)} %get-tuple-element.35), channel_id=1, source_target_pairs={{0,64},{64,128},{128,192},{192,0},{1,65},{65,129},{129,193},{193,1... | collective-permute-start | bytes 1572872 | tf_op jit(solution)/shard_map/ppermute | solution.py:466
  51.4 53.3 %collective-permute-start.7 = (bf16[64,16,256]{2,1,0:T(8,128)(2,1)}, bf16[64,16,256]{2,1,0:T(8,128)(2,1)S(1)}, u32[]{:S(2)}, u32[]{:S(2)}) collective-permute-start(bf16[64,16,256]{2,1,0:T(8,128)(2,1)} %get-tuple-element.36), channel_id=1, source_target_pairs={{0,128},{64,192},{128,0},{192,64},{1,129},{65,193},{129,1},{193,65... | collective-permute-start | bytes 1572872 | tf_op jit(solution)/shard_map/ppermute | solution.py:466
  52.6 52.0 %collective-permute-start.8 = (bf16[64,16,256]{2,1,0:T(8,128)(2,1)}, bf16[64,16,256]{2,1,0:T(8,128)(2,1)S(1)}, u32[]{:S(2)}, u32[]{:S(2)}) collective-permute-start(bf16[64,16,256]{2,1,0:T(8,128)(2,1)} %get-tuple-element.37), channel_id=1, source_target_pairs={{0,192},{64,0},{128,64},{192,128},{1,193},{65,1},{129,65},{193,129... | collective-permute-start | bytes 1572872 | tf_op jit(solution)/shard_map/ppermute | solution.py:466
  54.7 21.7 %collective-permute-start.10 = (f32[8,128]{1,0:T(8,128)}, f32[8,128]{1,0:T(8,128)S(1)}, u32[]{:S(2)}, u32[]{:S(2)}) collective-permute-start(f32[8,128]{1,0:T(8,128)} %get-tuple-element.38), channel_id=1, source_target_pairs={{0,128},{64,192},{128,0},{192,64},{1,129},{65,193},{129,1},{193,65... | collective-permute-start | bytes 12296 | tf_op jit(solution)/shard_map/ppermute | solution.py:466
  55.2 23.4 %collective-permute-start.11 = (f32[8,128]{1,0:T(8,128)}, f32[8,128]{1,0:T(8,128)S(1)}, u32[]{:S(2)}, u32[]{:S(2)}) collective-permute-start(f32[8,128]{1,0:T(8,128)} %get-tuple-element.38), channel_id=1, source_target_pairs={{0,192},{64,0},{128,64},{192,128},{1,193},{65,1},{129,65},{193,129... | collective-permute-start | bytes 12296 | tf_op jit(solution)/shard_map/ppermute | solution.py:466
  76.4 4.0 %collective-permute-start.9 = (f32[8,128]{1,0:T(8,128)}, f32[8,128]{1,0:T(8,128)S(1)}, u32[]{:S(2)}, u32[]{:S(2)}) collective-permute-start(f32[8,128]{1,0:T(8,128)} %get-tuple-element.38), channel_id=1, source_target_pairs={{0,64},{64,128},{128,192},{192,0},{1,65},{65,129},{129,193},{193,1... | collective-permute-start | bytes 12296 | tf_op jit(solution)/shard_map/ppermute | solution.py:466
  81.0 2.8 %collective-permute-start.12 = (f32[8,128]{1,0:T(8,128)S(1)}, f32[8,128]{1,0:T(8,128)S(1)}, u32[]{:S(2)}, u32[]{:S(2)}) collective-permute-start(f32[8,128]{1,0:T(8,128)S(1)} %add_add_fusion), channel_id=1, source_target_pairs={{0,1},{1,0},{2,3},{3,2},{4,5},{5,4},{6,7},{7,6},{8,9},{9,8},{10,11... | collective-permute-start | bytes 12296 | tf_op jit(solution)/shard_map/ppermute | solution.py:495
  104.7 0.8 copy-start.10
  104.7 1.0 copy-start.11
  104.7 1.2 copy-start.12
  113.8 14.2 %collective-permute-start.16 = (bf16[32,16,256]{2,1,0:T(8,128)(2,1)}, bf16[32,16,256]{2,1,0:T(8,128)(2,1)S(1)}, u32[]{:S(2)}, u32[]{:S(2)}) collective-permute-start(bf16[32,16,256]{2,1,0:T(8,128)(2,1)} %get-tuple-element.44), channel_id=1, source_target_pairs={{0,192},{64,0},{128,64},{192,128},{1,193},{65,1},{129,65},{193,129... | collective-permute-start | bytes 786440 | tf_op jit(solution)/shard_map/ppermute | solution.py:466
  115.6 12.5 %collective-permute-start.17 = (bf16[32,16,256]{2,1,0:T(8,128)(2,1)}, bf16[32,16,256]{2,1,0:T(8,128)(2,1)S(1)}, u32[]{:S(2)}, u32[]{:S(2)}) collective-permute-start(bf16[32,16,256]{2,1,0:T(8,128)(2,1)} %get-tuple-element.45), channel_id=1, source_target_pairs={{0,128},{64,192},{128,0},{192,64},{1,129},{65,193},{129,1},{193,65... | collective-permute-start | bytes 786440 | tf_op jit(solution)/shard_map/ppermute | solution.py:466
  116.8 13.7 %collective-permute-start.18 = (bf16[32,16,256]{2,1,0:T(8,128)(2,1)}, bf16[32,16,256]{2,1,0:T(8,128)(2,1)S(1)}, u32[]{:S(2)}, u32[]{:S(2)}) collective-permute-start(bf16[32,16,256]{2,1,0:T(8,128)(2,1)} %get-tuple-element.46), channel_id=1, source_target_pairs={{0,64},{64,128},{128,192},{192,0},{1,65},{65,129},{129,193},{193,1... | collective-permute-start | bytes 786440 | tf_op jit(solution)/shard_map/ppermute | solution.py:466
  124.8 7.6 %collective-permute-start.13 = (bf16[32,16,256]{2,1,0:T(8,128)(2,1)}, bf16[32,16,256]{2,1,0:T(8,128)(2,1)S(1)}, u32[]{:S(2)}, u32[]{:S(2)}) collective-permute-start(bf16[32,16,256]{2,1,0:T(8,128)(2,1)} %get-tuple-element.40), channel_id=1, source_target_pairs={{0,192},{64,0},{128,64},{192,128},{1,193},{65,1},{129,65},{193,129... | collective-permute-start | bytes 786440 | tf_op jit(solution)/shard_map/ppermute | solution.py:466
  127.5 7.0 %collective-permute-start.14 = (bf16[32,16,256]{2,1,0:T(8,128)(2,1)}, bf16[32,16,256]{2,1,0:T(8,128)(2,1)S(1)}, u32[]{:S(2)}, u32[]{:S(2)}) collective-permute-start(bf16[32,16,256]{2,1,0:T(8,128)(2,1)} %get-tuple-element.41), channel_id=1, source_target_pairs={{0,128},{64,192},{128,0},{192,64},{1,129},{65,193},{129,1},{193,65... | collective-permute-start | bytes 786440 | tf_op jit(solution)/shard_map/ppermute | solution.py:466
  128.0 14.0 %copy-start = (bf16[32,16,256]{2,1,0:T(8,128)(2,1)}, bf16[32,16,256]{2,1,0:T(8,128)(2,1)S(1)}, u32[]{:S(2)}) copy-start(bf16[32,16,256]{2,1,0:T(8,128)(2,1)S(1)} %collective-permute-done.16.refs_5_) | copy-start | bytes 786436
  128.0 14.0 %collective-permute-start.15 = (bf16[32,16,256]{2,1,0:T(8,128)(2,1)}, bf16[32,16,256]{2,1,0:T(8,128)(2,1)S(1)}, u32[]{:S(2)}, u32[]{:S(2)}) collective-permute-start(bf16[32,16,256]{2,1,0:T(8,128)(2,1)} %get-tuple-element.42), channel_id=1, source_target_pairs={{0,64},{64,128},{128,192},{192,0},{1,65},{65,129},{129,193},{193,1... | collective-permute-start | bytes 786440 | tf_op jit(solution)/shard_map/ppermute | solution.py:466
  128.1 13.9 %copy-start.1 = (bf16[32,16,256]{2,1,0:T(8,128)(2,1)}, bf16[32,16,256]{2,1,0:T(8,128)(2,1)S(1)}, u32[]{:S(2)}) copy-start(bf16[32,16,256]{2,1,0:T(8,128)(2,1)S(1)} %collective-permute-done.17.refs_6_) | copy-start | bytes 786436
  130.6 11.4 %copy-start.2 = (bf16[32,16,256]{2,1,0:T(8,128)(2,1)}, bf16[32,16,256]{2,1,0:T(8,128)(2,1)S(1)}, u32[]{:S(2)}) copy-start(bf16[32,16,256]{2,1,0:T(8,128)(2,1)S(1)} %collective-permute-done.18.refs_7_) | copy-start | bytes 786436
  132.4 9.6 %copy-start.3 = (bf16[32,16,256]{2,1,0:T(8,128)(2,1)}, bf16[32,16,256]{2,1,0:T(8,128)(2,1)S(1)}, u32[]{:S(2)}) copy-start(bf16[32,16,256]{2,1,0:T(8,128)(2,1)S(1)} %collective-permute-done.13.refs_1_) | copy-start | bytes 786436
  134.5 7.5 %copy-start.4 = (bf16[32,16,256]{2,1,0:T(8,128)(2,1)}, bf16[32,16,256]{2,1,0:T(8,128)(2,1)S(1)}, u32[]{:S(2)}) copy-start(bf16[32,16,256]{2,1,0:T(8,128)(2,1)S(1)} %collective-permute-done.14.refs_2_) | copy-start | bytes 786436
  142.0 0.7 copy-start.5

commit v3 on v2

--- a/solution.py
+++ b/solution.py
@@ -33,28 +33,6 @@
     return lax.ppermute(value, axis, pairs)
 
 
-def edge_columns(video):
-    frames, rows, cols, channels = video.shape
-    step = 4
-
-    def kernel(v_ref, first_ref, last_ref):
-        for r in range(step):
-            turned = jnp.swapaxes(v_ref[:, r], 0, 1)
-            first_ref[r] = turned[0]
-            last_ref[r] = turned[cols - 1]
-
-    return pl.pallas_call(
-        kernel,
-        grid=(rows // step,),
-        in_specs=[pl.BlockSpec((frames, step, cols, channels), lambda i: (0, i, 0, 0))],
-        out_specs=[pl.BlockSpec((step, frames, channels), lambda i: (i, 0, 0))] * 2,
-        out_shape=[jax.ShapeDtypeStruct((rows, frames, channels), BF16)] * 2,
-        compiler_params=params(),
-        cost_estimate=cost(0, video.size * 2),
-        name="edge_columns",
-    )(video)
-
-
 def to_pixels(video):
     frames, rows, cols, channels = video.shape
     step = 4
@@ -75,124 +53,115 @@
     )(video)
 
 
-def convolve(pad, base, span, cols, w_ref):
-    pieces = []
-    for row_step in range(3):
-        for col_step in range(3):
-            piece = pad[pl.ds(base + row_step, span), pl.ds(col_step, cols)]
-            pieces.append(piece.reshape(span * cols * piece.shape[2], piece.shape[3]))
-    window = jnp.concatenate(pieces, axis=1)
-    return jnp.dot(window, w_ref[...], preferred_element_type=F32)
-
-
-def end_frames(acc, total, frames, count):
-    slabs = total.shape[1] // 128
-    for j in range(slabs):
-        acc[j] = total[:, 128 * j : 128 * (j + 1)]
-    return [
-        jnp.concatenate(
-            [acc[j, pl.ds(frame, count, stride=frames)] for j in range(slabs)], axis=1
-        ).astype(BF16)
-        for frame in (0, frames - 1)
-    ]
-
-
-def inner_conv(pixels, left, right, w_space):
+def spatial_conv(pixels, left, right, above, below, w_space):
     rows, cols, frames, channels = pixels.shape
     span = 2
-    chunk = span * cols
-    count = chunk * frames
-
-    def kernel(p_ref, l_ref, r_ref, w_ref, out_ref, first_ref, last_ref, pad, acc):
+    count = span * cols * frames
+    unroll = 2
+
+    def kernel(p_ref, l_ref, r_ref, a_ref, b_ref, w_ref, out_ref, pad):
+        pad[0] = a_ref[...]
+        pad[rows + 1] = b_ref[...]
         for r in range(rows):
-            pad[r, 0] = l_ref[r]
-            pad[r, pl.ds(1, cols)] = p_ref[r]
-            pad[r, cols + 1] = r_ref[r]
+            pad[r + 1, 0] = l_ref[r]
+            pad[r + 1, pl.ds(1, cols)] = p_ref[r]
+            pad[r + 1, cols + 1] = r_ref[r]
 
         def body(i, carry):
-            base = i * span
-            total = convolve(pad, base, span, cols, w_ref)
-            out_ref[pl.ds(base + 1, span)] = total.astype(BF16).reshape(span, cols, frames, channels)
-            ends = end_frames(acc, total, frames, chunk)
-            for ref, value in zip((first_ref, last_ref), ends):
-                ref[pl.ds(pl.multiple_of(base * cols + cols, cols), chunk)] = value
+            for u in range(unroll):
+                base = (i * unroll + u) * span
+                pieces = []
+                for row_step in range(3):
+                    for col_step in range(3):
+                        piece = pad[pl.ds(base + row_step, span), pl.ds(col_step, cols)]
+                        pieces.append(piece.reshape(count, channels))
+                window = jnp.concatenate(pieces, axis=1)
+                total = jnp.dot(window, w_ref[...], preferred_element_type=F32)
+                out_ref[pl.ds(base, span)] = total.astype(BF16).reshape(
+                    span, cols, frames, channels
+                )
             return carry
 
-        lax.fori_loop(0, (rows - 2) // span, body, 0)
-
-    edge = jax.ShapeDtypeStruct((rows * cols, channels), BF16)
-    size = (rows - 2) * cols * frames * channels
+        lax.fori_loop(0, rows // span // unroll, body, 0)
+
+    size = rows * cols * frames * channels
     return pl.pallas_call(
         kernel,
-        out_shape=[jax.ShapeDtypeStruct((rows, cols, frames, channels), BF16), edge, edge],
-        scratch_shapes=[
-            pltpu.VMEM((rows, cols + 2, frames, channels), BF16),
-            pltpu.VMEM((channels // 128, count, 128), F32),
-        ],
+        out_shape=jax.ShapeDtypeStruct((rows, cols, frames, channels), BF16),
+        scratch_shapes=[pltpu.VMEM((rows + 2, cols + 2, frames, channels), BF16)],
         compiler_params=params(),
         cost_estimate=cost(2 * size * channels * 9, 4 * size),
-        name="inner_conv",
-    )(pixels, left, right, w_space)
-
-
-def outer_conv(pixels, left, right, above, below, w_space, results):
-    rows, cols, frames, channels = pixels.shape
-    count = cols * frames
-
-    def kernel(p_ref, l_ref, r_ref, a_ref, b_ref, w_ref, *refs):
-        outs, (pad, acc, wide, ends, sem) = refs[3:6], refs[6:]
+        name="spatial_conv",
+    )(pixels, left, right, above, below, w_space)
+
+
+def end_frames(video, left, right, above, below, w_space):
+    frames, rows, cols, channels = video.shape
+    lanes = 128
+    slabs = channels // lanes
+    pitch = cols + 8
+    taps = 9
+    ends = (0, frames - 1)
+
+    def kernel(v_ref, l_ref, r_ref, a_ref, b_ref, w_ref, early_ref, late_ref, held, side, wide, window, sem):
         fetch = [
-            pltpu.make_async_copy(
-                p_ref.at[pl.ds(start, 2)], pad.at[pl.ds(to, 2), pl.ds(1, cols)], sem.at[i]
-            )
-            for i, (start, to) in enumerate(((0, 1), (rows - 2, 3)))
+            pltpu.make_async_copy(v_ref.at[frame], held.at[k], sem.at[k])
+            for k, frame in enumerate(ends)
         ]
         for copy in fetch:
             copy.start()
-        pad[0] = a_ref[...]
-        pad[5] = b_ref[...]
-        for r, to in ((0, 1), (1, 2), (rows - 2, 3), (rows - 1, 4)):
-            pad[to, 0] = l_ref[r]
-            pad[to, cols + 1] = r_ref[r]
+        for j in range(slabs):
+            cut = slice(j * lanes, (j + 1) * lanes)
+            for n, ref in enumerate((l_ref, r_ref, a_ref, b_ref)):
+                size = ref.shape[0] * frames
+                side[n, j, pl.ds(0, size)] = ref[...].reshape(size, channels)[:, cut].astype(F32)
         for copy in fetch:
             copy.wait()
-        copies = []
-        for k, row in enumerate((0, rows - 1)):
-            total = convolve(pad, 3 * k, 1, cols, w_ref)
-            wide[k] = total.astype(BF16).reshape(cols, frames, channels)
-            for e, value in enumerate(end_frames(acc.at[k], total, frames, cols)):
-                ends[k, e] = value
-            copies.append((wide.at[k], outs[0].at[row]))
-            for e in range(2):
-                copies.append((ends.at[k, e], outs[1 + e].at[pl.ds(row * cols, cols)]))
-        started = []
-        for i, (source, target) in enumerate(copies):
-            copy = pltpu.make_async_copy(source, target, sem.at[2 + i])
-            copy.start()
-            started.append(copy)
-        for copy in started:
-            copy.wait()
+        outs = (early_ref, late_ref)
+        for k, frame in enumerate(ends):
+            for j in range(slabs):
+                cut = slice(j * lanes, (j + 1) * lanes)
+                for n, at in ((0, 7), (1, pitch)):
+                    wide[k, j, pl.ds(pitch + at, rows, stride=pitch)] = side[
+                        n, j, pl.ds(frame, rows, stride=frames)
+                    ]
+                for n, row in ((2, 0), (3, rows + 1)):
+                    wide[k, j, pl.ds(row * pitch + 7, cols + 2)] = side[
+                        n, j, pl.ds(frame, cols + 2, stride=frames)
+                    ]
+                for r in range(rows):
+                    wide[k, j, pl.ds((r + 1) * pitch + 8, cols)] = held[k, r, :, cut].astype(F32)
+            for tap in range(taps):
+                row_step, col_step = tap // 3, tap % 3
+                for r in range(rows):
+                    for j in range(slabs):
+                        at = tap * channels + j * lanes
+                        window[k, r * cols : (r + 1) * cols, at : at + lanes] = wide[
+                            k, j, pl.ds((r + row_step) * pitch + 7 + col_step, cols)
+                        ].astype(BF16)
+            outs[k][...] = jnp.dot(
+                window[k], w_ref[...], preferred_element_type=F32
+            ).astype(BF16)
 
     anywhere = pl.BlockSpec(memory_space=pl.ANY)
     vmem = pl.BlockSpec(memory_space=pltpu.VMEM)
-    size = 2 * cols * frames * channels
+    size = 2 * rows * cols * channels
     return pl.pallas_call(
         kernel,
-        in_specs=[anywhere] + [vmem] * 5 + [anywhere] * 3,
-        out_specs=[anywhere] * 3,
-        out_shape=[jax.ShapeDtypeStruct(a.shape, a.dtype) for a in results],
-        input_output_aliases={6: 0, 7: 1, 8: 2},
+        in_specs=[anywhere] + [vmem] * 5,
+        out_specs=[vmem] * 2,
+        out_shape=[jax.ShapeDtypeStruct((rows * cols, channels), BF16)] * 2,
         scratch_shapes=[
-            pltpu.VMEM((6, cols + 2, frames, channels), BF16),
-            pltpu.VMEM((2, channels // 128, count, 128), F32),
-            pltpu.VMEM((2, cols, frames, channels), BF16),
-            pltpu.VMEM((2, 2, cols, channels), BF16),
-            pltpu.SemaphoreType.DMA((8,)),
+            pltpu.VMEM((2, rows, cols, channels), BF16),
+            pltpu.VMEM((4, slabs, (cols + 2) * frames, lanes), F32),
+            pltpu.VMEM((2, slabs, (rows + 2) * pitch + 8, lanes), F32),
+            pltpu.VMEM((2, rows * cols, taps * channels), BF16),
+            pltpu.SemaphoreType.DMA((2,)),
         ],
         compiler_params=params(),
-        cost_estimate=cost(2 * size * channels * 9, 4 * size),
-        name="outer_conv",
-    )(pixels, left, right, above, below, w_space, *results)
+        cost_estimate=cost(2 * size * channels * taps, 4 * size),
+        name="end_frames",
+    )(video, left, right, above, below, w_space)
 
 
 def group_lanes(channels):
@@ -309,7 +278,7 @@
         outs, refs = refs[5 : 5 + parts], refs[5 + parts :]
         normed, projected, contexts, affine = refs[:2], refs[2:4], refs[4], refs[5]
         spread = lax.dot_general(
-            stats_ref[...],
+            jnp.sum(stats_ref[...], axis=0),
             group_lanes(channels),
             (((1,), (1,)), ((), ())),
             precision=lax.Precision.HIGHEST,
@@ -420,45 +389,46 @@
     )(*blocks, *rest)
 
 
-def from_pixels(me, halves, rows, cols):
-    parts = len(halves[0])
-    pixels, frames, channels = halves[0][0].shape
-    half_rows = pixels // cols
-    part_rows = half_rows * len(halves)
-    flat = [block for blocks in halves for block in blocks]
-    total = len(flat) * half_rows
+def from_pixels(me, blocks, moves, shape, result=None):
+    frames, rows, cols, channels = shape
+    parts = lax.axis_size("tm")
+    half_rows = blocks[0].shape[0] // cols
+    part_rows = rows // parts
+    total = len(blocks) * half_rows
+    given = [] if result is None else [result]
 
     def kernel(me_ref, *refs):
-        ins, out_ref, turned, sem = refs[: len(flat)], refs[-3], refs[-2], refs[-1]
+        ins, out_ref, turned, sem = refs[: len(blocks)], refs[-3], refs[-2], refs[-1]
         copies = []
-        for h in range(len(halves)):
-            for d in range(parts):
-                base = lax.rem(me_ref[0] + d, parts) * part_rows + h * half_rows
-                for r in range(half_rows):
-                    slot = len(copies)
-                    turned[slot] = jnp.swapaxes(ins[h * parts + d][pl.ds(r * cols, cols)], 0, 1)
-                    copy = pltpu.make_async_copy(
-                        turned.at[slot], out_ref.at[:, base + r], sem.at[slot]
-                    )
-                    copy.start()
-                    copies.append(copy)
+        for n, (d, h) in enumerate(moves):
+            base = lax.rem(me_ref[0] + d, parts) * part_rows + h * half_rows
+            for r in range(half_rows):
+                slot = len(copies)
+                turned[slot] = jnp.swapaxes(ins[n][pl.ds(r * cols, cols)], 0, 1)
+                copy = pltpu.make_async_copy(turned.at[slot], out_ref.at[:, base + r], sem.at[slot])
+                copy.start()
+                copies.append(copy)
         for copy in copies:
             copy.wait()
 
     vmem = pl.BlockSpec(memory_space=pltpu.VMEM)
+    anywhere = pl.BlockSpec(memory_space=pl.ANY)
     return pl.pallas_call(
         kernel,
-        in_specs=[pl.BlockSpec(memory_space=pltpu.SMEM)] + [vmem] * len(flat),
-        out_specs=pl.BlockSpec(memory_space=pl.ANY),
-        out_shape=jax.ShapeDtypeStruct((frames, rows, cols, channels), BF16),
+        in_specs=[pl.BlockSpec(memory_space=pltpu.SMEM)]
+        + [vmem] * len(blocks)
+        + [anywhere] * len(given),
+        out_specs=anywhere,
+        out_shape=jax.ShapeDtypeStruct(shape, BF16),
+        input_output_aliases={1 + len(blocks): 0} if given else {},
         scratch_shapes=[
             pltpu.VMEM((total, frames, cols, channels), BF16),
             pltpu.SemaphoreType.DMA((total,)),
         ],
         compiler_params=params(),
-        cost_estimate=cost(0, 4 * frames * rows * cols * channels),
+        cost_estimate=cost(0, 4 * total * frames * cols * channels),
         name="from_pixels",
-    )(me, *flat)
+    )(me, *blocks, *given)
 
 
 def rotate(value, step):
@@ -470,9 +440,8 @@
     frames, rows, cols, channels = video.shape
     parts = lax.axis_size("tm")
     me = lax.axis_index("tm").astype(jnp.int32).reshape(1)
-    first, last = edge_columns(video)
-    left = shift(last, WIDTH, 1)
-    right = shift(first, WIDTH, -1)
+    left = shift(jnp.swapaxes(video[:, :, cols - 1], 0, 1), WIDTH, 1)
+    right = shift(jnp.swapaxes(video[:, :, 0], 0, 1), WIDTH, -1)
     pixels = to_pixels(video)
 
     def border(r):
@@ -481,10 +450,10 @@
     above = shift(border(rows - 1), "height", 1)
     below = shift(border(0), "height", -1)
     taps = w_space.reshape(9 * channels, channels)
-    inner = inner_conv(pixels, left, right, taps)
-    spatial, early, late = outer_conv(pixels, left, right, above, below, taps, inner)
+    early, late = end_frames(video, left, right, above, below, taps)
     before = shift(late, "tm", 1)
     after = shift(early, "tm", -1)
+    spatial = spatial_conv(pixels, left, right, above, below, taps)
     blocks, stats = temporal_conv(
         me, spatial.reshape(rows * cols, frames, channels), before, after, w_time
     )
@@ -496,18 +465,21 @@
     others = ("height", "width_0")
     count = lax.axis_size(others)
     shared = jnp.broadcast_to(stats[None], (count, *stats.shape))
-    stats = jnp.sum(lax.all_to_all(shared, others, 0, 0), axis=0)
+    stats = lax.all_to_all(shared, others, 0, 0)
     cell_count = float(
         frames * parts * rows * lax.axis_size("height") * cols * lax.axis_size(WIDTH)
         * (channels // GROUPS)
     )
     weights = (norm_gain.reshape(1, -1), norm_bias.reshape(1, -1), w_qkv, w_out)
     share = rows * cols // parts // 2
-    halves = []
+    own, far = [], []
     for h in range(2):
         results = attention(moved, stats, *weights, cell_count, h * share, share)
-        halves.append([results[0]] + [rotate(results[d], -d) for d in range(1, parts)])
-    return from_pixels(me, halves, rows, cols)
+        own.append(results[0])
+        far.append([rotate(results[d], -d) for d in range(1, parts)])
+    moves = [(0, 0), (0, 1)] + [(d, 0) for d in range(1, parts)]
+    result = from_pixels(me, own + far[0], moves, video.shape)
+    return from_pixels(me, far[1], [(d, 1) for d in range(1, parts)], video.shape, result)
 
 
 def solution(mesh):

time: 146 us -> 142 us (0.973)
  waiting for transfers between devices: 41.4 us -> 38.1 us
  local copies, waits for them, and re-layouts: 4.24 us -> 7.3 us
  Pallas kernels: 45 us -> 43 us
    pallas_call x3 -> x2, Pallas kernels: 16.9 us -> 13.3 us  [the longest x1 9.2 us: spatial_conv(): pl.pallas_call(kernel, out_shape=jax.ShapeDtypeStruct((rows, cols, frames...]
    ppermute x12, waiting for transfers between devices: 35.5 us -> 32.7 us  [rotate(): lax.ppermute(value, 'tm', [(i, (i + step) % size) for i in range(size)])]
    slice x0 -> x1, local copies, waits for them, and re-layouts: none -> 2.07 us  [per_device(): right = shift(jnp.swapaxes(video[:, :, 0], 0, 1), WIDTH, -1)]
    pallas_call x1 -> x2, Pallas kernels: 2.97 us -> 4.49 us  [from_pixels(): pl.pallas_call(kernel, in_specs=[pl.BlockSpec(memory_space=pltpu.SMEM)] +...]
    unnamed x30 -> x32, local copies, waits for them, and re-layouts: 3.24 us -> 4.22 us
  transfers between devices with their start and end apart: 19 -> 19, of which waited for: 9 -> 8; matrix products, arithmetic and copies ran while one was open for 2% -> 1% of each run, Pallas kernels for 15% -> 17%
where the time goes in v3:
time: 142 us
  Pallas kernels  43 us (30%)
  waiting for transfers between devices  38.1 us (27%)
  starting transfers between devices  32.3 us (23%)
  blocking collectives  19.9 us (14%)
  local copies, waits for them, and re-layouts  7.3 us (5%)
    ppermute x12, waiting for transfers between devices, rotate(): lax.ppermute(value, 'tm', [(i, (i + step) % size) for i in range(size)])  32.7 us
    all_to_all x1, blocking collectives, per_device(): stats = lax.all_to_all(shared, others, 0, 0)  19.9 us
    pallas_call x2, Pallas kernels, attention(): pl.pallas_call(kernel, in_specs=[vmem] * (parts + len(rest)), out_specs=[...  16.1 us
    ppermute x6, starting transfers between devices, shift(): return lax.ppermute(value, axis, pairs)  15.8 us
    ppermute x12, starting transfers between devices, rotate(): lax.ppermute(value, 'tm', [(i, (i + step) % size) for i in range(size)])  14.8 us
    pallas_call x1, Pallas kernels, spatial_conv(): pl.pallas_call(kernel, out_shape=jax.ShapeDtypeStruct((rows, cols, frames...  9.2 us
    pallas_call x1, Pallas kernels, temporal_conv(): pl.pallas_call(kernel, in_specs=[pl.BlockSpec(memory_space=pltpu.SMEM)] +...  5.22 us
    ppermute x6, waiting for transfers between devices, shift(): return lax.ppermute(value, axis, pairs)  4.6 us
  transfers between devices with their start and end apart: 19, of which 8 were waited for; matrix products, arithmetic and copies ran while one was open for 1% of the time, Pallas kernels for 17%

profile of v3, /device:TPU:1, one launch (start us, length us, event | category | flops | bytes accessed | tf_op | source)
XLA Modules:
  0.0 141.8 jit_solution(9268633442161662239)
XLA Ops:
  0.0 2.1 %fusion = (bf16[16,16,1,256]{3,2,1,0:T(2,128)(2,1)S(1)}, bf16[16,16,1,256]{3,2,1,0:T(2,128)(2,1)S(1)}) fusion(bf16[16,16,16,256]{3,2,1,0:T(8,128)(2,1)} %v_ref.3), kind=kLoop, calls=%fused_computation.7 | loop fusion | bytes 524288 | tf_op jit(solution)/shard_map/slice | solution.py:444
  2.1 0.1 copy.16
  2.2 4.9 %collective-permute-start = (bf16[16,16,256]{2,1,0:T(8,128)(2,1)S(1)}, bf16[16,16,256]{2,1,0:T(8,128)(2,1)S(1)}, u32[]{:S(2)}, u32[]{:S(2)}) collective-permute-start(bf16[16,16,256]{2,1,0:T(8,128)(2,1)S(1)} %bitcast.22), channel_id=1, source_target_pairs={{0,1},{1,2},{2,3},{3,4},{4,5},{5,6},{6,7},{7,8},{8,9},{9,10},{10,1... | collective-permute-start | bytes 393224 | tf_op jit(solution)/shard_map/ppermute | solution.py:33
  7.2 0.1 copy.15
  7.3 1.9 %collective-permute-start.1 = (bf16[16,16,256]{2,1,0:T(8,128)(2,1)S(1)}, bf16[16,16,256]{2,1,0:T(8,128)(2,1)S(1)}, u32[]{:S(2)}, u32[]{:S(2)}) collective-permute-start(bf16[16,16,256]{2,1,0:T(8,128)(2,1)S(1)} %bitcast.23), channel_id=1, source_target_pairs={{1,0},{2,1},{3,2},{4,3},{5,4},{6,5},{7,6},{8,7},{9,8},{10,9},{11,1... | collective-permute-start | bytes 393224 | tf_op jit(solution)/shard_map/ppermute | solution.py:33
  9.2 4.0 %to_pixels.1.p_ref = bf16[16,16,16,256]{3,2,1,0:T(8,128)(2,1)} custom-call(bf16[16,16,16,256]{3,2,1,0:T(8,128)(2,1)} %v_ref.3), custom_call_target="tpu_custom_call" | custom-call | bytes 4194304 | tf_op jit(solution)/shard_map/to_pixels/pallas_call | solution.py:44
  13.2 1.0 slice_bitcast_fusion
  14.2 0.0 collective-permute-done.l_ref
  14.2 0.0 copy-start.6
  14.2 0.0 collective-permute-done.1.r_ref
  14.3 3.2 %collective-permute-start.2 = (bf16[18,16,256]{2,1,0:T(8,128)(2,1)S(1)}, bf16[18,16,256]{2,1,0:T(8,128)(2,1)S(1)}, u32[]{:S(2)}, u32[]{:S(2)}) collective-permute-start(bf16[18,16,256]{2,1,0:T(8,128)(2,1)S(1)} %pad_maximum_fusion), channel_id=1, source_target_pairs={{0,16},{16,32},{32,48},{1,17},{17,33},{33,49},{2,18},{18,34},{34,5... | collective-permute-start | bytes 442376 | tf_op jit(solution)/shard_map/ppermute | solution.py:33
  17.6 1.3 collective-permute-start.3
  18.9 0.7 collective-permute-done.2.a_ref
  19.6 3.8 %collective-permute-done.3.b_ref = bf16[18,16,256]{2,1,0:T(8,128)(2,1)S(1)} collective-permute-done((bf16[18,16,256]{2,1,0:T(8,128)(2,1)S(1)}, bf16[18,16,256]{2,1,0:T(8,128)(2,1)S(1)}, u32[]{:S(2)}, u32[]{:S(2)}) %collective-permute-start.3) | collective-permute-done | bytes 147488 | tf_op jit(solution)/shard_map/ppermute | solution.py:33
  23.4 0.0 copy-done.6
  23.5 0.7 copy-done.9
  24.1 4.1 %end_frames.1 = (bf16[256,256]{1,0:T(8,128)(2,1)}, bf16[256,256]{1,0:T(8,128)(2,1)}) custom-call(bf16[16,16,16,256]{3,2,1,0:T(8,128)(2,1)} %v_ref.3, bf16[16,16,256]{2,1,0:T(8,128)(2,1)} %copy-done.6, bf16[16,16,256]{2,1,0:T(8,128)(2,1)} %copy-done.7, bf16[18,16,256]{2,1,0:T(8,128)(2,1)} %copy-done.8, bf16[18,16,256]{2,1,0:T(8,128)(2,1)} %copy-done.9, ...), custom_call_target="tpu_custom_call" | custom-call | flops 603979776 | bytes 524288 | tf_op jit(solution)/shard_map/end_frames/pallas_call | solution.py:149
  28.2 3.1 %collective-permute-start.4 = (bf16[256,256]{1,0:T(8,128)(2,1)}, bf16[256,256]{1,0:T(8,128)(2,1)S(1)}, u32[]{:S(2)}, u32[]{:S(2)}) collective-permute-start(bf16[256,256]{1,0:T(8,128)(2,1)} %get-tuple-element.20), channel_id=1, source_target_pairs={{0,64},{64,128},{128,192},{1,65},{65,129},{129,193},{2,66},{66,130... | collective-permute-start | bytes 393224 | tf_op jit(solution)/shard_map/ppermute | solution.py:33
  31.3 1.3 collective-permute-start.5
  32.6 9.2 %spatial_conv.1 = bf16[16,16,16,256]{3,2,1,0:T(8,128)(2,1)} custom-call(bf16[16,16,16,256]{3,2,1,0:T(8,128)(2,1)} %to_pixels.1.p_ref, bf16[16,16,256]{2,1,0:T(8,128)(2,1)} %copy-done.6, bf16[16,16,256]{2,1,0:T(8,128)(2,1)} %copy-done.7, bf16[18,16,256]{2,1,0:T(8,128)(2,1)} %copy-done.8, bf16[18,16,256]{2,1,0:T(8,128)(2,1)} %copy-done.9, ...), custom_call_target="tpu_custom_call" | custom-call | flops 4831838208 | bytes 4194304 | tf_op jit(solution)/shard_map/spatial_conv/pallas_call | solution.py:88
  41.8 0.0 collective-permute-done.4.b_ref
  41.8 0.0 collective-permute-done.5.a_ref
  41.8 0.6 copy-done.13
  42.5 0.1 copy-done.14
  42.5 5.2 %temporal_conv.1 = (bf16[64,16,256]{2,1,0:T(8,128)(2,1)}, bf16[64,16,256]{2,1,0:T(8,128)(2,1)}, bf16[64,16,256]{2,1,0:T(8,128)(2,1)}, bf16[64,16,256]{2,1,0:T(8,128)(2,1)}, f32[8,128]{1,0:T(8,128)}) custom-call(s32[1]{0:T(128)} %bitcast.me_ref, bf16[256,16,256]{2,1,0:T(8,128)(2,1)} %bitcast.29, bf16[256,256]{1,0:T(8,128)(2,1)} %copy-done.13, ...), custom_call_target="tpu_custom_call" | custom-call | flops 1610612736 | bytes 4194304 | tf_op jit(solution)/shard_map/temporal_conv/pallas_call | solution.py:248
  47.7 2.1 %collective-permute-start.6 = (bf16[64,16,256]{2,1,0:T(8,128)(2,1)}, bf16[64,16,256]{2,1,0:T(8,128)(2,1)S(1)}, u32[]{:S(2)}, u32[]{:S(2)}) collective-permute-start(bf16[64,16,256]{2,1,0:T(8,128)(2,1)} %get-tuple-element.23), channel_id=1, source_target_pairs={{0,64},{64,128},{128,192},{192,0},{1,65},{65,129},{129,193},{193,1... | collective-permute-start | bytes 1572872 | tf_op jit(solution)/shard_map/ppermute | solution.py:436
  49.8 2.5 %collective-permute-start.7 = (bf16[64,16,256]{2,1,0:T(8,128)(2,1)}, bf16[64,16,256]{2,1,0:T(8,128)(2,1)S(1)}, u32[]{:S(2)}, u32[]{:S(2)}) collective-permute-start(bf16[64,16,256]{2,1,0:T(8,128)(2,1)} %get-tuple-element.24), channel_id=1, source_target_pairs={{0,128},{64,192},{128,0},{192,64},{1,129},{65,193},{129,1},{193,65... | collective-permute-start | bytes 1572872 | tf_op jit(solution)/shard_map/ppermute | solution.py:436
  52.3 1.1 collective-permute-start.8
  53.4 0.0 collective-permute-start.11
  53.4 2.1 %collective-permute-start.10 = (f32[8,128]{1,0:T(8,128)}, f32[8,128]{1,0:T(8,128)S(1)}, u32[]{:S(2)}, u32[]{:S(2)}) collective-permute-start(f32[8,128]{1,0:T(8,128)} %get-tuple-element.26), channel_id=1, source_target_pairs={{0,128},{64,192},{128,0},{192,64},{1,129},{65,193},{129,1},{193,65... | collective-permute-start | bytes 12296 | tf_op jit(solution)/shard_map/ppermute | solution.py:436
  55.5 20.1 %collective-permute-done.11 = f32[8,128]{1,0:T(8,128)S(1)} collective-permute-done((f32[8,128]{1,0:T(8,128)}, f32[8,128]{1,0:T(8,128)S(1)}, u32[]{:S(2)}, u32[]{:S(2)}) %collective-permute-start.11) | collective-permute-done | bytes 4128 | tf_op jit(solution)/shard_map/ppermute | solution.py:436
  75.6 1.1 collective-permute-start.9
  76.7 0.0 collective-permute-done.10
  76.7 2.7 %collective-permute-done.9 = f32[8,128]{1,0:T(8,128)S(1)} collective-permute-done((f32[8,128]{1,0:T(8,128)}, f32[8,128]{1,0:T(8,128)S(1)}, u32[]{:S(2)}, u32[]{:S(2)}) %collective-permute-start.9) | collective-permute-done | bytes 4128 | tf_op jit(solution)/shard_map/ppermute | solution.py:436
  79.5 0.7 add_add_fusion
  80.2 1.7 %collective-permute-start.12 = (f32[8,128]{1,0:T(8,128)S(1)}, f32[8,128]{1,0:T(8,128)S(1)}, u32[]{:S(2)}, u32[]{:S(2)}) collective-permute-start(f32[8,128]{1,0:T(8,128)S(1)} %add_add_fusion), channel_id=1, source_target_pairs={{0,1},{1,0},{2,3},{3,2},{4,5},{5,4},{6,7},{7,6},{8,9},{9,8},{10,11... | collective-permute-start | bytes 12296 | tf_op jit(solution)/shard_map/ppermute | solution.py:464
  81.9 0.8 collective-permute-done.12
  82.7 19.9 %all_to_all.5.refs_4_ = f32[32,8,128]{2,1,0:T(8,128)} all-to-all(f32[32,8,128]{2,1,0:T(8,128)S(1)} %broadcast_in_dim.2), channel_id=1, replica_groups=mesh['tm'=4,'height'=4,'width_0'=8,'width_1'=2] {'height','width_0'}, dimensions={0} | all-to-all | bytes 262144 | tf_op jit(solution)/shard_map/all_to_all | solution.py:468
  102.7 0.0 collective-permute-done.6.refs_1_
  102.7 0.0 collective-permute-done.7.refs_2_
  102.7 0.0 collective-permute-done.8.refs_3_
  102.7 0.7 copy-done.10
  103.4 0.2 copy-done.11
  103.6 0.2 copy-done.12
  103.8 8.0 %attention.3 = (bf16[32,16,256]{2,1,0:T(8,128)(2,1)}, bf16[32,16,256]{2,1,0:T(8,128)(2,1)}, bf16[32,16,256]{2,1,0:T(8,128)(2,1)}, bf16[32,16,256]{2,1,0:T(8,128)(2,1)}) custom-call(bf16[64,16,256]{2,1,0:T(8,128)(2,1)} %get-tuple-element.22.refs_0_, bf16[64,16,256]{2,1,0:T(8,128)(2,1)} %copy-done.10, bf16[64,16,256]{2,1,0:T(8,128)(2,1)} %copy-done.11, ...), custom_call_target="tpu_custom_call" | custom-call | flops 2147483648 | bytes 2097152 | tf_op jit(solution)/shard_map/attention/pallas_call | solution.py:378
  111.9 1.1 collective-permute-start.16
  113.0 0.9 collective-permute-start.17
  113.9 0.6 collective-permute-start.18
  114.5 8.0 %attention.2 = (bf16[32,16,256]{2,1,0:T(8,128)(2,1)}, bf16[32,16,256]{2,1,0:T(8,128)(2,1)}, bf16[32,16,256]{2,1,0:T(8,128)(2,1)}, bf16[32,16,256]{2,1,0:T(8,128)(2,1)}) custom-call(bf16[64,16,256]{2,1,0:T(8,128)(2,1)} %get-tuple-element.22.refs_0_, bf16[64,16,256]{2,1,0:T(8,128)(2,1)} %copy-done.10, bf16[64,16,256]{2,1,0:T(8,128)(2,1)} %copy-done.11, ...), custom_call_target="tpu_custom_call" | custom-call | flops 2147483648 | bytes 2097152 | tf_op jit(solution)/shard_map/attention/pallas_call | solution.py:378
  122.5 2.1 %collective-permute-start.13 = (bf16[32,16,256]{2,1,0:T(8,128)(2,1)}, bf16[32,16,256]{2,1,0:T(8,128)(2,1)S(1)}, u32[]{:S(2)}, u32[]{:S(2)}) collective-permute-start(bf16[32,16,256]{2,1,0:T(8,128)(2,1)} %get-tuple-element.27), channel_id=1, source_target_pairs={{0,192},{64,0},{128,64},{192,128},{1,193},{65,1},{129,65},{193,129... | collective-permute-start | bytes 786440 | tf_op jit(solution)/shard_map/ppermute | solution.py:436
  124.6 0.9 collective-permute-start.14
  125.5 0.0 collective-permute-done.16.refs_2_
  125.5 0.3 collective-permute-start.15
  125.8 0.0 collective-permute-done.17.refs_3_
  125.8 2.4 %collective-permute-done.18.refs_4_ = bf16[32,16,256]{2,1,0:T(8,128)(2,1)S(1)} collective-permute-done((bf16[32,16,256]{2,1,0:T(8,128)(2,1)}, bf16[32,16,256]{2,1,0:T(8,128)(2,1)S(1)}, u32[]{:S(2)}, u32[]{:S(2)}) %collective-permute-start.18) | collective-permute-done | bytes 262176 | tf_op jit(solution)/shard_map/ppermute | solution.py:436
  128.2 0.0 copy-done.1
  128.2 0.7 copy-done.3
  128.9 2.4 %from_pixels.2.refs_3_ = bf16[16,16,16,256]{3,2,1,0:T(8,128)(2,1)} custom-call(s32[1]{0:T(128)} %bitcast.me_ref, bf16[32,16,256]{2,1,0:T(8,128)(2,1)} %get-tuple-element.30.refs_0_, bf16[32,16,256]{2,1,0:T(8,128)(2,1)} %get-tuple-element.31.refs_1_, bf16[32,16,256]{2,1,0:T(8,128)(2,1)} %copy-done, bf16[32,16,256]{2,1,0:T(8,128)(2,1)} %copy-done.1, ...), custom_call_target="tpu_custom_call" | custom-call | bytes 2621440 | tf_op jit(solution)/shard_map/from_pixels/pallas_call | solution.py:416
  131.4 0.0 collective-permute-done.13.refs_0_
  131.4 0.2 collective-permute-done.14.refs_1_
  131.6 7.3 %collective-permute-done.15.refs_2_ = bf16[32,16,256]{2,1,0:T(8,128)(2,1)S(1)} collective-permute-done((bf16[32,16,256]{2,1,0:T(8,128)(2,1)}, bf16[32,16,256]{2,1,0:T(8,128)(2,1)S(1)}, u32[]{:S(2)}, u32[]{:S(2)}) %collective-permute-start.15) | collective-permute-done | bytes 262176 | tf_op jit(solution)/shard_map/ppermute | solution.py:436
  138.9 0.0 copy-done.4
  138.9 0.7 copy-done.5
  139.6 2.1 %from_pixels.3 = bf16[16,16,16,256]{3,2,1,0:T(8,128)(2,1)} custom-call(s32[1]{0:T(128)} %bitcast.me_ref, bf16[32,16,256]{2,1,0:T(8,128)(2,1)} %copy-done.2, bf16[32,16,256]{2,1,0:T(8,128)(2,1)} %copy-done.4, bf16[32,16,256]{2,1,0:T(8,128)(2,1)} %copy-done.5, bf16[16,16,16,256]{3,2,1,0:T(8,128)(2,1)} %from_pixels.2.refs_3_), custom_call_target="tpu_custom_call", output_to_operand_aliasing={{}: (4, {})} | custom-call | bytes 1572864 | tf_op jit(solution)/shard_map/from_pixels/pallas_call | solution.py:416
  (24 shorter events, 0.1 us)
Async XLA Ops:
  2.2 12.0 %collective-permute-start = (bf16[16,16,256]{2,1,0:T(8,128)(2,1)S(1)}, bf16[16,16,256]{2,1,0:T(8,128)(2,1)S(1)}, u32[]{:S(2)}, u32[]{:S(2)}) collective-permute-start(bf16[16,16,256]{2,1,0:T(8,128)(2,1)S(1)} %bitcast.22), channel_id=1, source_target_pairs={{0,1},{1,2},{2,3},{3,4},{4,5},{5,6},{6,7},{7,8},{8,9},{9,10},{10,1... | collective-permute-start | bytes 393224 | tf_op jit(solution)/shard_map/ppermute | solution.py:33
  7.3 6.9 %collective-permute-start.1 = (bf16[16,16,256]{2,1,0:T(8,128)(2,1)S(1)}, bf16[16,16,256]{2,1,0:T(8,128)(2,1)S(1)}, u32[]{:S(2)}, u32[]{:S(2)}) collective-permute-start(bf16[16,16,256]{2,1,0:T(8,128)(2,1)S(1)} %bitcast.23), channel_id=1, source_target_pairs={{1,0},{2,1},{3,2},{4,3},{5,4},{6,5},{7,6},{8,7},{9,8},{10,9},{11,1... | collective-permute-start | bytes 393224 | tf_op jit(solution)/shard_map/ppermute | solution.py:33
  14.2 9.2 %copy-start.6 = (bf16[16,16,256]{2,1,0:T(8,128)(2,1)}, bf16[16,16,256]{2,1,0:T(8,128)(2,1)S(1)}, u32[]{:S(2)}) copy-start(bf16[16,16,256]{2,1,0:T(8,128)(2,1)S(1)} %collective-permute-done.l_ref) | copy-start | bytes 393220
  14.3 9.2 %copy-start.7 = (bf16[16,16,256]{2,1,0:T(8,128)(2,1)}, bf16[16,16,256]{2,1,0:T(8,128)(2,1)S(1)}, u32[]{:S(2)}) copy-start(bf16[16,16,256]{2,1,0:T(8,128)(2,1)S(1)} %collective-permute-done.1.r_ref) | copy-start | bytes 393220
  14.3 5.3 %collective-permute-start.2 = (bf16[18,16,256]{2,1,0:T(8,128)(2,1)S(1)}, bf16[18,16,256]{2,1,0:T(8,128)(2,1)S(1)}, u32[]{:S(2)}, u32[]{:S(2)}) collective-permute-start(bf16[18,16,256]{2,1,0:T(8,128)(2,1)S(1)} %pad_maximum_fusion), channel_id=1, source_target_pairs={{0,16},{16,32},{32,48},{1,17},{17,33},{33,49},{2,18},{18,34},{34,5... | collective-permute-start | bytes 442376 | tf_op jit(solution)/shard_map/ppermute | solution.py:33
  17.6 5.9 %collective-permute-start.3 = (bf16[18,16,256]{2,1,0:T(8,128)(2,1)S(1)}, bf16[18,16,256]{2,1,0:T(8,128)(2,1)S(1)}, u32[]{:S(2)}, u32[]{:S(2)}) collective-permute-start(bf16[18,16,256]{2,1,0:T(8,128)(2,1)S(1)} %pad_maximum_fusion.1), channel_id=1, source_target_pairs={{16,0},{32,16},{48,32},{17,1},{33,17},{49,33},{18,2},{34,18},{50,3... | collective-permute-start | bytes 442376 | tf_op jit(solution)/shard_map/ppermute | solution.py:33
  19.6 3.9 %copy-start.8 = (bf16[18,16,256]{2,1,0:T(8,128)(2,1)}, bf16[18,16,256]{2,1,0:T(8,128)(2,1)S(1)}, u32[]{:S(2)}) copy-start(bf16[18,16,256]{2,1,0:T(8,128)(2,1)S(1)} %collective-permute-done.2.a_ref) | copy-start | bytes 442372
  23.4 0.7 copy-start.9
  28.2 13.6 %collective-permute-start.4 = (bf16[256,256]{1,0:T(8,128)(2,1)}, bf16[256,256]{1,0:T(8,128)(2,1)S(1)}, u32[]{:S(2)}, u32[]{:S(2)}) collective-permute-start(bf16[256,256]{1,0:T(8,128)(2,1)} %get-tuple-element.20), channel_id=1, source_target_pairs={{0,64},{64,128},{128,192},{1,65},{65,129},{129,193},{2,66},{66,130... | collective-permute-start | bytes 393224 | tf_op jit(solution)/shard_map/ppermute | solution.py:33
  31.3 10.5 %collective-permute-start.5 = (bf16[256,256]{1,0:T(8,128)(2,1)}, bf16[256,256]{1,0:T(8,128)(2,1)S(1)}, u32[]{:S(2)}, u32[]{:S(2)}) collective-permute-start(bf16[256,256]{1,0:T(8,128)(2,1)} %get-tuple-element.21), channel_id=1, source_target_pairs={{64,0},{128,64},{192,128},{65,1},{129,65},{193,129},{66,2},{130,66... | collective-permute-start | bytes 393224 | tf_op jit(solution)/shard_map/ppermute | solution.py:33
  41.8 0.6 copy-start.13
  41.8 0.7 copy-start.14
  47.7 54.9 %collective-permute-start.6 = (bf16[64,16,256]{2,1,0:T(8,128)(2,1)}, bf16[64,16,256]{2,1,0:T(8,128)(2,1)S(1)}, u32[]{:S(2)}, u32[]{:S(2)}) collective-permute-start(bf16[64,16,256]{2,1,0:T(8,128)(2,1)} %get-tuple-element.23), channel_id=1, source_target_pairs={{0,64},{64,128},{128,192},{192,0},{1,65},{65,129},{129,193},{193,1... | collective-permute-start | bytes 1572872 | tf_op jit(solution)/shard_map/ppermute | solution.py:436
  49.8 52.8 %collective-permute-start.7 = (bf16[64,16,256]{2,1,0:T(8,128)(2,1)}, bf16[64,16,256]{2,1,0:T(8,128)(2,1)S(1)}, u32[]{:S(2)}, u32[]{:S(2)}) collective-permute-start(bf16[64,16,256]{2,1,0:T(8,128)(2,1)} %get-tuple-element.24), channel_id=1, source_target_pairs={{0,128},{64,192},{128,0},{192,64},{1,129},{65,193},{129,1},{193,65... | collective-permute-start | bytes 1572872 | tf_op jit(solution)/shard_map/ppermute | solution.py:436
  52.3 50.4 %collective-permute-start.8 = (bf16[64,16,256]{2,1,0:T(8,128)(2,1)}, bf16[64,16,256]{2,1,0:T(8,128)(2,1)S(1)}, u32[]{:S(2)}, u32[]{:S(2)}) collective-permute-start(bf16[64,16,256]{2,1,0:T(8,128)(2,1)} %get-tuple-element.25), channel_id=1, source_target_pairs={{0,192},{64,0},{128,64},{192,128},{1,193},{65,1},{129,65},{193,129... | collective-permute-start | bytes 1572872 | tf_op jit(solution)/shard_map/ppermute | solution.py:436
  53.4 22.2 %collective-permute-start.11 = (f32[8,128]{1,0:T(8,128)}, f32[8,128]{1,0:T(8,128)S(1)}, u32[]{:S(2)}, u32[]{:S(2)}) collective-permute-start(f32[8,128]{1,0:T(8,128)} %get-tuple-element.26), channel_id=1, source_target_pairs={{0,192},{64,0},{128,64},{192,128},{1,193},{65,1},{129,65},{193,129... | collective-permute-start | bytes 12296 | tf_op jit(solution)/shard_map/ppermute | solution.py:436
  53.4 23.3 %collective-permute-start.10 = (f32[8,128]{1,0:T(8,128)}, f32[8,128]{1,0:T(8,128)S(1)}, u32[]{:S(2)}, u32[]{:S(2)}) collective-permute-start(f32[8,128]{1,0:T(8,128)} %get-tuple-element.26), channel_id=1, source_target_pairs={{0,128},{64,192},{128,0},{192,64},{1,129},{65,193},{129,1},{193,65... | collective-permute-start | bytes 12296 | tf_op jit(solution)/shard_map/ppermute | solution.py:436
  75.6 3.9 %collective-permute-start.9 = (f32[8,128]{1,0:T(8,128)}, f32[8,128]{1,0:T(8,128)S(1)}, u32[]{:S(2)}, u32[]{:S(2)}) collective-permute-start(f32[8,128]{1,0:T(8,128)} %get-tuple-element.26), channel_id=1, source_target_pairs={{0,64},{64,128},{128,192},{192,0},{1,65},{65,129},{129,193},{193,1... | collective-permute-start | bytes 12296 | tf_op jit(solution)/shard_map/ppermute | solution.py:436
  80.2 2.5 %collective-permute-start.12 = (f32[8,128]{1,0:T(8,128)S(1)}, f32[8,128]{1,0:T(8,128)S(1)}, u32[]{:S(2)}, u32[]{:S(2)}) collective-permute-start(f32[8,128]{1,0:T(8,128)S(1)} %add_add_fusion), channel_id=1, source_target_pairs={{0,1},{1,0},{2,3},{3,2},{4,5},{5,4},{6,7},{7,6},{8,9},{9,8},{10,11... | collective-permute-start | bytes 12296 | tf_op jit(solution)/shard_map/ppermute | solution.py:464
  102.7 0.8 copy-start.10
  102.7 1.0 copy-start.11
  102.7 1.2 copy-start.12
  111.9 13.6 %collective-permute-start.16 = (bf16[32,16,256]{2,1,0:T(8,128)(2,1)}, bf16[32,16,256]{2,1,0:T(8,128)(2,1)S(1)}, u32[]{:S(2)}, u32[]{:S(2)}) collective-permute-start(bf16[32,16,256]{2,1,0:T(8,128)(2,1)} %get-tuple-element.32), channel_id=1, source_target_pairs={{0,192},{64,0},{128,64},{192,128},{1,193},{65,1},{129,65},{193,129... | collective-permute-start | bytes 786440 | tf_op jit(solution)/shard_map/ppermute | solution.py:436
  113.0 12.8 %collective-permute-start.17 = (bf16[32,16,256]{2,1,0:T(8,128)(2,1)}, bf16[32,16,256]{2,1,0:T(8,128)(2,1)S(1)}, u32[]{:S(2)}, u32[]{:S(2)}) collective-permute-start(bf16[32,16,256]{2,1,0:T(8,128)(2,1)} %get-tuple-element.33), channel_id=1, source_target_pairs={{0,128},{64,192},{128,0},{192,64},{1,129},{65,193},{129,1},{193,65... | collective-permute-start | bytes 786440 | tf_op jit(solution)/shard_map/ppermute | solution.py:436
  113.9 14.3 %collective-permute-start.18 = (bf16[32,16,256]{2,1,0:T(8,128)(2,1)}, bf16[32,16,256]{2,1,0:T(8,128)(2,1)S(1)}, u32[]{:S(2)}, u32[]{:S(2)}) collective-permute-start(bf16[32,16,256]{2,1,0:T(8,128)(2,1)} %get-tuple-element.34), channel_id=1, source_target_pairs={{0,64},{64,128},{128,192},{192,0},{1,65},{65,129},{129,193},{193,1... | collective-permute-start | bytes 786440 | tf_op jit(solution)/shard_map/ppermute | solution.py:436
  122.5 8.8 %collective-permute-start.13 = (bf16[32,16,256]{2,1,0:T(8,128)(2,1)}, bf16[32,16,256]{2,1,0:T(8,128)(2,1)S(1)}, u32[]{:S(2)}, u32[]{:S(2)}) collective-permute-start(bf16[32,16,256]{2,1,0:T(8,128)(2,1)} %get-tuple-element.27), channel_id=1, source_target_pairs={{0,192},{64,0},{128,64},{192,128},{1,193},{65,1},{129,65},{193,129... | collective-permute-start | bytes 786440 | tf_op jit(solution)/shard_map/ppermute | solution.py:436
  124.6 7.0 %collective-permute-start.14 = (bf16[32,16,256]{2,1,0:T(8,128)(2,1)}, bf16[32,16,256]{2,1,0:T(8,128)(2,1)S(1)}, u32[]{:S(2)}, u32[]{:S(2)}) collective-permute-start(bf16[32,16,256]{2,1,0:T(8,128)(2,1)} %get-tuple-element.28), channel_id=1, source_target_pairs={{0,128},{64,192},{128,0},{192,64},{1,129},{65,193},{129,1},{193,65... | collective-permute-start | bytes 786440 | tf_op jit(solution)/shard_map/ppermute | solution.py:436
  125.5 2.7 %copy-start = (bf16[32,16,256]{2,1,0:T(8,128)(2,1)}, bf16[32,16,256]{2,1,0:T(8,128)(2,1)S(1)}, u32[]{:S(2)}) copy-start(bf16[32,16,256]{2,1,0:T(8,128)(2,1)S(1)} %collective-permute-done.16.refs_2_) | copy-start | bytes 786436
  125.5 13.4 %collective-permute-start.15 = (bf16[32,16,256]{2,1,0:T(8,128)(2,1)}, bf16[32,16,256]{2,1,0:T(8,128)(2,1)S(1)}, u32[]{:S(2)}, u32[]{:S(2)}) collective-permute-start(bf16[32,16,256]{2,1,0:T(8,128)(2,1)} %get-tuple-element.29), channel_id=1, source_target_pairs={{0,64},{64,128},{128,192},{192,0},{1,65},{65,129},{129,193},{193,1... | collective-permute-start | bytes 786440 | tf_op jit(solution)/shard_map/ppermute | solution.py:436
  125.8 2.4 %copy-start.1 = (bf16[32,16,256]{2,1,0:T(8,128)(2,1)}, bf16[32,16,256]{2,1,0:T(8,128)(2,1)S(1)}, u32[]{:S(2)}) copy-start(bf16[32,16,256]{2,1,0:T(8,128)(2,1)S(1)} %collective-permute-done.17.refs_3_) | copy-start | bytes 786436
  128.2 0.7 copy-start.3
  131.4 7.5 %copy-start.2 = (bf16[32,16,256]{2,1,0:T(8,128)(2,1)}, bf16[32,16,256]{2,1,0:T(8,128)(2,1)S(1)}, u32[]{:S(2)}) copy-start(bf16[32,16,256]{2,1,0:T(8,128)(2,1)S(1)} %collective-permute-done.13.refs_0_) | copy-start | bytes 786436
  131.6 7.3 %copy-start.4 = (bf16[32,16,256]{2,1,0:T(8,128)(2,1)}, bf16[32,16,256]{2,1,0:T(8,128)(2,1)S(1)}, u32[]{:S(2)}) copy-start(bf16[32,16,256]{2,1,0:T(8,128)(2,1)S(1)} %collective-permute-done.14.refs_1_) | copy-start | bytes 786436
  138.9 0.7 copy-start.5

commit v4 on v3

--- a/solution.py
+++ b/solution.py
@@ -13,7 +13,7 @@
 WIDTH = ("width_0", "width_1")
 BF16 = jnp.bfloat16
 F32 = jnp.float32
-VMEM_BYTES = 60 * 1024 * 1024
+VMEM_BYTES = 16 * 1024 * 1024
 
 
 def params(**kw):
@@ -33,39 +33,57 @@
     return lax.ppermute(value, axis, pairs)
 
 
-def to_pixels(video):
+def edge_columns(video):
     frames, rows, cols, channels = video.shape
-    step = 4
-
-    def kernel(v_ref, out_ref):
-        for r in range(step):
-            out_ref[r] = jnp.swapaxes(v_ref[:, r], 0, 1)
+
+    def kernel(v_ref, first_ref, last_ref):
+        for r in range(rows):
+            turned = jnp.swapaxes(v_ref[:, r], 0, 1)
+            first_ref[r] = turned[0]
+            last_ref[r] = turned[cols - 1]
 
     return pl.pallas_call(
         kernel,
-        grid=(rows // step,),
-        in_specs=[pl.BlockSpec((frames, step, cols, channels), lambda i: (0, i, 0, 0))],
-        out_specs=pl.BlockSpec((step, cols, frames, channels), lambda i: (i, 0, 0, 0)),
-        out_shape=jax.ShapeDtypeStruct((rows, cols, frames, channels), BF16),
-        compiler_params=params(),
-        cost_estimate=cost(0, 2 * video.size * 2),
-        name="to_pixels",
+        out_shape=[jax.ShapeDtypeStruct((rows, frames, channels), BF16)] * 2,
+        compiler_params=params(),
+        cost_estimate=cost(0, video.size * 2),
+        name="edge_columns",
     )(video)
 
 
-def spatial_conv(pixels, left, right, above, below, w_space):
-    rows, cols, frames, channels = pixels.shape
+def extend_columns(first, last, above, below):
+    rows, frames, channels = first.shape
+    cols = above.shape[1]
+
+    def kernel(f_ref, l_ref, a_ref, b_ref, *outs):
+        for ref, row in ((a_ref, 0), (b_ref, rows + 1)):
+            turned = jnp.swapaxes(ref[...], 0, 1)
+            outs[0][row] = turned[0]
+            outs[1][row] = turned[cols - 1]
+        for out, ref in zip(outs, (f_ref, l_ref)):
+            out[pl.ds(1, rows)] = ref[...]
+
+    return pl.pallas_call(
+        kernel,
+        out_shape=[jax.ShapeDtypeStruct((rows + 2, frames, channels), BF16)] * 2,
+        compiler_params=params(),
+        cost_estimate=cost(0, 8 * first.size),
+        name="extend_columns",
+    )(first, last, above, below)
+
+
+def spatial_conv(video, above, below, left, right, w_space):
+    frames, rows, cols, channels = video.shape
     span = 2
     count = span * cols * frames
     unroll = 2
 
-    def kernel(p_ref, l_ref, r_ref, a_ref, b_ref, w_ref, out_ref, pad):
-        pad[0] = a_ref[...]
-        pad[rows + 1] = b_ref[...]
-        for r in range(rows):
-            pad[r + 1, 0] = l_ref[r]
-            pad[r + 1, pl.ds(1, cols)] = p_ref[r]
-            pad[r + 1, cols + 1] = r_ref[r]
+    def kernel(v_ref, a_ref, b_ref, l_ref, r_ref, w_ref, out_ref, pad):
+        for r in range(rows + 2):
+            row = a_ref[...] if r == 0 else b_ref[...] if r == rows + 1 else v_ref[:, r - 1]
+            pad[r, 0] = l_ref[r]
+            pad[r, pl.ds(1, cols)] = jnp.swapaxes(row, 0, 1)
+            pad[r, cols + 1] = r_ref[r]
 
         def body(i, carry):
             for u in range(unroll):
@@ -92,10 +110,10 @@
         compiler_params=params(),
         cost_estimate=cost(2 * size * channels * 9, 4 * size),
         name="spatial_conv",
-    )(pixels, left, right, above, below, w_space)
-
-
-def end_frames(video, left, right, above, below, w_space):
+    )(video, above, below, left, right, w_space)
+
+
+def end_frames(video, above, below, left, right, w_space):
     frames, rows, cols, channels = video.shape
     lanes = 128
     slabs = channels // lanes
@@ -103,7 +121,7 @@
     taps = 9
     ends = (0, frames - 1)
 
-    def kernel(v_ref, l_ref, r_ref, a_ref, b_ref, w_ref, early_ref, late_ref, held, side, wide, window, sem):
+    def kernel(v_ref, a_ref, b_ref, l_ref, r_ref, w_ref, early_ref, late_ref, held, side, wide, window, sem):
         fetch = [
             pltpu.make_async_copy(v_ref.at[frame], held.at[k], sem.at[k])
             for k, frame in enumerate(ends)
@@ -112,9 +130,9 @@
             copy.start()
         for j in range(slabs):
             cut = slice(j * lanes, (j + 1) * lanes)
-            for n, ref in enumerate((l_ref, r_ref, a_ref, b_ref)):
-                size = ref.shape[0] * frames
-                side[n, j, pl.ds(0, size)] = ref[...].reshape(size, channels)[:, cut].astype(F32)
+            for n, ref in enumerate((l_ref, r_ref)):
+                size = (rows + 2) * frames
+                side[n, j] = ref[...].reshape(size, channels)[:, cut].astype(F32)
         for copy in fetch:
             copy.wait()
         outs = (early_ref, late_ref)
@@ -122,13 +140,11 @@
             for j in range(slabs):
                 cut = slice(j * lanes, (j + 1) * lanes)
                 for n, at in ((0, 7), (1, pitch)):
-                    wide[k, j, pl.ds(pitch + at, rows, stride=pitch)] = side[
-                        n, j, pl.ds(frame, rows, stride=frames)
+                    wide[k, j, pl.ds(at, rows + 2, stride=pitch)] = side[
+                        n, j, pl.ds(frame, rows + 2, stride=frames)
                     ]
-                for n, row in ((2, 0), (3, rows + 1)):
-                    wide[k, j, pl.ds(row * pitch + 7, cols + 2)] = side[
-                        n, j, pl.ds(frame, cols + 2, stride=frames)
-                    ]
+                for ref, row in ((a_ref, 0), (b_ref, rows + 1)):
+                    wide[k, j, pl.ds(row * pitch + 8, cols)] = ref[frame, :, cut].astype(F32)
                 for r in range(rows):
                     wide[k, j, pl.ds((r + 1) * pitch + 8, cols)] = held[k, r, :, cut].astype(F32)
             for tap in range(taps):
@@ -153,7 +169,7 @@
         out_shape=[jax.ShapeDtypeStruct((rows * cols, channels), BF16)] * 2,
         scratch_shapes=[
             pltpu.VMEM((2, rows, cols, channels), BF16),
-            pltpu.VMEM((4, slabs, (cols + 2) * frames, lanes), F32),
+            pltpu.VMEM((2, slabs, (rows + 2) * frames, lanes), F32),
             pltpu.VMEM((2, slabs, (rows + 2) * pitch + 8, lanes), F32),
             pltpu.VMEM((2, rows * cols, taps * channels), BF16),
             pltpu.SemaphoreType.DMA((2,)),
@@ -161,7 +177,7 @@
         compiler_params=params(),
         cost_estimate=cost(2 * size * channels * taps, 4 * size),
         name="end_frames",
-    )(video, left, right, above, below, w_space)
+    )(video, above, below, left, right, w_space)
 
 
 def group_lanes(channels):
@@ -440,20 +456,16 @@
     frames, rows, cols, channels = video.shape
     parts = lax.axis_size("tm")
     me = lax.axis_index("tm").astype(jnp.int32).reshape(1)
-    left = shift(jnp.swapaxes(video[:, :, cols - 1], 0, 1), WIDTH, 1)
-    right = shift(jnp.swapaxes(video[:, :, 0], 0, 1), WIDTH, -1)
-    pixels = to_pixels(video)
-
-    def border(r):
-        return jnp.concatenate([left[r][None], pixels[r], right[r][None]], axis=0)
-
-    above = shift(border(rows - 1), "height", 1)
-    below = shift(border(0), "height", -1)
+    above = shift(video[:, rows - 1], "height", 1)
+    below = shift(video[:, 0], "height", -1)
+    first, last = extend_columns(*edge_columns(video), above, below)
+    left = shift(last, WIDTH, 1)
+    right = shift(first, WIDTH, -1)
     taps = w_space.reshape(9 * channels, channels)
-    early, late = end_frames(video, left, right, above, below, taps)
+    early, late = end_frames(video, above, below, left, right, taps)
     before = shift(late, "tm", 1)
     after = shift(early, "tm", -1)
-    spatial = spatial_conv(pixels, left, right, above, below, taps)
+    spatial = spatial_conv(video, above, below, left, right, taps)
     blocks, stats = temporal_conv(
         me, spatial.reshape(rows * cols, frames, channels), before, after, w_time
     )

time: 142 us -> 126 us (0.89)
  Pallas kernels: 43 us -> 23.4 us
  local copies, waits for them, and re-layouts: 7.3 us -> 3.89 us
  blocking collectives: 19.9 us -> 23.1 us
  starting transfers between devices: 32.3 us -> 34.6 us
  waiting for transfers between devices: 38.1 us -> 39.8 us
    pallas_call x2, Pallas kernels: 16.1 us -> 10.9 us  [attention(): pl.pallas_call(kernel, in_specs=[vmem] * (parts + len(rest)), out_specs=[...]
    pallas_call x1 -> x2, Pallas kernels: 3.98 us -> 0.29 us  [the longest x1 0.25 us: edge_columns(): pl.pallas_call(kernel, out_shape=[jax.ShapeDtypeStruct((rows, frames, cha...]
    all_to_all x1, blocking collectives: 19.9 us -> 23.1 us  [per_device(): stats = lax.all_to_all(shared, others, 0, 0)]
    pallas_call x1, Pallas kernels: 9.2 us -> 6.07 us  [spatial_conv(): pl.pallas_call(kernel, out_shape=jax.ShapeDtypeStruct((rows, cols, frames...]
    pallas_call x1, Pallas kernels: 4.07 us -> 1.18 us  [end_frames(): pl.pallas_call(kernel, in_specs=[anywhere] + [vmem] * 5, out_specs=[vmem]...]
    pallas_call x2, Pallas kernels: 4.49 us -> 2.12 us  [from_pixels(): pl.pallas_call(kernel, in_specs=[pl.BlockSpec(memory_space=pltpu.SMEM)] +...]
    pallas_call x1, Pallas kernels: 5.22 us -> 2.88 us  [temporal_conv(): pl.pallas_call(kernel, in_specs=[pl.BlockSpec(memory_space=pltpu.SMEM)] +...]
    slice x3 -> x0, local copies, waits for them, and re-layouts: 2.08 us -> none  [the longest x1 2.07 us: per_device(): right = shift(jnp.swapaxes(video[:, :, 0], 0, 1), WIDTH, -1)]
  transfers between devices with their start and end apart: 19 -> 19, of which waited for: 8 -> 9; matrix products, arithmetic and copies ran while one was open for 1% -> 0% of each run, Pallas kernels for 17% -> 10%
where the time goes in v4:
time: 126 us; the launch traced here: 125 us
  waiting for transfers between devices  39.8 us (32%)
  starting transfers between devices  34.6 us (27%)
  Pallas kernels  23.4 us (19%)
  blocking collectives  23.1 us (18%)
  local copies, waits for them, and re-layouts  3.89 us (3%)
    ppermute x12, waiting for transfers between devices, rotate(): lax.ppermute(value, 'tm', [(i, (i + step) % size) for i in range(size)])  34.4 us
    all_to_all x1, blocking collectives, per_device(): stats = lax.all_to_all(shared, others, 0, 0)  23.1 us
    ppermute x6, starting transfers between devices, shift(): return lax.ppermute(value, axis, pairs)  17.8 us
    ppermute x12, starting transfers between devices, rotate(): lax.ppermute(value, 'tm', [(i, (i + step) % size) for i in range(size)])  15.6 us
    pallas_call x2, Pallas kernels, attention(): pl.pallas_call(kernel, in_specs=[vmem] * (parts + len(rest)), out_specs=[...  10.9 us
    pallas_call x1, Pallas kernels, spatial_conv(): pl.pallas_call(kernel, out_shape=jax.ShapeDtypeStruct((rows, cols, frames...  6.07 us
    ppermute x6, waiting for transfers between devices, shift(): return lax.ppermute(value, axis, pairs)  4.6 us
    unnamed x16, local copies, waits for them, and re-layouts  2.89 us
  transfers between devices with their start and end apart: 19, of which 9 were waited for; matrix products, arithmetic and copies ran while one was open for 0% of the time, Pallas kernels for 10%

profile of v4, /device:TPU:1, one launch (start us, length us, event | category | flops | bytes accessed | tf_op | source)
XLA Modules:
  0.0 125.2 jit_solution(5888701461023724670)
XLA Ops:
  0.0 1.0 slice_bitcast_fusion
  1.0 1.3 %collective-permute-start.1 = (bf16[16,16,256]{2,1,0:T(8,128)(2,1)S(1)}, bf16[16,16,256]{2,1,0:T(8,128)(2,1)S(1)}, u32[]{:S(2)}, u32[]{:S(2)}) collective-permute-start(bf16[16,16,256]{2,1,0:T(8,128)(2,1)S(1)} %get-tuple-element.43), channel_id=1, source_target_pairs={{16,0},{32,16},{48,32},{17,1},{33,17},{49,33},{18,2},{34,18},{50,3... | collective-permute-start | bytes 393224 | tf_op jit(solution)/shard_map/ppermute | solution.py:33
  2.3 4.7 %collective-permute-start = (bf16[16,16,256]{2,1,0:T(8,128)(2,1)S(1)}, bf16[16,16,256]{2,1,0:T(8,128)(2,1)S(1)}, u32[]{:S(2)}, u32[]{:S(2)}) collective-permute-start(bf16[16,16,256]{2,1,0:T(8,128)(2,1)S(1)} %get-tuple-element.44), channel_id=1, source_target_pairs={{0,16},{16,32},{32,48},{1,17},{17,33},{33,49},{2,18},{18,34},{34,5... | collective-permute-start | bytes 393224 | tf_op jit(solution)/shard_map/ppermute | solution.py:33
  7.0 0.0 copy-start
  7.0 1.6 %copy-done = bf16[16,16,16,256]{3,2,1,0:T(8,128)(2,1)S(1)} copy-done((bf16[16,16,16,256]{3,2,1,0:T(8,128)(2,1)S(1)}, bf16[16,16,16,256]{3,2,1,0:T(8,128)(2,1)}, u32[]{:S(2)}) %copy-start) | copy-done | bytes 2097176
  8.5 0.0 copy-start.1
  8.6 0.2 edge_columns.1
  8.8 0.0 collective-permute-done.1.b_ref
  8.8 0.1 collective-permute-done.a_ref
  8.9 5.4 %collective-permute-start.2 = (bf16[18,16,256]{2,1,0:T(8,128)(2,1)S(1)}, bf16[18,16,256]{2,1,0:T(8,128)(2,1)S(1)}, u32[]{:S(2)}, u32[]{:S(2)}) collective-permute-start(bf16[18,16,256]{2,1,0:T(8,128)(2,1)S(1)} %get-tuple-element.26), channel_id=1, source_target_pairs={{0,1},{1,2},{2,3},{3,4},{4,5},{5,6},{6,7},{7,8},{8,9},{9,10},{10,1... | collective-permute-start | bytes 442376 | tf_op jit(solution)/shard_map/ppermute | solution.py:33
  14.3 1.9 %collective-permute-start.3 = (bf16[18,16,256]{2,1,0:T(8,128)(2,1)S(1)}, bf16[18,16,256]{2,1,0:T(8,128)(2,1)S(1)}, u32[]{:S(2)}, u32[]{:S(2)}) collective-permute-start(bf16[18,16,256]{2,1,0:T(8,128)(2,1)S(1)} %get-tuple-element.27), channel_id=1, source_target_pairs={{1,0},{2,1},{3,2},{4,3},{5,4},{6,5},{7,6},{8,7},{9,8},{10,9},{11,1... | collective-permute-start | bytes 442376 | tf_op jit(solution)/shard_map/ppermute | solution.py:33
  16.3 0.1 collective-permute-done.2.l_ref
  16.4 4.4 %collective-permute-done.3.r_ref = bf16[18,16,256]{2,1,0:T(8,128)(2,1)S(1)} collective-permute-done((bf16[18,16,256]{2,1,0:T(8,128)(2,1)S(1)}, bf16[18,16,256]{2,1,0:T(8,128)(2,1)S(1)}, u32[]{:S(2)}, u32[]{:S(2)}) %collective-permute-start.3) | collective-permute-done | bytes 147488 | tf_op jit(solution)/shard_map/ppermute | solution.py:33
  20.8 0.0 copy-done.1
  20.8 0.0 copy-start.2
  20.8 1.3 %copy-done.2 = bf16[3,3,256,256]{3,2,1,0:T(8,128)(2,1)S(1)} copy-done((bf16[3,3,256,256]{3,2,1,0:T(8,128)(2,1)S(1)}, bf16[3,3,256,256]{3,2,1,0:T(8,128)(2,1)}, u32[]{:S(2)}) %copy-start.2) | copy-done | bytes 1179672
  22.1 1.2 end_frames.1
  23.3 3.1 %collective-permute-start.4 = (bf16[256,256]{1,0:T(8,128)(2,1)S(1)}, bf16[256,256]{1,0:T(8,128)(2,1)S(1)}, u32[]{:S(2)}, u32[]{:S(2)}) collective-permute-start(bf16[256,256]{1,0:T(8,128)(2,1)S(1)} %get-tuple-element.28), channel_id=1, source_target_pairs={{0,64},{64,128},{128,192},{1,65},{65,129},{129,193},{2,66},{66,130... | collective-permute-start | bytes 393224 | tf_op jit(solution)/shard_map/ppermute | solution.py:33
  26.4 0.0 copy-start.3
  26.4 1.4 %collective-permute-start.5 = (bf16[256,256]{1,0:T(8,128)(2,1)S(1)}, bf16[256,256]{1,0:T(8,128)(2,1)S(1)}, u32[]{:S(2)}, u32[]{:S(2)}) collective-permute-start(bf16[256,256]{1,0:T(8,128)(2,1)S(1)} %get-tuple-element.29), channel_id=1, source_target_pairs={{64,0},{128,64},{192,128},{65,1},{129,65},{193,129},{66,2},{130,66... | collective-permute-start | bytes 393224 | tf_op jit(solution)/shard_map/ppermute | solution.py:33
  27.8 6.1 %spatial_conv.1 = bf16[16,16,16,256]{3,2,1,0:T(8,128)(2,1)S(1)} custom-call(bf16[16,16,16,256]{3,2,1,0:T(8,128)(2,1)S(1)} %copy-done.1, bf16[16,16,256]{2,1,0:T(8,128)(2,1)S(1)} %collective-permute-done.a_ref, bf16[16,16,256]{2,1,0:T(8,128)(2,1)S(1)} %collective-permute-done.1.b_ref, bf16[18,16,256]{2,1,0:T(8,128)(2,1)S(1)} %collective-permute-done.2.l_ref, ...), custom_call_target="tpu_custom_call" | custom-call | flops 4831838208 | bytes 4194304 | tf_op jit(solution)/shard_map/spatial_conv/pallas_call | solution.py:106
  33.9 0.0 collective-permute-done.4.b_ref
  33.9 0.0 collective-permute-done.5.a_ref
  33.9 0.0 copy-done.3
  33.9 0.0 copy-start.4
  33.9 0.0 copy-start.5
  34.0 0.0 copy-start.6
  34.0 0.0 copy-start.7
  34.0 2.9 %temporal_conv.1 = (bf16[64,16,256]{2,1,0:T(8,128)(2,1)S(1)}, bf16[64,16,256]{2,1,0:T(8,128)(2,1)S(1)}, bf16[64,16,256]{2,1,0:T(8,128)(2,1)S(1)}, bf16[64,16,256]{2,1,0:T(8,128)(2,1)S(1)}, f32[8,128]{1,0:T(8,128)S(1)}) custom-call(s32[1]{0:T(128)} %bitcast.me_ref, bf16[256,16,256]{2,1,0:T(8,128)(2,1)S(1)} %bitcast.21, ...), custom_call_target="tpu_custom_call" | custom-call | flops 1610612736 | bytes 4194304 | tf_op jit(solution)/shard_map/temporal_conv/pallas_call | solution.py:264
  36.9 2.2 %collective-permute-start.6 = (bf16[64,16,256]{2,1,0:T(8,128)(2,1)S(1)}, bf16[64,16,256]{2,1,0:T(8,128)(2,1)S(1)}, u32[]{:S(2)}, u32[]{:S(2)}) collective-permute-start(bf16[64,16,256]{2,1,0:T(8,128)(2,1)S(1)} %get-tuple-element.31), channel_id=1, source_target_pairs={{0,64},{64,128},{128,192},{192,0},{1,65},{65,129},{129,193},{193,1... | collective-permute-start | bytes 1572872 | tf_op jit(solution)/shard_map/ppermute | solution.py:452
  39.0 2.5 %collective-permute-start.7 = (bf16[64,16,256]{2,1,0:T(8,128)(2,1)S(1)}, bf16[64,16,256]{2,1,0:T(8,128)(2,1)S(1)}, u32[]{:S(2)}, u32[]{:S(2)}) collective-permute-start(bf16[64,16,256]{2,1,0:T(8,128)(2,1)S(1)} %get-tuple-element.32), channel_id=1, source_target_pairs={{0,128},{64,192},{128,0},{192,64},{1,129},{65,193},{129,1},{193,65... | collective-permute-start | bytes 1572872 | tf_op jit(solution)/shard_map/ppermute | solution.py:452
  41.5 1.1 collective-permute-start.8
  42.6 0.0 collective-permute-start.11
  42.6 2.1 %collective-permute-start.10 = (f32[8,128]{1,0:T(8,128)S(1)}, f32[8,128]{1,0:T(8,128)S(1)}, u32[]{:S(2)}, u32[]{:S(2)}) collective-permute-start(f32[8,128]{1,0:T(8,128)S(1)} %get-tuple-element.34), channel_id=1, source_target_pairs={{0,128},{64,192},{128,0},{192,64},{1,129},{65,193},{129,1},{193,65... | collective-permute-start | bytes 12296 | tf_op jit(solution)/shard_map/ppermute | solution.py:452
  44.7 17.7 %collective-permute-done.11 = f32[8,128]{1,0:T(8,128)S(1)} collective-permute-done((f32[8,128]{1,0:T(8,128)S(1)}, f32[8,128]{1,0:T(8,128)S(1)}, u32[]{:S(2)}, u32[]{:S(2)}) %collective-permute-start.11) | collective-permute-done | bytes 4128 | tf_op jit(solution)/shard_map/ppermute | solution.py:452
  62.4 1.7 %collective-permute-start.9 = (f32[8,128]{1,0:T(8,128)S(1)}, f32[8,128]{1,0:T(8,128)S(1)}, u32[]{:S(2)}, u32[]{:S(2)}) collective-permute-start(f32[8,128]{1,0:T(8,128)S(1)} %get-tuple-element.34), channel_id=1, source_target_pairs={{0,64},{64,128},{128,192},{192,0},{1,65},{65,129},{129,193},{193,1... | collective-permute-start | bytes 12296 | tf_op jit(solution)/shard_map/ppermute | solution.py:452
  64.1 0.0 collective-permute-done.10
  64.1 2.0 %collective-permute-done.9 = f32[8,128]{1,0:T(8,128)S(1)} collective-permute-done((f32[8,128]{1,0:T(8,128)S(1)}, f32[8,128]{1,0:T(8,128)S(1)}, u32[]{:S(2)}, u32[]{:S(2)}) %collective-permute-start.9) | collective-permute-done | bytes 4128 | tf_op jit(solution)/shard_map/ppermute | solution.py:452
  66.1 1.1 collective-permute-start.12
  67.2 0.8 collective-permute-done.12
  68.0 23.1 %all_to_all.5.refs_4_ = f32[32,8,128]{2,1,0:T(8,128)S(1)} all-to-all(f32[32,8,128]{2,1,0:T(8,128)S(1)} %broadcast_in_dim.2), channel_id=1, replica_groups=mesh['tm'=4,'height'=4,'width_0'=8,'width_1'=2] {'height','width_0'}, dimensions={0} | all-to-all | bytes 262144 | tf_op jit(solution)/shard_map/all_to_all | solution.py:480
  91.2 0.0 collective-permute-done.6.refs_1_
  91.2 0.0 collective-permute-done.7.refs_2_
  91.2 0.0 collective-permute-done.8.refs_3_
  91.2 0.0 copy-done.4
  91.2 0.0 copy-done.5
  91.2 0.0 copy-done.6
  91.2 0.0 copy-done.7
  91.2 5.4 %attention.3 = (bf16[32,16,256]{2,1,0:T(8,128)(2,1)S(1)}, bf16[32,16,256]{2,1,0:T(8,128)(2,1)S(1)}, bf16[32,16,256]{2,1,0:T(8,128)(2,1)S(1)}, bf16[32,16,256]{2,1,0:T(8,128)(2,1)S(1)}) custom-call(bf16[64,16,256]{2,1,0:T(8,128)(2,1)S(1)} %get-tuple-element.30.refs_0_, bf16[64,16,256]{2,1,0:T(8,128)(2,1)S(1)} %collective-permute-done.6.refs_1_, ...), custom_call_target="tpu_custom_call" | custom-call | flops 2147483648 | bytes 2097152 | tf_op jit(solution)/shard_map/attention/pallas_call | solution.py:394
  96.7 1.2 collective-permute-start.16
  97.9 0.9 collective-permute-start.17
  98.8 0.5 collective-permute-start.18
  99.2 5.4 %attention.2 = (bf16[32,16,256]{2,1,0:T(8,128)(2,1)S(1)}, bf16[32,16,256]{2,1,0:T(8,128)(2,1)S(1)}, bf16[32,16,256]{2,1,0:T(8,128)(2,1)S(1)}, bf16[32,16,256]{2,1,0:T(8,128)(2,1)S(1)}) custom-call(bf16[64,16,256]{2,1,0:T(8,128)(2,1)S(1)} %get-tuple-element.30.refs_0_, bf16[64,16,256]{2,1,0:T(8,128)(2,1)S(1)} %collective-permute-done.6.refs_1_, ...), custom_call_target="tpu_custom_call" | custom-call | flops 2147483648 | bytes 2097152 | tf_op jit(solution)/shard_map/attention/pallas_call | solution.py:394
  104.7 2.3 %collective-permute-start.13 = (bf16[32,16,256]{2,1,0:T(8,128)(2,1)S(1)}, bf16[32,16,256]{2,1,0:T(8,128)(2,1)S(1)}, u32[]{:S(2)}, u32[]{:S(2)}) collective-permute-start(bf16[32,16,256]{2,1,0:T(8,128)(2,1)S(1)} %get-tuple-element.35), channel_id=1, source_target_pairs={{0,192},{64,0},{128,64},{192,128},{1,193},{65,1},{129,65},{193,129... | collective-permute-start | bytes 786440 | tf_op jit(solution)/shard_map/ppermute | solution.py:452
  107.0 0.9 collective-permute-start.14
  107.9 0.0 collective-permute-done.16.refs_2_
  107.9 0.3 collective-permute-start.15
  108.2 0.0 collective-permute-done.17.refs_3_
  108.2 6.4 %collective-permute-done.18.refs_4_ = bf16[32,16,256]{2,1,0:T(8,128)(2,1)S(1)} collective-permute-done((bf16[32,16,256]{2,1,0:T(8,128)(2,1)S(1)}, bf16[32,16,256]{2,1,0:T(8,128)(2,1)S(1)}, u32[]{:S(2)}, u32[]{:S(2)}) %collective-permute-start.18) | collective-permute-done | bytes 262176 | tf_op jit(solution)/shard_map/ppermute | solution.py:452
  114.6 1.2 from_pixels.2.refs_3_
  115.7 0.0 collective-permute-done.13.refs_0_
  115.8 1.0 collective-permute-done.14.refs_1_
  116.8 7.3 %collective-permute-done.15.refs_2_ = bf16[32,16,256]{2,1,0:T(8,128)(2,1)S(1)} collective-permute-done((bf16[32,16,256]{2,1,0:T(8,128)(2,1)S(1)}, bf16[32,16,256]{2,1,0:T(8,128)(2,1)S(1)}, u32[]{:S(2)}, u32[]{:S(2)}) %collective-permute-start.15) | collective-permute-done | bytes 262176 | tf_op jit(solution)/shard_map/ppermute | solution.py:452
  124.1 1.0 from_pixels.3
  (4 shorter events, 0.1 us)
Async XLA Ops:
  1.0 7.8 %collective-permute-start.1 = (bf16[16,16,256]{2,1,0:T(8,128)(2,1)S(1)}, bf16[16,16,256]{2,1,0:T(8,128)(2,1)S(1)}, u32[]{:S(2)}, u32[]{:S(2)}) collective-permute-start(bf16[16,16,256]{2,1,0:T(8,128)(2,1)S(1)} %get-tuple-element.43), channel_id=1, source_target_pairs={{16,0},{32,16},{48,32},{17,1},{33,17},{49,33},{18,2},{34,18},{50,3... | collective-permute-start | bytes 393224 | tf_op jit(solution)/shard_map/ppermute | solution.py:33
  2.3 6.6 %collective-permute-start = (bf16[16,16,256]{2,1,0:T(8,128)(2,1)S(1)}, bf16[16,16,256]{2,1,0:T(8,128)(2,1)S(1)}, u32[]{:S(2)}, u32[]{:S(2)}) collective-permute-start(bf16[16,16,256]{2,1,0:T(8,128)(2,1)S(1)} %get-tuple-element.44), channel_id=1, source_target_pairs={{0,16},{16,32},{32,48},{1,17},{17,33},{33,49},{2,18},{18,34},{34,5... | collective-permute-start | bytes 393224 | tf_op jit(solution)/shard_map/ppermute | solution.py:33
  7.0 1.6 %copy-start = (bf16[16,16,16,256]{3,2,1,0:T(8,128)(2,1)S(1)}, bf16[16,16,16,256]{3,2,1,0:T(8,128)(2,1)}, u32[]{:S(2)}) copy-start(bf16[16,16,16,256]{3,2,1,0:T(8,128)(2,1)} %v_ref.5) | copy-start | bytes 6291460
  8.5 12.2 %copy-start.1 = (bf16[16,16,16,256]{3,2,1,0:T(8,128)(2,1)S(1)}, bf16[16,16,16,256]{3,2,1,0:T(8,128)(2,1)}, u32[]{:S(2)}) copy-start(bf16[16,16,16,256]{3,2,1,0:T(8,128)(2,1)} %v_ref.5) | copy-start | bytes 6291460
  8.9 7.5 %collective-permute-start.2 = (bf16[18,16,256]{2,1,0:T(8,128)(2,1)S(1)}, bf16[18,16,256]{2,1,0:T(8,128)(2,1)S(1)}, u32[]{:S(2)}, u32[]{:S(2)}) collective-permute-start(bf16[18,16,256]{2,1,0:T(8,128)(2,1)S(1)} %get-tuple-element.26), channel_id=1, source_target_pairs={{0,1},{1,2},{2,3},{3,4},{4,5},{5,6},{6,7},{7,8},{8,9},{9,10},{10,1... | collective-permute-start | bytes 442376 | tf_op jit(solution)/shard_map/ppermute | solution.py:33
  14.3 6.5 %collective-permute-start.3 = (bf16[18,16,256]{2,1,0:T(8,128)(2,1)S(1)}, bf16[18,16,256]{2,1,0:T(8,128)(2,1)S(1)}, u32[]{:S(2)}, u32[]{:S(2)}) collective-permute-start(bf16[18,16,256]{2,1,0:T(8,128)(2,1)S(1)} %get-tuple-element.27), channel_id=1, source_target_pairs={{1,0},{2,1},{3,2},{4,3},{5,4},{6,5},{7,6},{8,7},{9,8},{10,9},{11,1... | collective-permute-start | bytes 442376 | tf_op jit(solution)/shard_map/ppermute | solution.py:33
  20.8 1.3 %copy-start.2 = (bf16[3,3,256,256]{3,2,1,0:T(8,128)(2,1)S(1)}, bf16[3,3,256,256]{3,2,1,0:T(8,128)(2,1)}, u32[]{:S(2)}) copy-start(bf16[3,3,256,256]{3,2,1,0:T(8,128)(2,1)} %param.8) | copy-start | bytes 3538948
  23.3 10.6 %collective-permute-start.4 = (bf16[256,256]{1,0:T(8,128)(2,1)S(1)}, bf16[256,256]{1,0:T(8,128)(2,1)S(1)}, u32[]{:S(2)}, u32[]{:S(2)}) collective-permute-start(bf16[256,256]{1,0:T(8,128)(2,1)S(1)} %get-tuple-element.28), channel_id=1, source_target_pairs={{0,64},{64,128},{128,192},{1,65},{65,129},{129,193},{2,66},{66,130... | collective-permute-start | bytes 393224 | tf_op jit(solution)/shard_map/ppermute | solution.py:33
  26.4 7.5 %copy-start.3 = (bf16[3,256,256]{2,1,0:T(8,128)(2,1)S(1)}, bf16[3,256,256]{2,1,0:T(8,128)(2,1)}, u32[]{:S(2)}) copy-start(bf16[3,256,256]{2,1,0:T(8,128)(2,1)} %param.9) | copy-start | bytes 1179652
  26.4 7.5 %collective-permute-start.5 = (bf16[256,256]{1,0:T(8,128)(2,1)S(1)}, bf16[256,256]{1,0:T(8,128)(2,1)S(1)}, u32[]{:S(2)}, u32[]{:S(2)}) collective-permute-start(bf16[256,256]{1,0:T(8,128)(2,1)S(1)} %get-tuple-element.29), channel_id=1, source_target_pairs={{64,0},{128,64},{192,128},{65,1},{129,65},{193,129},{66,2},{130,66... | collective-permute-start | bytes 393224 | tf_op jit(solution)/shard_map/ppermute | solution.py:33
  33.9 57.3 %copy-start.4 = (bf16[256,768]{1,0:T(8,128)(2,1)S(1)}, bf16[256,768]{1,0:T(8,128)(2,1)}, u32[]{:S(2)}) copy-start(bf16[256,768]{1,0:T(8,128)(2,1)} %refs_7_.3) | copy-start | bytes 1179652
  33.9 57.3 %copy-start.5 = (bf16[256,256]{1,0:T(8,128)(2,1)S(1)}, bf16[256,256]{1,0:T(8,128)(2,1)}, u32[]{:S(2)}) copy-start(bf16[256,256]{1,0:T(8,128)(2,1)} %refs_8_.3) | copy-start | bytes 393220
  34.0 57.2 %copy-start.6 = (f32[256]{0:T(256)S(1)}, f32[256]{0:T(256)}, u32[]{:S(2)}) copy-start(f32[256]{0:T(256)} %param.10) | copy-start | bytes 3076
  34.0 57.2 %copy-start.7 = (f32[256]{0:T(256)S(1)}, f32[256]{0:T(256)}, u32[]{:S(2)}) copy-start(f32[256]{0:T(256)} %param.11) | copy-start | bytes 3076
  36.9 54.3 %collective-permute-start.6 = (bf16[64,16,256]{2,1,0:T(8,128)(2,1)S(1)}, bf16[64,16,256]{2,1,0:T(8,128)(2,1)S(1)}, u32[]{:S(2)}, u32[]{:S(2)}) collective-permute-start(bf16[64,16,256]{2,1,0:T(8,128)(2,1)S(1)} %get-tuple-element.31), channel_id=1, source_target_pairs={{0,64},{64,128},{128,192},{192,0},{1,65},{65,129},{129,193},{193,1... | collective-permute-start | bytes 1572872 | tf_op jit(solution)/shard_map/ppermute | solution.py:452
  39.0 52.2 %collective-permute-start.7 = (bf16[64,16,256]{2,1,0:T(8,128)(2,1)S(1)}, bf16[64,16,256]{2,1,0:T(8,128)(2,1)S(1)}, u32[]{:S(2)}, u32[]{:S(2)}) collective-permute-start(bf16[64,16,256]{2,1,0:T(8,128)(2,1)S(1)} %get-tuple-element.32), channel_id=1, source_target_pairs={{0,128},{64,192},{128,0},{192,64},{1,129},{65,193},{129,1},{193,65... | collective-permute-start | bytes 1572872 | tf_op jit(solution)/shard_map/ppermute | solution.py:452
  41.5 49.7 %collective-permute-start.8 = (bf16[64,16,256]{2,1,0:T(8,128)(2,1)S(1)}, bf16[64,16,256]{2,1,0:T(8,128)(2,1)S(1)}, u32[]{:S(2)}, u32[]{:S(2)}) collective-permute-start(bf16[64,16,256]{2,1,0:T(8,128)(2,1)S(1)} %get-tuple-element.33), channel_id=1, source_target_pairs={{0,192},{64,0},{128,64},{192,128},{1,193},{65,1},{129,65},{193,129... | collective-permute-start | bytes 1572872 | tf_op jit(solution)/shard_map/ppermute | solution.py:452
  42.6 19.8 %collective-permute-start.11 = (f32[8,128]{1,0:T(8,128)S(1)}, f32[8,128]{1,0:T(8,128)S(1)}, u32[]{:S(2)}, u32[]{:S(2)}) collective-permute-start(f32[8,128]{1,0:T(8,128)S(1)} %get-tuple-element.34), channel_id=1, source_target_pairs={{0,192},{64,0},{128,64},{192,128},{1,193},{65,1},{129,65},{193,129... | collective-permute-start | bytes 12296 | tf_op jit(solution)/shard_map/ppermute | solution.py:452
  42.6 21.5 %collective-permute-start.10 = (f32[8,128]{1,0:T(8,128)S(1)}, f32[8,128]{1,0:T(8,128)S(1)}, u32[]{:S(2)}, u32[]{:S(2)}) collective-permute-start(f32[8,128]{1,0:T(8,128)S(1)} %get-tuple-element.34), channel_id=1, source_target_pairs={{0,128},{64,192},{128,0},{192,64},{1,129},{65,193},{129,1},{193,65... | collective-permute-start | bytes 12296 | tf_op jit(solution)/shard_map/ppermute | solution.py:452
  62.4 3.7 %collective-permute-start.9 = (f32[8,128]{1,0:T(8,128)S(1)}, f32[8,128]{1,0:T(8,128)S(1)}, u32[]{:S(2)}, u32[]{:S(2)}) collective-permute-start(f32[8,128]{1,0:T(8,128)S(1)} %get-tuple-element.34), channel_id=1, source_target_pairs={{0,64},{64,128},{128,192},{192,0},{1,65},{65,129},{129,193},{193,1... | collective-permute-start | bytes 12296 | tf_op jit(solution)/shard_map/ppermute | solution.py:452
  66.1 2.0 %collective-permute-start.12 = (f32[8,128]{1,0:T(8,128)S(1)}, f32[8,128]{1,0:T(8,128)S(1)}, u32[]{:S(2)}, u32[]{:S(2)}) collective-permute-start(f32[8,128]{1,0:T(8,128)S(1)} %add_add_fusion), channel_id=1, source_target_pairs={{0,1},{1,0},{2,3},{3,2},{4,5},{5,4},{6,7},{7,6},{8,9},{9,8},{10,11... | collective-permute-start | bytes 12296 | tf_op jit(solution)/shard_map/ppermute | solution.py:476
  96.7 11.2 %collective-permute-start.16 = (bf16[32,16,256]{2,1,0:T(8,128)(2,1)S(1)}, bf16[32,16,256]{2,1,0:T(8,128)(2,1)S(1)}, u32[]{:S(2)}, u32[]{:S(2)}) collective-permute-start(bf16[32,16,256]{2,1,0:T(8,128)(2,1)S(1)} %get-tuple-element.40), channel_id=1, source_target_pairs={{0,192},{64,0},{128,64},{192,128},{1,193},{65,1},{129,65},{193,129... | collective-permute-start | bytes 786440 | tf_op jit(solution)/shard_map/ppermute | solution.py:452
  97.9 10.3 %collective-permute-start.17 = (bf16[32,16,256]{2,1,0:T(8,128)(2,1)S(1)}, bf16[32,16,256]{2,1,0:T(8,128)(2,1)S(1)}, u32[]{:S(2)}, u32[]{:S(2)}) collective-permute-start(bf16[32,16,256]{2,1,0:T(8,128)(2,1)S(1)} %get-tuple-element.41), channel_id=1, source_target_pairs={{0,128},{64,192},{128,0},{192,64},{1,129},{65,193},{129,1},{193,65... | collective-permute-start | bytes 786440 | tf_op jit(solution)/shard_map/ppermute | solution.py:452
  98.8 15.8 %collective-permute-start.18 = (bf16[32,16,256]{2,1,0:T(8,128)(2,1)S(1)}, bf16[32,16,256]{2,1,0:T(8,128)(2,1)S(1)}, u32[]{:S(2)}, u32[]{:S(2)}) collective-permute-start(bf16[32,16,256]{2,1,0:T(8,128)(2,1)S(1)} %get-tuple-element.42), channel_id=1, source_target_pairs={{0,64},{64,128},{128,192},{192,0},{1,65},{65,129},{129,193},{193,1... | collective-permute-start | bytes 786440 | tf_op jit(solution)/shard_map/ppermute | solution.py:452
  104.7 11.1 %collective-permute-start.13 = (bf16[32,16,256]{2,1,0:T(8,128)(2,1)S(1)}, bf16[32,16,256]{2,1,0:T(8,128)(2,1)S(1)}, u32[]{:S(2)}, u32[]{:S(2)}) collective-permute-start(bf16[32,16,256]{2,1,0:T(8,128)(2,1)S(1)} %get-tuple-element.35), channel_id=1, source_target_pairs={{0,192},{64,0},{128,64},{192,128},{1,193},{65,1},{129,65},{193,129... | collective-permute-start | bytes 786440 | tf_op jit(solution)/shard_map/ppermute | solution.py:452
  107.0 9.8 %collective-permute-start.14 = (bf16[32,16,256]{2,1,0:T(8,128)(2,1)S(1)}, bf16[32,16,256]{2,1,0:T(8,128)(2,1)S(1)}, u32[]{:S(2)}, u32[]{:S(2)}) collective-permute-start(bf16[32,16,256]{2,1,0:T(8,128)(2,1)S(1)} %get-tuple-element.36), channel_id=1, source_target_pairs={{0,128},{64,192},{128,0},{192,64},{1,129},{65,193},{129,1},{193,65... | collective-permute-start | bytes 786440 | tf_op jit(solution)/shard_map/ppermute | solution.py:452
  107.9 16.2 %collective-permute-start.15 = (bf16[32,16,256]{2,1,0:T(8,128)(2,1)S(1)}, bf16[32,16,256]{2,1,0:T(8,128)(2,1)S(1)}, u32[]{:S(2)}, u32[]{:S(2)}) collective-permute-start(bf16[32,16,256]{2,1,0:T(8,128)(2,1)S(1)} %get-tuple-element.37), channel_id=1, source_target_pairs={{0,64},{64,128},{128,192},{192,0},{1,65},{65,129},{129,193},{193,1... | collective-permute-start | bytes 786440 | tf_op jit(solution)/shard_map/ppermute | solution.py:452

commit v5 on v4

--- a/solution.py
+++ b/solution.py
@@ -120,6 +120,7 @@
     pitch = cols + 8
     taps = 9
     ends = (0, frames - 1)
+    whole_rows = -(-(rows + 2) // 8) * 8
 
     def kernel(v_ref, a_ref, b_ref, l_ref, r_ref, w_ref, early_ref, late_ref, held, side, wide, window, sem):
         fetch = [
@@ -132,7 +133,7 @@
             cut = slice(j * lanes, (j + 1) * lanes)
             for n, ref in enumerate((l_ref, r_ref)):
                 size = (rows + 2) * frames
-                side[n, j] = ref[...].reshape(size, channels)[:, cut].astype(F32)
+                side[n, j, pl.ds(0, size)] = ref[...].reshape(size, channels)[:, cut].astype(F32)
         for copy in fetch:
             copy.wait()
         outs = (early_ref, late_ref)
@@ -169,8 +170,8 @@
         out_shape=[jax.ShapeDtypeStruct((rows * cols, channels), BF16)] * 2,
         scratch_shapes=[
             pltpu.VMEM((2, rows, cols, channels), BF16),
-            pltpu.VMEM((2, slabs, (rows + 2) * frames, lanes), F32),
-            pltpu.VMEM((2, slabs, (rows + 2) * pitch + 8, lanes), F32),
+            pltpu.VMEM((2, slabs, whole_rows * frames, lanes), F32),
+            pltpu.VMEM((2, slabs, (whole_rows + 1) * pitch, lanes), F32),
             pltpu.VMEM((2, rows * cols, taps * channels), BF16),
             pltpu.SemaphoreType.DMA((2,)),
         ],
@@ -180,11 +181,11 @@
     )(video, above, below, left, right, w_space)
 
 
-def group_lanes(channels):
+def group_lanes(channels, first):
     shape = (channels, 128)
     channel = lax.broadcasted_iota(jnp.int32, shape, 0)
     lane = lax.broadcasted_iota(jnp.int32, shape, 1)
-    return (channel // (channels // GROUPS) == lane).astype(F32)
+    return (channel // (channels // GROUPS) + first == lane).astype(F32)
 
 
 def temporal_conv(me, spatial, before, after, w_time):
@@ -251,13 +252,17 @@
                 prepare(t + 1)
             if t > 0:
                 sums = finish(t - 1, sums)
-        folded = [jnp.sum(v, axis=0, keepdims=True) for v in sums] + [jnp.zeros((6, channels), F32)]
-        stats_ref[...] = jnp.dot(
-            jnp.concatenate(folded, axis=0),
-            group_lanes(channels),
-            precision=lax.Precision.HIGHEST,
-            preferred_element_type=F32,
-        )
+        spread = [
+            jnp.dot(
+                value,
+                group_lanes(channels, k * GROUPS),
+                precision=lax.Precision.HIGHEST,
+                preferred_element_type=F32,
+            )
+            for k, value in enumerate(sums)
+        ]
+        row = jnp.sum(spread[0] + spread[1], axis=0, keepdims=True)
+        stats_ref[...] = jnp.broadcast_to(row, (8, 128))
 
     vmem = pl.BlockSpec(memory_space=pltpu.VMEM)
     size = pixels * frames * channels
@@ -293,15 +298,19 @@
         stats_ref, gain_ref, bias_ref, qkv_ref, out_w_ref = refs[:5]
         outs, refs = refs[5 : 5 + parts], refs[5 + parts :]
         normed, projected, contexts, affine = refs[:2], refs[2:4], refs[4], refs[5]
-        spread = lax.dot_general(
-            jnp.sum(stats_ref[...], axis=0),
-            group_lanes(channels),
-            (((1,), (1,)), ((), ())),
-            precision=lax.Precision.HIGHEST,
-            preferred_element_type=F32,
-        )
-        mean = spread[0:1] / cell_count
-        var = jnp.maximum(spread[1:2] / cell_count - mean * mean, 0.0)
+        total = jnp.sum(stats_ref[...], axis=0)
+        sums, squares = [
+            lax.dot_general(
+                total,
+                group_lanes(channels, k * GROUPS),
+                (((1,), (1,)), ((), ())),
+                precision=lax.Precision.HIGHEST,
+                preferred_element_type=F32,
+            )[0:1]
+            for k in range(2)
+        ]
+        mean = sums / cell_count
+        var = jnp.maximum(squares / cell_count - mean * mean, 0.0)
         scale = 0.5 * lax.rsqrt(var + 1e-05) * gain_ref[...]
         affine[0:8] = jnp.broadcast_to(scale, (8, channels))
         affine[8:16] = jnp.broadcast_to(0.5 * bias_ref[...] - mean * scale, (8, channels))
@@ -458,10 +467,10 @@
     me = lax.axis_index("tm").astype(jnp.int32).reshape(1)
     above = shift(video[:, rows - 1], "height", 1)
     below = shift(video[:, 0], "height", -1)
+    taps = w_space.reshape(9 * channels, channels)
     first, last = extend_columns(*edge_columns(video), above, below)
     left = shift(last, WIDTH, 1)
     right = shift(first, WIDTH, -1)
-    taps = w_space.reshape(9 * channels, channels)
     early, late = end_frames(video, above, below, left, right, taps)
     before = shift(late, "tm", 1)
     after = shift(early, "tm", -1)
@@ -488,7 +497,9 @@
     for h in range(2):
         results = attention(moved, stats, *weights, cell_count, h * share, share)
         own.append(results[0])
-        far.append([rotate(results[d], -d) for d in range(1, parts)])
+        far.append([])
+        for d in range(1, parts):
+            far[h].append(rotate(results[d], -d))
     moves = [(0, 0), (0, 1)] + [(d, 0) for d in range(1, parts)]
     result = from_pixels(me, own + far[0], moves, video.shape)
     return from_pixels(me, far[1], [(d, 1) for d in range(1, parts)], video.shape, result)

time: 126 us -> 126 us (level)
  no operation moved by 1% of the time
where the time goes in v5:
time: 126 us; the launch traced here: 125 us
  waiting for transfers between devices  39.8 us (32%)
  starting transfers between devices  34.6 us (27%)
  Pallas kernels  23.5 us (19%)
  blocking collectives  23.1 us (18%)
  local copies, waits for them, and re-layouts  3.89 us (3%)
    ppermute x12, waiting for transfers between devices, rotate(): lax.ppermute(value, 'tm', [(i, (i + step) % size) for i in range(size)])  34.4 us
    all_to_all x1, blocking collectives, per_device(): stats = lax.all_to_all(shared, others, 0, 0)  23.1 us
    ppermute x6, starting transfers between devices, shift(): return lax.ppermute(value, axis, pairs)  17.8 us
    ppermute x12, starting transfers between devices, rotate(): lax.ppermute(value, 'tm', [(i, (i + step) % size) for i in range(size)])  15.6 us
    pallas_call x2, Pallas kernels, attention(): pl.pallas_call(kernel, in_specs=[vmem] * (parts + len(rest)), out_specs=[...  10.9 us
    pallas_call x1, Pallas kernels, spatial_conv(): pl.pallas_call(kernel, out_shape=jax.ShapeDtypeStruct((rows, cols, frames...  6.07 us
    ppermute x6, waiting for transfers between devices, shift(): return lax.ppermute(value, axis, pairs)  4.6 us
    pallas_call x1, Pallas kernels, temporal_conv(): pl.pallas_call(kernel, in_specs=[pl.BlockSpec(memory_space=pltpu.SMEM)] +...  2.96 us
  transfers between devices with their start and end apart: 19, of which 9 were waited for; matrix products, arithmetic and copies ran while one was open for 0% of the time, Pallas kernels for 10%

profile of v5, /device:TPU:1, one launch (start us, length us, event | category | flops | bytes accessed | tf_op | source)
XLA Modules:
  0.0 125.3 jit_solution(15913774301908313867)
XLA Ops:
  0.0 1.0 slice_bitcast_fusion
  1.0 1.3 %collective-permute-start.1 = (bf16[16,16,256]{2,1,0:T(8,128)(2,1)S(1)}, bf16[16,16,256]{2,1,0:T(8,128)(2,1)S(1)}, u32[]{:S(2)}, u32[]{:S(2)}) collective-permute-start(bf16[16,16,256]{2,1,0:T(8,128)(2,1)S(1)} %get-tuple-element.43), channel_id=1, source_target_pairs={{16,0},{32,16},{48,32},{17,1},{33,17},{49,33},{18,2},{34,18},{50,3... | collective-permute-start | bytes 393224 | tf_op jit(solution)/shard_map/ppermute | solution.py:33
  2.3 4.7 %collective-permute-start = (bf16[16,16,256]{2,1,0:T(8,128)(2,1)S(1)}, bf16[16,16,256]{2,1,0:T(8,128)(2,1)S(1)}, u32[]{:S(2)}, u32[]{:S(2)}) collective-permute-start(bf16[16,16,256]{2,1,0:T(8,128)(2,1)S(1)} %get-tuple-element.44), channel_id=1, source_target_pairs={{0,16},{16,32},{32,48},{1,17},{17,33},{33,49},{2,18},{18,34},{34,5... | collective-permute-start | bytes 393224 | tf_op jit(solution)/shard_map/ppermute | solution.py:33
  7.0 0.0 copy-start
  7.0 1.6 %copy-done = bf16[16,16,16,256]{3,2,1,0:T(8,128)(2,1)S(1)} copy-done((bf16[16,16,16,256]{3,2,1,0:T(8,128)(2,1)S(1)}, bf16[16,16,16,256]{3,2,1,0:T(8,128)(2,1)}, u32[]{:S(2)}) %copy-start) | copy-done | bytes 2097176
  8.5 0.0 copy-start.1
  8.6 0.2 edge_columns.1
  8.8 0.0 collective-permute-done.1.b_ref
  8.8 0.1 collective-permute-done.a_ref
  8.9 5.4 %collective-permute-start.2 = (bf16[18,16,256]{2,1,0:T(8,128)(2,1)S(1)}, bf16[18,16,256]{2,1,0:T(8,128)(2,1)S(1)}, u32[]{:S(2)}, u32[]{:S(2)}) collective-permute-start(bf16[18,16,256]{2,1,0:T(8,128)(2,1)S(1)} %get-tuple-element.26), channel_id=1, source_target_pairs={{0,1},{1,2},{2,3},{3,4},{4,5},{5,6},{6,7},{7,8},{8,9},{9,10},{10,1... | collective-permute-start | bytes 442376 | tf_op jit(solution)/shard_map/ppermute | solution.py:33
  14.3 1.9 %collective-permute-start.3 = (bf16[18,16,256]{2,1,0:T(8,128)(2,1)S(1)}, bf16[18,16,256]{2,1,0:T(8,128)(2,1)S(1)}, u32[]{:S(2)}, u32[]{:S(2)}) collective-permute-start(bf16[18,16,256]{2,1,0:T(8,128)(2,1)S(1)} %get-tuple-element.27), channel_id=1, source_target_pairs={{1,0},{2,1},{3,2},{4,3},{5,4},{6,5},{7,6},{8,7},{9,8},{10,9},{11,1... | collective-permute-start | bytes 442376 | tf_op jit(solution)/shard_map/ppermute | solution.py:33
  16.3 0.1 collective-permute-done.2.l_ref
  16.4 4.4 %collective-permute-done.3.r_ref = bf16[18,16,256]{2,1,0:T(8,128)(2,1)S(1)} collective-permute-done((bf16[18,16,256]{2,1,0:T(8,128)(2,1)S(1)}, bf16[18,16,256]{2,1,0:T(8,128)(2,1)S(1)}, u32[]{:S(2)}, u32[]{:S(2)}) %collective-permute-start.3) | collective-permute-done | bytes 147488 | tf_op jit(solution)/shard_map/ppermute | solution.py:33
  20.8 0.0 copy-done.1
  20.8 0.0 copy-start.2
  20.8 1.3 %copy-done.2 = bf16[3,3,256,256]{3,2,1,0:T(8,128)(2,1)S(1)} copy-done((bf16[3,3,256,256]{3,2,1,0:T(8,128)(2,1)S(1)}, bf16[3,3,256,256]{3,2,1,0:T(8,128)(2,1)}, u32[]{:S(2)}) %copy-start.2) | copy-done | bytes 1179672
  22.1 1.2 end_frames.1
  23.2 3.1 %collective-permute-start.4 = (bf16[256,256]{1,0:T(8,128)(2,1)S(1)}, bf16[256,256]{1,0:T(8,128)(2,1)S(1)}, u32[]{:S(2)}, u32[]{:S(2)}) collective-permute-start(bf16[256,256]{1,0:T(8,128)(2,1)S(1)} %get-tuple-element.28), channel_id=1, source_target_pairs={{0,64},{64,128},{128,192},{1,65},{65,129},{129,193},{2,66},{66,130... | collective-permute-start | bytes 393224 | tf_op jit(solution)/shard_map/ppermute | solution.py:33
  26.4 0.0 copy-start.3
  26.4 1.4 %collective-permute-start.5 = (bf16[256,256]{1,0:T(8,128)(2,1)S(1)}, bf16[256,256]{1,0:T(8,128)(2,1)S(1)}, u32[]{:S(2)}, u32[]{:S(2)}) collective-permute-start(bf16[256,256]{1,0:T(8,128)(2,1)S(1)} %get-tuple-element.29), channel_id=1, source_target_pairs={{64,0},{128,64},{192,128},{65,1},{129,65},{193,129},{66,2},{130,66... | collective-permute-start | bytes 393224 | tf_op jit(solution)/shard_map/ppermute | solution.py:33
  27.8 6.1 %spatial_conv.1 = bf16[16,16,16,256]{3,2,1,0:T(8,128)(2,1)S(1)} custom-call(bf16[16,16,16,256]{3,2,1,0:T(8,128)(2,1)S(1)} %copy-done.1, bf16[16,16,256]{2,1,0:T(8,128)(2,1)S(1)} %collective-permute-done.a_ref, bf16[16,16,256]{2,1,0:T(8,128)(2,1)S(1)} %collective-permute-done.1.b_ref, bf16[18,16,256]{2,1,0:T(8,128)(2,1)S(1)} %collective-permute-done.2.l_ref, ...), custom_call_target="tpu_custom_call" | custom-call | flops 4831838208 | bytes 4194304 | tf_op jit(solution)/shard_map/spatial_conv/pallas_call | solution.py:106
  33.9 0.0 collective-permute-done.4.b_ref
  33.9 0.0 collective-permute-done.5.a_ref
  33.9 0.0 copy-done.3
  33.9 0.0 copy-start.4
  33.9 0.0 copy-start.5
  34.0 0.0 copy-start.6
  34.0 0.0 copy-start.7
  34.0 3.0 %temporal_conv.1 = (bf16[64,16,256]{2,1,0:T(8,128)(2,1)S(1)}, bf16[64,16,256]{2,1,0:T(8,128)(2,1)S(1)}, bf16[64,16,256]{2,1,0:T(8,128)(2,1)S(1)}, bf16[64,16,256]{2,1,0:T(8,128)(2,1)S(1)}, f32[8,128]{1,0:T(8,128)S(1)}) custom-call(s32[1]{0:T(128)} %bitcast.me_ref, bf16[256,16,256]{2,1,0:T(8,128)(2,1)S(1)} %bitcast.21, ...), custom_call_target="tpu_custom_call" | custom-call | flops 1610612736 | bytes 4194304 | tf_op jit(solution)/shard_map/temporal_conv/pallas_call | solution.py:269
  36.9 2.2 %collective-permute-start.6 = (bf16[64,16,256]{2,1,0:T(8,128)(2,1)S(1)}, bf16[64,16,256]{2,1,0:T(8,128)(2,1)S(1)}, u32[]{:S(2)}, u32[]{:S(2)}) collective-permute-start(bf16[64,16,256]{2,1,0:T(8,128)(2,1)S(1)} %get-tuple-element.31), channel_id=1, source_target_pairs={{0,64},{64,128},{128,192},{192,0},{1,65},{65,129},{129,193},{193,1... | collective-permute-start | bytes 1572872 | tf_op jit(solution)/shard_map/ppermute | solution.py:461
  39.1 2.5 %collective-permute-start.7 = (bf16[64,16,256]{2,1,0:T(8,128)(2,1)S(1)}, bf16[64,16,256]{2,1,0:T(8,128)(2,1)S(1)}, u32[]{:S(2)}, u32[]{:S(2)}) collective-permute-start(bf16[64,16,256]{2,1,0:T(8,128)(2,1)S(1)} %get-tuple-element.32), channel_id=1, source_target_pairs={{0,128},{64,192},{128,0},{192,64},{1,129},{65,193},{129,1},{193,65... | collective-permute-start | bytes 1572872 | tf_op jit(solution)/shard_map/ppermute | solution.py:461
  41.6 1.1 collective-permute-start.8
  42.7 0.0 collective-permute-start.11
  42.7 2.1 %collective-permute-start.10 = (f32[8,128]{1,0:T(8,128)S(1)}, f32[8,128]{1,0:T(8,128)S(1)}, u32[]{:S(2)}, u32[]{:S(2)}) collective-permute-start(f32[8,128]{1,0:T(8,128)S(1)} %get-tuple-element.34), channel_id=1, source_target_pairs={{0,128},{64,192},{128,0},{192,64},{1,129},{65,193},{129,1},{193,65... | collective-permute-start | bytes 12296 | tf_op jit(solution)/shard_map/ppermute | solution.py:461
  44.8 17.7 %collective-permute-done.11 = f32[8,128]{1,0:T(8,128)S(1)} collective-permute-done((f32[8,128]{1,0:T(8,128)S(1)}, f32[8,128]{1,0:T(8,128)S(1)}, u32[]{:S(2)}, u32[]{:S(2)}) %collective-permute-start.11) | collective-permute-done | bytes 4128 | tf_op jit(solution)/shard_map/ppermute | solution.py:461
  62.5 1.7 %collective-permute-start.9 = (f32[8,128]{1,0:T(8,128)S(1)}, f32[8,128]{1,0:T(8,128)S(1)}, u32[]{:S(2)}, u32[]{:S(2)}) collective-permute-start(f32[8,128]{1,0:T(8,128)S(1)} %get-tuple-element.34), channel_id=1, source_target_pairs={{0,64},{64,128},{128,192},{192,0},{1,65},{65,129},{129,193},{193,1... | collective-permute-start | bytes 12296 | tf_op jit(solution)/shard_map/ppermute | solution.py:461
  64.2 0.0 collective-permute-done.10
  64.2 2.0 %collective-permute-done.9 = f32[8,128]{1,0:T(8,128)S(1)} collective-permute-done((f32[8,128]{1,0:T(8,128)S(1)}, f32[8,128]{1,0:T(8,128)S(1)}, u32[]{:S(2)}, u32[]{:S(2)}) %collective-permute-start.9) | collective-permute-done | bytes 4128 | tf_op jit(solution)/shard_map/ppermute | solution.py:461
  66.1 1.1 collective-permute-start.12
  67.3 0.8 collective-permute-done.12
  68.1 23.1 %all_to_all.5.refs_4_ = f32[32,8,128]{2,1,0:T(8,128)S(1)} all-to-all(f32[32,8,128]{2,1,0:T(8,128)S(1)} %broadcast_in_dim.2), channel_id=1, replica_groups=mesh['tm'=4,'height'=4,'width_0'=8,'width_1'=2] {'height','width_0'}, dimensions={0} | all-to-all | bytes 262144 | tf_op jit(solution)/shard_map/all_to_all | solution.py:489
  91.2 0.0 collective-permute-done.6.refs_1_
  91.2 0.0 collective-permute-done.7.refs_2_
  91.2 0.0 collective-permute-done.8.refs_3_
  91.3 0.0 copy-done.4
  91.3 0.0 copy-done.5
  91.3 0.0 copy-done.6
  91.3 0.0 copy-done.7
  91.3 5.4 %attention.3 = (bf16[32,16,256]{2,1,0:T(8,128)(2,1)S(1)}, bf16[32,16,256]{2,1,0:T(8,128)(2,1)S(1)}, bf16[32,16,256]{2,1,0:T(8,128)(2,1)S(1)}, bf16[32,16,256]{2,1,0:T(8,128)(2,1)S(1)}) custom-call(bf16[64,16,256]{2,1,0:T(8,128)(2,1)S(1)} %get-tuple-element.30.refs_0_, bf16[64,16,256]{2,1,0:T(8,128)(2,1)S(1)} %collective-permute-done.6.refs_1_, ...), custom_call_target="tpu_custom_call" | custom-call | flops 2147483648 | bytes 2097152 | tf_op jit(solution)/shard_map/attention/pallas_call | solution.py:403
  96.7 1.2 collective-permute-start.16
  97.9 0.9 collective-permute-start.17
  98.8 0.5 collective-permute-start.18
  99.3 5.4 %attention.2 = (bf16[32,16,256]{2,1,0:T(8,128)(2,1)S(1)}, bf16[32,16,256]{2,1,0:T(8,128)(2,1)S(1)}, bf16[32,16,256]{2,1,0:T(8,128)(2,1)S(1)}, bf16[32,16,256]{2,1,0:T(8,128)(2,1)S(1)}) custom-call(bf16[64,16,256]{2,1,0:T(8,128)(2,1)S(1)} %get-tuple-element.30.refs_0_, bf16[64,16,256]{2,1,0:T(8,128)(2,1)S(1)} %collective-permute-done.6.refs_1_, ...), custom_call_target="tpu_custom_call" | custom-call | flops 2147483648 | bytes 2097152 | tf_op jit(solution)/shard_map/attention/pallas_call | solution.py:403
  104.7 2.3 %collective-permute-start.13 = (bf16[32,16,256]{2,1,0:T(8,128)(2,1)S(1)}, bf16[32,16,256]{2,1,0:T(8,128)(2,1)S(1)}, u32[]{:S(2)}, u32[]{:S(2)}) collective-permute-start(bf16[32,16,256]{2,1,0:T(8,128)(2,1)S(1)} %get-tuple-element.35), channel_id=1, source_target_pairs={{0,192},{64,0},{128,64},{192,128},{1,193},{65,1},{129,65},{193,129... | collective-permute-start | bytes 786440 | tf_op jit(solution)/shard_map/ppermute | solution.py:461
  107.0 0.9 collective-permute-start.14
  107.9 0.0 collective-permute-done.16.refs_2_
  107.9 0.3 collective-permute-start.15
  108.2 0.0 collective-permute-done.17.refs_3_
  108.2 6.4 %collective-permute-done.18.refs_4_ = bf16[32,16,256]{2,1,0:T(8,128)(2,1)S(1)} collective-permute-done((bf16[32,16,256]{2,1,0:T(8,128)(2,1)S(1)}, bf16[32,16,256]{2,1,0:T(8,128)(2,1)S(1)}, u32[]{:S(2)}, u32[]{:S(2)}) %collective-permute-start.18) | collective-permute-done | bytes 262176 | tf_op jit(solution)/shard_map/ppermute | solution.py:461
  114.6 1.2 from_pixels.2.refs_3_
  115.8 0.0 collective-permute-done.13.refs_0_
  115.8 1.0 collective-permute-done.14.refs_1_
  116.8 7.3 %collective-permute-done.15.refs_2_ = bf16[32,16,256]{2,1,0:T(8,128)(2,1)S(1)} collective-permute-done((bf16[32,16,256]{2,1,0:T(8,128)(2,1)S(1)}, bf16[32,16,256]{2,1,0:T(8,128)(2,1)S(1)}, u32[]{:S(2)}, u32[]{:S(2)}) %collective-permute-start.15) | collective-permute-done | bytes 262176 | tf_op jit(solution)/shard_map/ppermute | solution.py:461
  124.2 1.0 from_pixels.3
  (4 shorter events, 0.1 us)
Async XLA Ops:
  1.0 7.8 %collective-permute-start.1 = (bf16[16,16,256]{2,1,0:T(8,128)(2,1)S(1)}, bf16[16,16,256]{2,1,0:T(8,128)(2,1)S(1)}, u32[]{:S(2)}, u32[]{:S(2)}) collective-permute-start(bf16[16,16,256]{2,1,0:T(8,128)(2,1)S(1)} %get-tuple-element.43), channel_id=1, source_target_pairs={{16,0},{32,16},{48,32},{17,1},{33,17},{49,33},{18,2},{34,18},{50,3... | collective-permute-start | bytes 393224 | tf_op jit(solution)/shard_map/ppermute | solution.py:33
  2.3 6.6 %collective-permute-start = (bf16[16,16,256]{2,1,0:T(8,128)(2,1)S(1)}, bf16[16,16,256]{2,1,0:T(8,128)(2,1)S(1)}, u32[]{:S(2)}, u32[]{:S(2)}) collective-permute-start(bf16[16,16,256]{2,1,0:T(8,128)(2,1)S(1)} %get-tuple-element.44), channel_id=1, source_target_pairs={{0,16},{16,32},{32,48},{1,17},{17,33},{33,49},{2,18},{18,34},{34,5... | collective-permute-start | bytes 393224 | tf_op jit(solution)/shard_map/ppermute | solution.py:33
  7.0 1.6 %copy-start = (bf16[16,16,16,256]{3,2,1,0:T(8,128)(2,1)S(1)}, bf16[16,16,16,256]{3,2,1,0:T(8,128)(2,1)}, u32[]{:S(2)}) copy-start(bf16[16,16,16,256]{3,2,1,0:T(8,128)(2,1)} %v_ref.5) | copy-start | bytes 6291460
  8.5 12.2 %copy-start.1 = (bf16[16,16,16,256]{3,2,1,0:T(8,128)(2,1)S(1)}, bf16[16,16,16,256]{3,2,1,0:T(8,128)(2,1)}, u32[]{:S(2)}) copy-start(bf16[16,16,16,256]{3,2,1,0:T(8,128)(2,1)} %v_ref.5) | copy-start | bytes 6291460
  8.9 7.5 %collective-permute-start.2 = (bf16[18,16,256]{2,1,0:T(8,128)(2,1)S(1)}, bf16[18,16,256]{2,1,0:T(8,128)(2,1)S(1)}, u32[]{:S(2)}, u32[]{:S(2)}) collective-permute-start(bf16[18,16,256]{2,1,0:T(8,128)(2,1)S(1)} %get-tuple-element.26), channel_id=1, source_target_pairs={{0,1},{1,2},{2,3},{3,4},{4,5},{5,6},{6,7},{7,8},{8,9},{9,10},{10,1... | collective-permute-start | bytes 442376 | tf_op jit(solution)/shard_map/ppermute | solution.py:33
  14.3 6.5 %collective-permute-start.3 = (bf16[18,16,256]{2,1,0:T(8,128)(2,1)S(1)}, bf16[18,16,256]{2,1,0:T(8,128)(2,1)S(1)}, u32[]{:S(2)}, u32[]{:S(2)}) collective-permute-start(bf16[18,16,256]{2,1,0:T(8,128)(2,1)S(1)} %get-tuple-element.27), channel_id=1, source_target_pairs={{1,0},{2,1},{3,2},{4,3},{5,4},{6,5},{7,6},{8,7},{9,8},{10,9},{11,1... | collective-permute-start | bytes 442376 | tf_op jit(solution)/shard_map/ppermute | solution.py:33
  20.8 1.3 %copy-start.2 = (bf16[3,3,256,256]{3,2,1,0:T(8,128)(2,1)S(1)}, bf16[3,3,256,256]{3,2,1,0:T(8,128)(2,1)}, u32[]{:S(2)}) copy-start(bf16[3,3,256,256]{3,2,1,0:T(8,128)(2,1)} %param.8) | copy-start | bytes 3538948
  23.2 10.7 %collective-permute-start.4 = (bf16[256,256]{1,0:T(8,128)(2,1)S(1)}, bf16[256,256]{1,0:T(8,128)(2,1)S(1)}, u32[]{:S(2)}, u32[]{:S(2)}) collective-permute-start(bf16[256,256]{1,0:T(8,128)(2,1)S(1)} %get-tuple-element.28), channel_id=1, source_target_pairs={{0,64},{64,128},{128,192},{1,65},{65,129},{129,193},{2,66},{66,130... | collective-permute-start | bytes 393224 | tf_op jit(solution)/shard_map/ppermute | solution.py:33
  26.4 7.5 %copy-start.3 = (bf16[3,256,256]{2,1,0:T(8,128)(2,1)S(1)}, bf16[3,256,256]{2,1,0:T(8,128)(2,1)}, u32[]{:S(2)}) copy-start(bf16[3,256,256]{2,1,0:T(8,128)(2,1)} %param.9) | copy-start | bytes 1179652
  26.4 7.5 %collective-permute-start.5 = (bf16[256,256]{1,0:T(8,128)(2,1)S(1)}, bf16[256,256]{1,0:T(8,128)(2,1)S(1)}, u32[]{:S(2)}, u32[]{:S(2)}) collective-permute-start(bf16[256,256]{1,0:T(8,128)(2,1)S(1)} %get-tuple-element.29), channel_id=1, source_target_pairs={{64,0},{128,64},{192,128},{65,1},{129,65},{193,129},{66,2},{130,66... | collective-permute-start | bytes 393224 | tf_op jit(solution)/shard_map/ppermute | solution.py:33
  33.9 57.3 %copy-start.4 = (bf16[256,768]{1,0:T(8,128)(2,1)S(1)}, bf16[256,768]{1,0:T(8,128)(2,1)}, u32[]{:S(2)}) copy-start(bf16[256,768]{1,0:T(8,128)(2,1)} %refs_7_.3) | copy-start | bytes 1179652
  33.9 57.3 %copy-start.5 = (bf16[256,256]{1,0:T(8,128)(2,1)S(1)}, bf16[256,256]{1,0:T(8,128)(2,1)}, u32[]{:S(2)}) copy-start(bf16[256,256]{1,0:T(8,128)(2,1)} %refs_8_.3) | copy-start | bytes 393220
  34.0 57.3 %copy-start.6 = (f32[256]{0:T(256)S(1)}, f32[256]{0:T(256)}, u32[]{:S(2)}) copy-start(f32[256]{0:T(256)} %param.10) | copy-start | bytes 3076
  34.0 57.3 %copy-start.7 = (f32[256]{0:T(256)S(1)}, f32[256]{0:T(256)}, u32[]{:S(2)}) copy-start(f32[256]{0:T(256)} %param.11) | copy-start | bytes 3076
  36.9 54.3 %collective-permute-start.6 = (bf16[64,16,256]{2,1,0:T(8,128)(2,1)S(1)}, bf16[64,16,256]{2,1,0:T(8,128)(2,1)S(1)}, u32[]{:S(2)}, u32[]{:S(2)}) collective-permute-start(bf16[64,16,256]{2,1,0:T(8,128)(2,1)S(1)} %get-tuple-element.31), channel_id=1, source_target_pairs={{0,64},{64,128},{128,192},{192,0},{1,65},{65,129},{129,193},{193,1... | collective-permute-start | bytes 1572872 | tf_op jit(solution)/shard_map/ppermute | solution.py:461
  39.1 52.2 %collective-permute-start.7 = (bf16[64,16,256]{2,1,0:T(8,128)(2,1)S(1)}, bf16[64,16,256]{2,1,0:T(8,128)(2,1)S(1)}, u32[]{:S(2)}, u32[]{:S(2)}) collective-permute-start(bf16[64,16,256]{2,1,0:T(8,128)(2,1)S(1)} %get-tuple-element.32), channel_id=1, source_target_pairs={{0,128},{64,192},{128,0},{192,64},{1,129},{65,193},{129,1},{193,65... | collective-permute-start | bytes 1572872 | tf_op jit(solution)/shard_map/ppermute | solution.py:461
  41.6 49.7 %collective-permute-start.8 = (bf16[64,16,256]{2,1,0:T(8,128)(2,1)S(1)}, bf16[64,16,256]{2,1,0:T(8,128)(2,1)S(1)}, u32[]{:S(2)}, u32[]{:S(2)}) collective-permute-start(bf16[64,16,256]{2,1,0:T(8,128)(2,1)S(1)} %get-tuple-element.33), channel_id=1, source_target_pairs={{0,192},{64,0},{128,64},{192,128},{1,193},{65,1},{129,65},{193,129... | collective-permute-start | bytes 1572872 | tf_op jit(solution)/shard_map/ppermute | solution.py:461
  42.7 19.8 %collective-permute-start.11 = (f32[8,128]{1,0:T(8,128)S(1)}, f32[8,128]{1,0:T(8,128)S(1)}, u32[]{:S(2)}, u32[]{:S(2)}) collective-permute-start(f32[8,128]{1,0:T(8,128)S(1)} %get-tuple-element.34), channel_id=1, source_target_pairs={{0,192},{64,0},{128,64},{192,128},{1,193},{65,1},{129,65},{193,129... | collective-permute-start | bytes 12296 | tf_op jit(solution)/shard_map/ppermute | solution.py:461
  42.7 21.5 %collective-permute-start.10 = (f32[8,128]{1,0:T(8,128)S(1)}, f32[8,128]{1,0:T(8,128)S(1)}, u32[]{:S(2)}, u32[]{:S(2)}) collective-permute-start(f32[8,128]{1,0:T(8,128)S(1)} %get-tuple-element.34), channel_id=1, source_target_pairs={{0,128},{64,192},{128,0},{192,64},{1,129},{65,193},{129,1},{193,65... | collective-permute-start | bytes 12296 | tf_op jit(solution)/shard_map/ppermute | solution.py:461
  62.5 3.7 %collective-permute-start.9 = (f32[8,128]{1,0:T(8,128)S(1)}, f32[8,128]{1,0:T(8,128)S(1)}, u32[]{:S(2)}, u32[]{:S(2)}) collective-permute-start(f32[8,128]{1,0:T(8,128)S(1)} %get-tuple-element.34), channel_id=1, source_target_pairs={{0,64},{64,128},{128,192},{192,0},{1,65},{65,129},{129,193},{193,1... | collective-permute-start | bytes 12296 | tf_op jit(solution)/shard_map/ppermute | solution.py:461
  66.1 2.0 %collective-permute-start.12 = (f32[8,128]{1,0:T(8,128)S(1)}, f32[8,128]{1,0:T(8,128)S(1)}, u32[]{:S(2)}, u32[]{:S(2)}) collective-permute-start(f32[8,128]{1,0:T(8,128)S(1)} %add_add_fusion), channel_id=1, source_target_pairs={{0,1},{1,0},{2,3},{3,2},{4,5},{5,4},{6,7},{7,6},{8,9},{9,8},{10,11... | collective-permute-start | bytes 12296 | tf_op jit(solution)/shard_map/ppermute | solution.py:485
  96.7 11.1 %collective-permute-start.16 = (bf16[32,16,256]{2,1,0:T(8,128)(2,1)S(1)}, bf16[32,16,256]{2,1,0:T(8,128)(2,1)S(1)}, u32[]{:S(2)}, u32[]{:S(2)}) collective-permute-start(bf16[32,16,256]{2,1,0:T(8,128)(2,1)S(1)} %get-tuple-element.40), channel_id=1, source_target_pairs={{0,192},{64,0},{128,64},{192,128},{1,193},{65,1},{129,65},{193,129... | collective-permute-start | bytes 786440 | tf_op jit(solution)/shard_map/ppermute | solution.py:461
  97.9 10.3 %collective-permute-start.17 = (bf16[32,16,256]{2,1,0:T(8,128)(2,1)S(1)}, bf16[32,16,256]{2,1,0:T(8,128)(2,1)S(1)}, u32[]{:S(2)}, u32[]{:S(2)}) collective-permute-start(bf16[32,16,256]{2,1,0:T(8,128)(2,1)S(1)} %get-tuple-element.41), channel_id=1, source_target_pairs={{0,128},{64,192},{128,0},{192,64},{1,129},{65,193},{129,1},{193,65... | collective-permute-start | bytes 786440 | tf_op jit(solution)/shard_map/ppermute | solution.py:461
  98.8 15.8 %collective-permute-start.18 = (bf16[32,16,256]{2,1,0:T(8,128)(2,1)S(1)}, bf16[32,16,256]{2,1,0:T(8,128)(2,1)S(1)}, u32[]{:S(2)}, u32[]{:S(2)}) collective-permute-start(bf16[32,16,256]{2,1,0:T(8,128)(2,1)S(1)} %get-tuple-element.42), channel_id=1, source_target_pairs={{0,64},{64,128},{128,192},{192,0},{1,65},{65,129},{129,193},{193,1... | collective-permute-start | bytes 786440 | tf_op jit(solution)/shard_map/ppermute | solution.py:461
  104.7 11.1 %collective-permute-start.13 = (bf16[32,16,256]{2,1,0:T(8,128)(2,1)S(1)}, bf16[32,16,256]{2,1,0:T(8,128)(2,1)S(1)}, u32[]{:S(2)}, u32[]{:S(2)}) collective-permute-start(bf16[32,16,256]{2,1,0:T(8,128)(2,1)S(1)} %get-tuple-element.35), channel_id=1, source_target_pairs={{0,192},{64,0},{128,64},{192,128},{1,193},{65,1},{129,65},{193,129... | collective-permute-start | bytes 786440 | tf_op jit(solution)/shard_map/ppermute | solution.py:461
  107.0 9.8 %collective-permute-start.14 = (bf16[32,16,256]{2,1,0:T(8,128)(2,1)S(1)}, bf16[32,16,256]{2,1,0:T(8,128)(2,1)S(1)}, u32[]{:S(2)}, u32[]{:S(2)}) collective-permute-start(bf16[32,16,256]{2,1,0:T(8,128)(2,1)S(1)} %get-tuple-element.36), channel_id=1, source_target_pairs={{0,128},{64,192},{128,0},{192,64},{1,129},{65,193},{129,1},{193,65... | collective-permute-start | bytes 786440 | tf_op jit(solution)/shard_map/ppermute | solution.py:461
  107.9 16.3 %collective-permute-start.15 = (bf16[32,16,256]{2,1,0:T(8,128)(2,1)S(1)}, bf16[32,16,256]{2,1,0:T(8,128)(2,1)S(1)}, u32[]{:S(2)}, u32[]{:S(2)}) collective-permute-start(bf16[32,16,256]{2,1,0:T(8,128)(2,1)S(1)} %get-tuple-element.37), channel_id=1, source_target_pairs={{0,64},{64,128},{128,192},{192,0},{1,65},{65,129},{129,193},{193,1... | collective-permute-start | bytes 786440 | tf_op jit(solution)/shard_map/ppermute | solution.py:461
